TPU v7x, 512 devices: a whole 4x8x8 slice. The times are simulated.
512 devices in a mesh: img: 8 (over y_lo, core), fsdp: 64 (over x, z, y_hi).
Axes of the slice: x: 4, y: 8 (y_hi: 2, y_lo: 4; y = y_hi * 4 + y_lo), z: 8, core: 2. Of those that a mesh axis runs over, the one named last changes fastest.
Arguments:
- text_states: bfloat16 [16384, 8192], P('fsdp')
- text_gain: float32 [8192], replicated, may hold values from 0.1 to 1.9
- vision: bfloat16 [8, 512, 8192], P('img', 'fsdp'), may hold values from -6 to 6
- q_weight: bfloat16 [8192, 4096], P('fsdp', 'img'), may hold values from -0.0625 to 0.0625
- k_weight: bfloat16 [8192, 1024], P('fsdp', 'img'), may hold values from -0.0625 to 0.0625
- v_weight: bfloat16 [8192, 1024], P('fsdp', 'img'), may hold values from -0.0625 to 0.0625
- q_gain: float32 [128], replicated, may hold values from 1 to 16
- k_gain: float32 [128], replicated, may hold values from 1 to 16
- owners: int32 [256, 4], P('fsdp'), may hold values from 0 to 7
- counts: int32 [256], P('fsdp'), may hold values from 0 to 4
- gate_value: float32 [1], replicated, may hold values from 0.3 to 1.5
Outputs:
- attended: bfloat16 [16384, 4096], P('fsdp', 'img')
All inputs are finite; a program needn't handle non-finite values.
Results may differ from a plain program's by a relative error of at most 0.025.
The roundings to bfloat16 on the way count: a program that leaves them out, or rounds other values in their place, can miss the bound.
Values may be sent and summed in bfloat16 or wider, within the bound.
No kernel may reach another device: no remote copies, remote signals or barrier semaphores. Data moves between devices by JAX's collectives and lax.ppermute only.
A program may use at most 64 MiB of HBM per device.

v0:
```python
import functools

import jax
import jax.numpy as jnp
from jax import lax
from jax.experimental import pallas as pl
from jax.experimental.pallas import tpu as pltpu
from jax.sharding import Mesh, PartitionSpec as P


norm_epsilon = 1e-05
masked_score = -1e30


IMG = ("yl", "co")
FSDP = ("x", "z", "yh")
SIZES = (4, 2, 4, 8, 2)


def shift(array, axis, step):
    size = lax.axis_size(axis)
    return lax.ppermute(array, axis, [(i, (i + step) % size) for i in range(size)])


def exchange(array, axes):
    return lax.all_to_all(array, axes, 0, 0, tiled=True)


def head_norm(values, gain):
    mean_square = jnp.mean(values * values, axis=-1, keepdims=True)
    return values * lax.rsqrt(mean_square + norm_epsilon) * gain


def whole(shape):
    return pl.BlockSpec(shape, lambda *_: (0,) * len(shape))


scalar = pl.BlockSpec(memory_space=pltpu.SMEM)


def half_kernel(choice, states, gain, *rest):
    out = rest[-1]
    rows, width = states.shape
    depth = 128
    squares = jnp.zeros((rows, depth), jnp.float32)
    for j in range(width // depth):
        wide = states[:, j * depth : (j + 1) * depth].astype(jnp.float32)
        squares += wide * wide
    scale = lax.rsqrt(jnp.sum(squares, axis=-1, keepdims=True) / width + norm_epsilon)
    pair = choice[1] == 0
    for j in range(out.shape[1] // depth):
        low = slice(2 * j * depth, (2 * j + 1) * depth)
        high = slice((2 * j + 1) * depth, (2 * j + 2) * depth)
        kept = jnp.where(pair, states[:, low], states[:, high]).astype(jnp.float32)
        kept_gain = jnp.where(pair, gain[:, low], gain[:, high])
        out[:, j * depth : (j + 1) * depth] = (kept * scale * kept_gain).astype(out.dtype)


def half_rows(states, gain, choice, steps, rows, blocks=None, base=None, first=0):
    width = states.shape[1]
    blocks = blocks or steps
    held = () if base is None else (base,)
    return pl.pallas_call(
        half_kernel,
        grid_spec=pltpu.PrefetchScalarGridSpec(
            num_scalar_prefetch=1,
            grid=(steps,),
            in_specs=[
                pl.BlockSpec((rows, width), lambda i, c: (c[0] + first + i, 0)),
                pl.BlockSpec((1, width), lambda i, c: (0, 0)),
                *(pl.BlockSpec(memory_space=pl.ANY) for _ in held),
            ],
            out_specs=pl.BlockSpec((rows, width // 2), lambda i, c: (first + i, 0)),
        ),
        out_shape=jax.ShapeDtypeStruct((blocks * rows, width // 2), jnp.bfloat16),
        input_output_aliases={3: 0} if held else {},
        name="half_rows",
    )(choice, states, gain, *held)


def columns_kernel(x, vision, out):
    copies, z, _, width = out.shape
    span = width // x
    for c in range(copies):
        for k in range(z):
            for j in range(x):
                start = (j * z + k) * span
                out[c, k, :, j * span : (j + 1) * span] = vision[:, start : start + span]


def columns_of(vision, copies, x, z):
    tokens, width = vision.shape
    shape = (copies, z, tokens, width // z)
    return pl.pallas_call(
        functools.partial(columns_kernel, x),
        in_specs=[whole(vision.shape)],
        out_specs=whole(shape),
        grid=(1,),
        out_shape=jax.ShapeDtypeStruct(shape, vision.dtype),
        name="columns",
    )(vision)


def partial_kernel(spot, here, there, *rest):
    *weights, out = rest
    z, _, yl, tokens, width = out.shape
    x = len(weights)
    span = weights[0].shape[0]
    for c, part in enumerate((here, there)):
        product = jnp.zeros((part.shape[0], width), jnp.float32)
        for k, weight in enumerate(weights):
            start = pl.multiple_of(lax.rem(spot[0] + x - k, x) * span, span)
            product += jnp.dot(
                part[:, pl.ds(start, span)], weight[...], preferred_element_type=jnp.float32
            )
        for a in range(yl):
            for k in range(z):
                row = (a * z + k) * tokens
                out[k, c, a] = product[row : row + tokens]


def partial_sums(here, there, spot, weights, z, yl, tokens):
    shape = (z, 2, yl, tokens, weights[0].shape[1])
    return pl.pallas_call(
        partial_kernel,
        in_specs=[scalar, whole(here.shape), whole(there.shape), *(whole(w.shape) for w in weights)],
        out_specs=whole(shape),
        grid=(1,),
        out_shape=jax.ShapeDtypeStruct(shape, jnp.float32),
        name="partial_sums",
    )(spot, here, there, *weights)


def pair_kernel(odd, parts, k_gain, out):
    sources, cores, yl, tokens, width = parts.shape
    head = width // 2
    copies = out.shape[0]
    swap = odd[0] != 0
    total = parts[0]
    for s in range(1, sources):
        total = total + parts[s]
    rows = jnp.concatenate([total[c, a] for c in range(cores) for a in range(yl)], axis=0)
    keys = head_norm(rows[:, :head], k_gain[...]).astype(out.dtype)
    values = rows[:, head:].astype(out.dtype)
    half = yl * tokens
    for a in range(yl):
        near = slice(a * tokens, (a + 1) * tokens)
        far = slice(half + a * tokens, half + (a + 1) * tokens)
        for piece, lanes in ((keys, slice(0, head)), (values, slice(head, width))):
            even_core = jnp.where(swap, piece[far], piece[near])
            odd_core = jnp.where(swap, piece[near], piece[far])
            for c in range(copies):
                out[c, 2 * a, :, lanes] = even_core
                out[c, 2 * a + 1, :, lanes] = odd_core


def pairs_of(odd, parts, k_gain, copies):
    _, cores, yl, tokens, width = parts.shape
    shape = (copies, cores * yl, tokens, width)
    return pl.pallas_call(
        pair_kernel,
        in_specs=[scalar, whole(parts.shape), whole(k_gain.shape)],
        out_specs=whole(shape),
        grid=(1,),
        out_shape=jax.ShapeDtypeStruct(shape, jnp.bfloat16),
        name="key_value_pairs",
    )(odd, parts, k_gain)


def attention_kernel(
    part, yl, where, owners, counts, gate, query, back, q_gain, own, after, before, low, high, out
):
    block = pl.program_id(0)
    rows, width = query.shape
    images = own.shape[0]
    half = low.shape[0]
    head = q_gain.shape[1]
    heads = width // head
    slots = owners.shape[1]
    scale = head ** (-0.5)
    gain = q_gain[...]
    shares = []
    for j in range(rows // part):
        index = block * (rows // part) + j
        core = lax.rem(index // yl + where[1], 2)
        near = lax.rem(where[0] + yl - lax.rem(index, yl), yl)
        shares.append(back[pl.ds(pl.multiple_of((core * yl + near) * part, part), part), :])
    total = query[...] + jnp.concatenate(shares, axis=0)
    parts = []
    for h in range(heads):
        parts.append(head_norm(total[:, h * head : (h + 1) * head], gain).astype(jnp.bfloat16))
    queries = jnp.concatenate(parts, axis=0)
    count = counts[block]
    names = [owners[block, j] for j in range(slots)]
    scores = []
    values = []
    live = jnp.bool_(False)
    for j in range(slots):
        valid = j < count
        for i in range(j):
            valid = valid & (names[i] != names[j])
        live = live | valid
        image = jnp.clip(names[j], 0, images - 1)
        lower = jnp.minimum(image, half - 1)
        upper = jnp.maximum(image - half, 0)
        across = jnp.where(image < half, low[lower], high[upper])
        pairs = jnp.concatenate((own[image], after[image], before[image], across), axis=0)
        values.append(pairs[:, head:])
        score = (
            lax.dot_general(
                queries, pairs[:, :head], (((1,), (1,)), ((), ())), preferred_element_type=jnp.float32
            )
            * scale
        )
        scores.append(jnp.where(valid, score, masked_score))
    top = jnp.max(scores[0], axis=1, keepdims=True)
    for j in range(1, slots):
        top = jnp.maximum(top, jnp.max(scores[j], axis=1, keepdims=True))
    denominator = jnp.zeros_like(top)
    numerator = jnp.zeros((rows * heads, head), jnp.float32)
    for j in range(slots):
        weights = jnp.exp(scores[j] - top).astype(jnp.bfloat16)
        denominator += jnp.sum(weights.astype(jnp.float32), axis=1, keepdims=True)
        numerator += jnp.dot(weights, values[j], preferred_element_type=jnp.float32)
    factor = jnp.where(live, jnp.tanh(jnp.full((1, head), gate[0], jnp.float32)), 0.0)
    attended = (numerator / denominator * factor).astype(out.dtype)
    for h in range(heads):
        out[:, h * head : (h + 1) * head] = attended[h * rows : (h + 1) * rows]


def attention(where, owners, counts, gate_value, query, back, q_gain, pieces, part, yl):
    blocks = owners.shape[0]
    tokens, width = query.shape
    rows = tokens // blocks
    return pl.pallas_call(
        functools.partial(attention_kernel, part, yl),
        grid=(blocks,),
        in_specs=[
            *(scalar,) * 4,
            pl.BlockSpec((rows, width), lambda b: (b, 0)),
            whole(back.shape),
            whole(q_gain.shape),
            *(whole(p.shape) for p in pieces),
        ],
        out_specs=pl.BlockSpec((rows, width), lambda b: (b, 0)),
        out_shape=jax.ShapeDtypeStruct((tokens, width), jnp.bfloat16),
        name="attention",
    )(where, owners, counts, gate_value, query, back, q_gain, *pieces)


def on_device(
    text_states,
    text_gain,
    vision,
    q_weight,
    k_weight,
    v_weight,
    q_gain,
    k_gain,
    owners,
    counts,
    gate_value,
):
    head = q_gain.shape[0]
    tokens = vision.shape[1]
    rows = text_states.shape[0]
    width = text_states.shape[1]
    yl, co, x, z, yh = (lax.axis_size(a) for a in IMG + FSDP)
    first = lax.axis_index("yh") == 0

    q_half = lax.all_gather(q_weight, ("x", "z"), axis=0, tiled=True)

    columns = columns_of(vision.reshape(tokens, width), yl, x, z)
    here = exchange(columns.reshape(yl * z, tokens, width // z), ("yl", "z"))

    joined = jnp.concatenate((k_weight, v_weight), axis=1)
    other = shift(joined, "yh", 1)
    both = jnp.where(
        first,
        jnp.concatenate((joined, other), axis=0),
        jnp.concatenate((other, joined), axis=0),
    )
    pair_weight = (both, *(shift(both, "x", k) for k in range(1, x)))

    part = rows // (yl * co)
    place = lax.axis_index("co") * yl + lax.axis_index("yl")
    mine = lax.axis_index("yh")
    gain = text_gain[None]
    sent = half_rows(text_states, gain, jnp.stack((place, 1 - mine)).astype(jnp.int32), 1, part)
    came = [
        lax.ppermute(
            sent,
            ("yl", "yh"),
            [(a * yh + h, (a + k) % yl * yh + 1 - h) for a in range(yl) for h in range(yh)],
        )
        for k in range(yl)
    ]
    guest = jnp.concatenate(came, axis=0)
    guest_other = shift(guest, "co", 1)
    text_half = None
    choice = jnp.stack((0 * mine, mine)).astype(jnp.int32)
    pieces = 4
    blocks = yl * co
    for k in range(pieces):
        steps = blocks // pieces
        text_half = half_rows(text_states, gain, choice, steps, part, blocks, text_half, k * steps)

    there = shift(here, "co", 1)
    partial = partial_sums(
        here.reshape(yl * z * tokens, width // z),
        there.reshape(yl * z * tokens, width // z),
        lax.axis_index("x").astype(jnp.int32)[None],
        pair_weight,
        z,
        yl,
        tokens,
    )
    parts = exchange(partial, "z")
    odd = lax.axis_index("co").astype(jnp.int32)[None]
    pair = pairs_of(odd, parts, k_gain[None], z * yh)
    own = exchange(pair, ("z", "yh"))
    own = own.transpose(1, 0, 2, 3).reshape(yl * co, z * yh * tokens, 2 * head)
    after = shift(own, "x", 1)
    before = shift(own, "x", -1)
    half = yl * co // 2
    low = shift(after[:half], "x", 1)
    high = shift(before[half:], "x", -1)

    guest_query = jnp.concatenate(
        (
            jnp.dot(guest, q_half, preferred_element_type=jnp.float32),
            jnp.dot(guest_other, q_half, preferred_element_type=jnp.float32),
        ),
        axis=0,
    )
    back = shift(guest_query, "yh", 1)
    query = jnp.dot(text_half, q_half, preferred_element_type=jnp.float32)
    where = jnp.stack((lax.axis_index("yl"), lax.axis_index("co"))).astype(jnp.int32)
    return attention(
        where,
        owners,
        counts,
        gate_value,
        query,
        back,
        q_gain[None],
        (own, after, before, low, high),
        part,
        yl,
    )


def solution(mesh):
    fine = Mesh(mesh.devices.reshape(SIZES), IMG + FSDP)
    in_specs = (
        P(FSDP, None),
        P(),
        P(IMG, FSDP, None),
        P(FSDP, IMG),
        P(FSDP, IMG),
        P(FSDP, IMG),
        P(),
        P(),
        P(FSDP, None),
        P(FSDP),
        P(),
    )
    return jax.shard_map(
        on_device, mesh=fine, in_specs=in_specs, out_specs=P(FSDP, IMG), check_vma=False
    )
```

profile of v0, /device:TPU:6, one launch (start us, length us, event | category | flops | bytes accessed | tf_op | source)
XLA Modules:
  0.0 197.2 jit_solution(6565901061588131634)
XLA Ops:
  6.5 0.7 all-gather.2.cloned.1.call-update
  7.3 1.8 columns.1
  9.0 30.3 %all_to_all.15 = bf16[32,8,1024]{2,1,0:T(8,128)(2,1)S(1)} all-to-all(bf16[32,8,1024]{2,1,0:T(8,128)(2,1)} %bitcast.25), channel_id=1, replica_groups=mesh['yl'=4,'co'=2,'x'=4,'z'=8,'yh'=2] {'yl','z'}, dimensions={0} | all-to-all | bytes 1048576 | tf_op jit(solution)/shard_map/all_to_all | solution.py:26
  39.3 1.9 collective-permute-start.6
  41.3 0.8 constant_dynamic-update-slice_fusion.5
  42.0 0.8 constant_dynamic-update-slice_fusion.4
  42.8 5.2 %collective-permute-start.7 = (bf16[128,256]{1,0:T(8,128)(2,1)S(1)}, bf16[128,256]{1,0:T(8,128)(2,1)S(1)}, u32[]{:S(2)}, u32[]{:S(2)}) collective-permute-start(bf16[128,256]{1,0:T(8,128)(2,1)S(1)} %constant_dynamic-update-slice_fusion.4), channel_id=1, source_target_pairs={{0,1},{1,0},{2,3},{3,2},{4,5},{5,4},{6,7},{7,6},{8,9},{9,8},{10,11... | collective-permute-start | bytes 196616 | tf_op jit(solution)/shard_map/ppermute | solution.py:22
  48.0 0.7 pad_add_fusion.2.choice
  48.7 2.7 %half_rows.9 = bf16[32,4096]{1,0:T(8,128)(2,1)} custom-call(s32[2]{0:T(128)} %pad_add_fusion.2.choice, bf16[256,8192]{1,0:T(8,128)(2,1)} %states.9, f32[1,8192]{1,0:T(1,128)} %bitcast.26), custom_call_target="tpu_custom_call" | custom-call | tf_op jit(solution)/shard_map/half_rows/pallas_call | solution.py:63
  51.4 4.5 %collective-permute-start = (bf16[32,4096]{1,0:T(8,128)(2,1)}, bf16[32,4096]{1,0:T(8,128)(2,1)S(1)}, u32[]{:S(2)}, u32[]{:S(2)}) collective-permute-start(bf16[32,4096]{1,0:T(8,128)(2,1)} %half_rows.9), channel_id=1, source_target_pairs={{0,1},{1,0},{128,129},{129,128},{256,257},{257,256},{384,385},{385... | collective-permute-start | bytes 786440 | tf_op jit(solution)/shard_map/ppermute | solution.py:291
  55.9 0.0 collective-permute-done.7
  56.0 2.4 %collective-permute-start.8 = (bf16[256,256]{1,0:T(8,128)(2,1)S(1)}, bf16[256,256]{1,0:T(8,128)(2,1)S(1)}, u32[]{:S(2)}, u32[]{:S(2)}) collective-permute-start(bf16[256,256]{1,0:T(8,128)(2,1)S(1)} %maximum_select_fusion.rest_0_), channel_id=1, source_target_pairs={{0,16},{16,32},{32,48},{48,0},{1,17},{17,33},{33,49},{49,1},{2,18}... | collective-permute-start | bytes 393224 | tf_op jit(solution)/shard_map/ppermute | solution.py:22
  58.4 4.3 %collective-permute-start.9 = (bf16[256,256]{1,0:T(8,128)(2,1)S(1)}, bf16[256,256]{1,0:T(8,128)(2,1)S(1)}, u32[]{:S(2)}, u32[]{:S(2)}) collective-permute-start(bf16[256,256]{1,0:T(8,128)(2,1)S(1)} %maximum_select_fusion.rest_0_), channel_id=1, source_target_pairs={{0,32},{16,48},{32,0},{48,16},{1,33},{17,49},{33,1},{49,17},{2,34}... | collective-permute-start | bytes 393224 | tf_op jit(solution)/shard_map/ppermute | solution.py:22
  62.7 1.9 collective-permute-start.10
  64.6 0.0 collective-permute-done.8.rest_1_
  64.7 2.2 %collective-permute-done.9.rest_2_ = bf16[256,256]{1,0:T(8,128)(2,1)S(1)} collective-permute-done((bf16[256,256]{1,0:T(8,128)(2,1)S(1)}, bf16[256,256]{1,0:T(8,128)(2,1)S(1)}, u32[]{:S(2)}, u32[]{:S(2)}) %collective-permute-start.9) | collective-permute-done | bytes 131104 | tf_op jit(solution)/shard_map/ppermute | solution.py:22
  66.8 3.9 %collective-permute-done.10.rest_3_ = bf16[256,256]{1,0:T(8,128)(2,1)S(1)} collective-permute-done((bf16[256,256]{1,0:T(8,128)(2,1)S(1)}, bf16[256,256]{1,0:T(8,128)(2,1)S(1)}, u32[]{:S(2)}, u32[]{:S(2)}) %collective-permute-start.10) | collective-permute-done | bytes 131104 | tf_op jit(solution)/shard_map/ppermute | solution.py:22
  70.8 0.0 collective-permute-done.6
  70.8 0.0 copy-done.8
  70.8 0.0 copy-done.12
  70.8 0.0 copy-done.13
  70.8 0.6 copy-done.14
  71.4 0.2 copy-done.7
  71.6 2.6 %partial_sums.1 = f32[8,2,4,8,256]{4,3,2,1,0:T(8,128)} custom-call(s32[1]{0:T(128)} %bitcast.7.spot, bf16[256,1024]{1,0:T(8,128)(2,1)} %bitcast.24, bf16[256,1024]{1,0:T(8,128)(2,1)} %bitcast.31, bf16[256,256]{1,0:T(8,128)(2,1)} %copy-done.8, bf16[256,256]{1,0:T(8,128)(2,1)} %copy-done.12, bf16[256,256]{1,0:T(8,128)(2,1)} %copy-done.13, ...), custom_call_target="tpu_custom_call" | custom-call | tf_op jit(solution)/shard_map/partial_sums/pallas_call | solution.py:124
  74.2 5.1 %all-to-all-start.1 = ((f32[8,2,4,8,256]{4,3,2,1,0:T(8,128)}), f32[8,2,4,8,256]{4,3,2,1,0:T(8,128)S(1)}, u32[]{:S(2)}, u32[]{:S(2)}) async-start(f32[8,2,4,8,256]{4,3,2,1,0:T(8,128)} %partial_sums.1), calls=%async_computation.1 | async-start | bytes 1048576 | tf_op jit(solution)/shard_map/all_to_all | solution.py:26
  79.3 3.6 %collective-permute-start.1 = (bf16[32,4096]{1,0:T(8,128)(2,1)}, bf16[32,4096]{1,0:T(8,128)(2,1)S(1)}, u32[]{:S(2)}, u32[]{:S(2)}) collective-permute-start(bf16[32,4096]{1,0:T(8,128)(2,1)} %half_rows.9), channel_id=1, source_target_pairs={{0,129},{1,128},{128,257},{129,256},{256,385},{257,384},{384,1},{3... | collective-permute-start | bytes 786440 | tf_op jit(solution)/shard_map/ppermute | solution.py:291
  82.9 4.8 %collective-permute-start.2 = (bf16[32,4096]{1,0:T(8,128)(2,1)}, bf16[32,4096]{1,0:T(8,128)(2,1)S(1)}, u32[]{:S(2)}, u32[]{:S(2)}) collective-permute-start(bf16[32,4096]{1,0:T(8,128)(2,1)} %half_rows.9), channel_id=1, source_target_pairs={{0,257},{1,256},{128,385},{129,384},{256,1},{257,0},{384,129},{385... | collective-permute-start | bytes 786440 | tf_op jit(solution)/shard_map/ppermute | solution.py:291
  87.7 3.7 %collective-permute-start.3 = (bf16[32,4096]{1,0:T(8,128)(2,1)}, bf16[32,4096]{1,0:T(8,128)(2,1)S(1)}, u32[]{:S(2)}, u32[]{:S(2)}) collective-permute-start(bf16[32,4096]{1,0:T(8,128)(2,1)} %half_rows.9), channel_id=1, source_target_pairs={{0,385},{1,384},{128,1},{129,0},{256,129},{257,128},{384,257},{385... | collective-permute-start | bytes 786440 | tf_op jit(solution)/shard_map/ppermute | solution.py:291
  91.4 0.0 collective-permute-done
  91.4 15.7 %collective-permute-done.1 = bf16[32,4096]{1,0:T(8,128)(2,1)S(1)} collective-permute-done((bf16[32,4096]{1,0:T(8,128)(2,1)}, bf16[32,4096]{1,0:T(8,128)(2,1)S(1)}, u32[]{:S(2)}, u32[]{:S(2)}) %collective-permute-start.1) | collective-permute-done | bytes 262176 | tf_op jit(solution)/shard_map/ppermute | solution.py:291
  107.1 0.0 all-to-all-done.1.parts
  107.1 0.0 copy-start.3
  107.1 0.8 copy-done.3
  107.9 2.0 %key_value_pairs.1 = bf16[16,8,8,256]{3,2,1,0:T(8,128)(2,1)} custom-call(s32[1]{0:T(128)} %bitcast.1.odd, f32[8,2,4,8,256]{4,3,2,1,0:T(8,128)} %copy-done.3, f32[1,128]{1,0:T(1,128)} %bitcast.33), custom_call_target="tpu_custom_call" | custom-call | tf_op jit(solution)/shard_map/key_value_pairs/pallas_call | solution.py:160
  109.9 8.6 %all-to-all-start.2 = ((bf16[16,8,8,256]{3,2,1,0:T(8,128)(2,1)}), bf16[16,8,8,256]{3,2,1,0:T(8,128)(2,1)S(1)}, u32[]{:S(2)}, u32[]{:S(2)}) async-start(bf16[16,8,8,256]{3,2,1,0:T(8,128)(2,1)} %key_value_pairs.1), calls=%async_computation.2 | async-start | bytes 1048576 | tf_op jit(solution)/shard_map/all_to_all | solution.py:26
  118.5 0.0 collective-permute-done.2
  118.6 0.0 collective-permute-done.3
  118.6 1.9 collective-permute-start.4
  121.2 0.6 pad_add_fusion.1.choice
  121.8 3.0 %half_rows.5.rest_0_ = bf16[256,4096]{1,0:T(8,128)(2,1)} custom-call(s32[2]{0:T(128)} %pad_add_fusion.1.choice, bf16[256,8192]{1,0:T(8,128)(2,1)} %states.9, f32[1,8192]{1,0:T(1,128)} %bitcast.27), custom_call_target="tpu_custom_call" | custom-call | tf_op jit(solution)/shard_map/half_rows/pallas_call | solution.py:63
  124.8 3.0 %half_rows.6.rest_0_ = bf16[256,4096]{1,0:T(8,128)(2,1)} custom-call(s32[2]{0:T(128)} %pad_add_fusion.1.choice, bf16[256,8192]{1,0:T(8,128)(2,1)} %states.9, f32[1,8192]{1,0:T(1,128)} %bitcast.28, bf16[256,4096]{1,0:T(8,128)(2,1)} %half_rows.5.rest_0_), custom_call_target="tpu_custom_call", output_to_operand_aliasing={{}: (3, {})} | custom-call | tf_op jit(solution)/shard_map/half_rows/pallas_call | solution.py:63
  127.7 2.9 %half_rows.7.rest_0_ = bf16[256,4096]{1,0:T(8,128)(2,1)} custom-call(s32[2]{0:T(128)} %pad_add_fusion.1.choice, bf16[256,8192]{1,0:T(8,128)(2,1)} %states.9, f32[1,8192]{1,0:T(1,128)} %bitcast.29, bf16[256,4096]{1,0:T(8,128)(2,1)} %half_rows.6.rest_0_), custom_call_target="tpu_custom_call", output_to_operand_aliasing={{}: (3, {})} | custom-call | tf_op jit(solution)/shard_map/half_rows/pallas_call | solution.py:63
  130.7 3.0 %half_rows.8 = bf16[256,4096]{1,0:T(8,128)(2,1)} custom-call(s32[2]{0:T(128)} %pad_add_fusion.1.choice, bf16[256,8192]{1,0:T(8,128)(2,1)} %states.9, f32[1,8192]{1,0:T(1,128)} %bitcast.30, bf16[256,4096]{1,0:T(8,128)(2,1)} %half_rows.7.rest_0_), custom_call_target="tpu_custom_call", output_to_operand_aliasing={{}: (3, {})} | custom-call | tf_op jit(solution)/shard_map/half_rows/pallas_call | solution.py:63
  133.6 0.7 all-to-all-done.2
  134.4 3.2 %collective-permute-start.11 = (bf16[8,128,256]{2,1,0:T(8,128)(2,1)S(1)}, bf16[8,128,256]{2,1,0:T(8,128)(2,1)S(1)}, u32[]{:S(2)}, u32[]{:S(2)}) collective-permute-start(bf16[8,128,256]{2,1,0:T(8,128)(2,1)S(1)} %copy_bitcast_fusion.own), channel_id=1, source_target_pairs={{0,16},{16,32},{32,48},{48,0},{1,17},{17,33},{33,49},{49,1},{2,18}... | collective-permute-start | bytes 1572872 | tf_op jit(solution)/shard_map/ppermute | solution.py:22
  137.5 7.7 %collective-permute-start.12 = (bf16[8,128,256]{2,1,0:T(8,128)(2,1)S(1)}, bf16[8,128,256]{2,1,0:T(8,128)(2,1)S(1)}, u32[]{:S(2)}, u32[]{:S(2)}) collective-permute-start(bf16[8,128,256]{2,1,0:T(8,128)(2,1)S(1)} %copy_bitcast_fusion.own), channel_id=1, source_target_pairs={{0,48},{16,0},{32,16},{48,32},{1,49},{17,1},{33,17},{49,33},{2,50}... | collective-permute-start | bytes 1572872 | tf_op jit(solution)/shard_map/ppermute | solution.py:22
  145.3 0.0 all-gather.2.cloned.1.call-done
  145.3 3.1 %fusion.1 = f32[128,512]{1,0:T(8,128)S(1)} fusion(bf16[128,4096]{1,0:T(8,128)(2,1)S(1)} %constant_dynamic-update-slice_fusion, bf16[4096,512]{1,0:T(8,128)(2,1)} %all-gather.2.cloned.1.call-done), kind=kOutput, calls=%fused_computation.13 | convolution fusion | flops 536870912 | bytes 5505024 | tf_op jit(solution)/shard_map/dot_general | solution.py:331
  148.4 0.0 copy-start
  148.4 0.0 collective-permute-done.4
  148.4 0.4 copy-done.1
  148.7 2.2 %fusion.2 = f32[128,512]{1,0:T(8,128)S(1)} fusion(bf16[128,4096]{1,0:T(8,128)(2,1)} %collective-permute-done.4, bf16[4096,512]{1,0:T(8,128)(2,1)S(1)} %copy-done.1), kind=kOutput, calls=%fused_computation.14 | convolution fusion | flops 536870912 | bytes 5505024 | tf_op jit(solution)/shard_map/dot_general | solution.py:332
  151.0 2.9 %collective-permute-start.5 = (f32[256,512]{1,0:T(8,128)S(1)}, f32[256,512]{1,0:T(8,128)S(1)}, u32[]{:S(2)}, u32[]{:S(2)}) collective-permute-start(f32[256,512]{1,0:T(8,128)S(1)} %pad_maximum_fusion), channel_id=1, source_target_pairs={{0,1},{1,0},{2,3},{3,2},{4,5},{5,4},{6,7},{7,6},{8,9},{9,8},{10,11... | collective-permute-start | bytes 1572872 | tf_op jit(solution)/shard_map/ppermute | solution.py:22
  153.9 0.7 pad_add_fusion.where
  154.6 1.3 collective-permute-done.11.after
  155.9 4.8 %collective-permute-start.13 = (bf16[4,128,256]{2,1,0:T(8,128)(2,1)S(1)}, bf16[4,128,256]{2,1,0:T(8,128)(2,1)S(1)}, u32[]{:S(2)}, u32[]{:S(2)}) collective-permute-start(bf16[4,128,256]{2,1,0:T(8,128)(2,1)S(1)} %slice.8), channel_id=1, source_target_pairs={{0,16},{16,32},{32,48},{48,0},{1,17},{17,33},{33,49},{49,1},{2,18}... | collective-permute-start | bytes 786440 | tf_op jit(solution)/shard_map/ppermute | solution.py:22
  160.7 0.4 collective-permute-done.12.before
  161.2 1.9 collective-permute-start.14
  163.1 2.0 %fusion.query = f32[256,512]{1,0:T(8,128)} fusion(bf16[256,4096]{1,0:T(8,128)(2,1)S(1)} %copy-done, bf16[4096,512]{1,0:T(8,128)(2,1)S(1)} %copy-done.1), kind=kOutput, calls=%fused_computation.12 | convolution fusion | flops 1073741824 | bytes 6815744 | tf_op jit(solution)/shard_map/dot_general | solution.py:337
  165.2 2.1 %collective-permute-done.13.low = bf16[4,128,256]{2,1,0:T(8,128)(2,1)S(1)} collective-permute-done((bf16[4,128,256]{2,1,0:T(8,128)(2,1)S(1)}, bf16[4,128,256]{2,1,0:T(8,128)(2,1)S(1)}, u32[]{:S(2)}, u32[]{:S(2)}) %collective-permute-start.13) | collective-permute-done | bytes 262176 | tf_op jit(solution)/shard_map/ppermute | solution.py:22
  167.3 4.9 %collective-permute-done.14.high = bf16[4,128,256]{2,1,0:T(8,128)(2,1)S(1)} collective-permute-done((bf16[4,128,256]{2,1,0:T(8,128)(2,1)S(1)}, bf16[4,128,256]{2,1,0:T(8,128)(2,1)S(1)}, u32[]{:S(2)}, u32[]{:S(2)}) %collective-permute-start.14) | collective-permute-done | bytes 262176 | tf_op jit(solution)/shard_map/ppermute | solution.py:22
  172.2 10.0 %collective-permute-done.5.back = f32[256,512]{1,0:T(8,128)S(1)} collective-permute-done((f32[256,512]{1,0:T(8,128)S(1)}, f32[256,512]{1,0:T(8,128)S(1)}, u32[]{:S(2)}, u32[]{:S(2)}) %collective-permute-start.5) | collective-permute-done | bytes 524320 | tf_op jit(solution)/shard_map/ppermute | solution.py:22
  182.1 0.8 copy-done.9
  182.9 7.4 %attention.1 = bf16[256,512]{1,0:T(8,128)(2,1)} custom-call(s32[2]{0:T(128)} %pad_add_fusion.where, s32[4,4]{1,0:T(4,128)} %owners.1, s32[4]{0:T(128)} %counts.1, f32[1]{0:T(128)S(6)} %copy.24.gate, f32[256,512]{1,0:T(8,128)} %fusion.query, f32[256,512]{1,0:T(8,128)} %copy-done.9, f32[1,128]{1,0:T(1,128)} %bitcast.34, bf16[8,128,256]{2,1,0:T(8,128)(2,1)} %copy-done.4, ...), custom_call_target="tpu_custom_call" | custom-call | tf_op jit(solution)/shard_map/attention/pallas_call | solution.py:235
  (30 shorter events, 0.3 us)
Async XLA Ops:
  6.5 138.7 %all-gather.2.cloned.1.call-start = ((), (), s32[]{:S(2)}) async-start(), calls=%async_computation.3 | async-start | bytes 4325376 | tf_op jit(solution)/shard_map/all_gather | solution.py:271
  39.3 31.4 %copy-start.2 = (bf16[32,8,1024]{2,1,0:T(8,128)(2,1)}, bf16[32,8,1024]{2,1,0:T(8,128)(2,1)S(1)}, u32[]{:S(2)}) copy-start(bf16[32,8,1024]{2,1,0:T(8,128)(2,1)S(1)} %all_to_all.15) | copy-start | bytes 1572868
  39.3 31.4 %collective-permute-start.6 = (bf16[32,8,1024]{2,1,0:T(8,128)(2,1)S(1)}, bf16[32,8,1024]{2,1,0:T(8,128)(2,1)S(1)}, u32[]{:S(2)}, u32[]{:S(2)}) collective-permute-start(bf16[32,8,1024]{2,1,0:T(8,128)(2,1)S(1)} %all_to_all.15), channel_id=1, source_target_pairs={{0,64},{64,0},{1,65},{65,1},{2,66},{66,2},{3,67},{67,3},{4,68},{68... | collective-permute-start | bytes 1572872 | tf_op jit(solution)/shard_map/ppermute | solution.py:22
  42.8 13.1 %collective-permute-start.7 = (bf16[128,256]{1,0:T(8,128)(2,1)S(1)}, bf16[128,256]{1,0:T(8,128)(2,1)S(1)}, u32[]{:S(2)}, u32[]{:S(2)}) collective-permute-start(bf16[128,256]{1,0:T(8,128)(2,1)S(1)} %constant_dynamic-update-slice_fusion.4), channel_id=1, source_target_pairs={{0,1},{1,0},{2,3},{3,2},{4,5},{5,4},{6,7},{7,6},{8,9},{9,8},{10,11... | collective-permute-start | bytes 196616 | tf_op jit(solution)/shard_map/ppermute | solution.py:22
  51.4 40.0 %collective-permute-start = (bf16[32,4096]{1,0:T(8,128)(2,1)}, bf16[32,4096]{1,0:T(8,128)(2,1)S(1)}, u32[]{:S(2)}, u32[]{:S(2)}) collective-permute-start(bf16[32,4096]{1,0:T(8,128)(2,1)} %half_rows.9), channel_id=1, source_target_pairs={{0,1},{1,0},{128,129},{129,128},{256,257},{257,256},{384,385},{385... | collective-permute-start | bytes 786440 | tf_op jit(solution)/shard_map/ppermute | solution.py:291
  56.0 14.8 %copy-start.8 = (bf16[256,256]{1,0:T(8,128)(2,1)}, bf16[256,256]{1,0:T(8,128)(2,1)S(1)}, u32[]{:S(2)}) copy-start(bf16[256,256]{1,0:T(8,128)(2,1)S(1)} %maximum_select_fusion.rest_0_) | copy-start | bytes 393220
  56.0 8.7 %collective-permute-start.8 = (bf16[256,256]{1,0:T(8,128)(2,1)S(1)}, bf16[256,256]{1,0:T(8,128)(2,1)S(1)}, u32[]{:S(2)}, u32[]{:S(2)}) collective-permute-start(bf16[256,256]{1,0:T(8,128)(2,1)S(1)} %maximum_select_fusion.rest_0_), channel_id=1, source_target_pairs={{0,16},{16,32},{32,48},{48,0},{1,17},{17,33},{33,49},{49,1},{2,18}... | collective-permute-start | bytes 393224 | tf_op jit(solution)/shard_map/ppermute | solution.py:22
  58.4 8.5 %collective-permute-start.9 = (bf16[256,256]{1,0:T(8,128)(2,1)S(1)}, bf16[256,256]{1,0:T(8,128)(2,1)S(1)}, u32[]{:S(2)}, u32[]{:S(2)}) collective-permute-start(bf16[256,256]{1,0:T(8,128)(2,1)S(1)} %maximum_select_fusion.rest_0_), channel_id=1, source_target_pairs={{0,32},{16,48},{32,0},{48,16},{1,33},{17,49},{33,1},{49,17},{2,34}... | collective-permute-start | bytes 393224 | tf_op jit(solution)/shard_map/ppermute | solution.py:22
  62.7 8.1 %collective-permute-start.10 = (bf16[256,256]{1,0:T(8,128)(2,1)S(1)}, bf16[256,256]{1,0:T(8,128)(2,1)S(1)}, u32[]{:S(2)}, u32[]{:S(2)}) collective-permute-start(bf16[256,256]{1,0:T(8,128)(2,1)S(1)} %maximum_select_fusion.rest_0_), channel_id=1, source_target_pairs={{0,48},{16,0},{32,16},{48,32},{1,49},{17,1},{33,17},{49,33},{2,50}... | collective-permute-start | bytes 393224 | tf_op jit(solution)/shard_map/ppermute | solution.py:22
  64.6 6.2 %copy-start.12 = (bf16[256,256]{1,0:T(8,128)(2,1)}, bf16[256,256]{1,0:T(8,128)(2,1)S(1)}, u32[]{:S(2)}) copy-start(bf16[256,256]{1,0:T(8,128)(2,1)S(1)} %collective-permute-done.8.rest_1_) | copy-start | bytes 393220
  66.8 4.0 %copy-start.13 = (bf16[256,256]{1,0:T(8,128)(2,1)}, bf16[256,256]{1,0:T(8,128)(2,1)S(1)}, u32[]{:S(2)}) copy-start(bf16[256,256]{1,0:T(8,128)(2,1)S(1)} %collective-permute-done.9.rest_2_) | copy-start | bytes 393220
  70.8 0.6 copy-start.14
  70.8 0.8 copy-start.7
  74.2 32.9 %all-to-all-start.1 = ((f32[8,2,4,8,256]{4,3,2,1,0:T(8,128)}), f32[8,2,4,8,256]{4,3,2,1,0:T(8,128)S(1)}, u32[]{:S(2)}, u32[]{:S(2)}) async-start(f32[8,2,4,8,256]{4,3,2,1,0:T(8,128)} %partial_sums.1), calls=%async_computation.1 | async-start | bytes 1048576 | tf_op jit(solution)/shard_map/all_to_all | solution.py:26
  79.3 27.8 %collective-permute-start.1 = (bf16[32,4096]{1,0:T(8,128)(2,1)}, bf16[32,4096]{1,0:T(8,128)(2,1)S(1)}, u32[]{:S(2)}, u32[]{:S(2)}) collective-permute-start(bf16[32,4096]{1,0:T(8,128)(2,1)} %half_rows.9), channel_id=1, source_target_pairs={{0,129},{1,128},{128,257},{129,256},{256,385},{257,384},{384,1},{3... | collective-permute-start | bytes 786440 | tf_op jit(solution)/shard_map/ppermute | solution.py:291
  82.9 35.6 %collective-permute-start.2 = (bf16[32,4096]{1,0:T(8,128)(2,1)}, bf16[32,4096]{1,0:T(8,128)(2,1)S(1)}, u32[]{:S(2)}, u32[]{:S(2)}) collective-permute-start(bf16[32,4096]{1,0:T(8,128)(2,1)} %half_rows.9), channel_id=1, source_target_pairs={{0,257},{1,256},{128,385},{129,384},{256,1},{257,0},{384,129},{385... | collective-permute-start | bytes 786440 | tf_op jit(solution)/shard_map/ppermute | solution.py:291
  87.7 30.9 %collective-permute-start.3 = (bf16[32,4096]{1,0:T(8,128)(2,1)}, bf16[32,4096]{1,0:T(8,128)(2,1)S(1)}, u32[]{:S(2)}, u32[]{:S(2)}) collective-permute-start(bf16[32,4096]{1,0:T(8,128)(2,1)} %half_rows.9), channel_id=1, source_target_pairs={{0,385},{1,384},{128,1},{129,0},{256,129},{257,128},{384,257},{385... | collective-permute-start | bytes 786440 | tf_op jit(solution)/shard_map/ppermute | solution.py:291
  107.1 0.8 copy-start.3
  109.9 24.4 %all-to-all-start.2 = ((bf16[16,8,8,256]{3,2,1,0:T(8,128)(2,1)}), bf16[16,8,8,256]{3,2,1,0:T(8,128)(2,1)S(1)}, u32[]{:S(2)}, u32[]{:S(2)}) async-start(bf16[16,8,8,256]{3,2,1,0:T(8,128)(2,1)} %key_value_pairs.1), calls=%async_computation.2 | async-start | bytes 1048576 | tf_op jit(solution)/shard_map/all_to_all | solution.py:26
  118.6 29.7 %collective-permute-start.4 = (bf16[128,4096]{1,0:T(8,128)(2,1)S(1)}, bf16[128,4096]{1,0:T(8,128)(2,1)}, u32[]{:S(2)}, u32[]{:S(2)}) collective-permute-start(bf16[128,4096]{1,0:T(8,128)(2,1)S(1)} %constant_dynamic-update-slice_fusion), channel_id=1, source_target_pairs={{0,64},{64,0},{1,65},{65,1},{2,66},{66,2},{3,67},{67,3},{4,68},{68... | collective-permute-start | bytes 3145736 | tf_op jit(solution)/shard_map/ppermute | solution.py:22
  134.4 16.6 %copy-start.4 = (bf16[8,128,256]{2,1,0:T(8,128)(2,1)}, bf16[8,128,256]{2,1,0:T(8,128)(2,1)S(1)}, u32[]{:S(2)}) copy-start(bf16[8,128,256]{2,1,0:T(8,128)(2,1)S(1)} %copy_bitcast_fusion.own) | copy-start | bytes 1572868
  134.4 21.5 %collective-permute-start.11 = (bf16[8,128,256]{2,1,0:T(8,128)(2,1)S(1)}, bf16[8,128,256]{2,1,0:T(8,128)(2,1)S(1)}, u32[]{:S(2)}, u32[]{:S(2)}) collective-permute-start(bf16[8,128,256]{2,1,0:T(8,128)(2,1)S(1)} %copy_bitcast_fusion.own), channel_id=1, source_target_pairs={{0,16},{16,32},{32,48},{48,0},{1,17},{17,33},{33,49},{49,1},{2,18}... | collective-permute-start | bytes 1572872 | tf_op jit(solution)/shard_map/ppermute | solution.py:22
  137.5 23.7 %collective-permute-start.12 = (bf16[8,128,256]{2,1,0:T(8,128)(2,1)S(1)}, bf16[8,128,256]{2,1,0:T(8,128)(2,1)S(1)}, u32[]{:S(2)}, u32[]{:S(2)}) collective-permute-start(bf16[8,128,256]{2,1,0:T(8,128)(2,1)S(1)} %copy_bitcast_fusion.own), channel_id=1, source_target_pairs={{0,48},{16,0},{32,16},{48,32},{1,49},{17,1},{33,17},{49,33},{2,50}... | collective-permute-start | bytes 1572872 | tf_op jit(solution)/shard_map/ppermute | solution.py:22
  145.3 3.5 %copy-start.1 = (bf16[4096,512]{1,0:T(8,128)(2,1)S(1)}, bf16[4096,512]{1,0:T(8,128)(2,1)}, u32[]{:S(2)}) copy-start(bf16[4096,512]{1,0:T(8,128)(2,1)} %all-gather.2.cloned.1.call-done) | copy-start | bytes 12582916
  148.4 14.8 %copy-start = (bf16[256,4096]{1,0:T(8,128)(2,1)S(1)}, bf16[256,4096]{1,0:T(8,128)(2,1)}, u32[]{:S(2)}) copy-start(bf16[256,4096]{1,0:T(8,128)(2,1)} %half_rows.8) | copy-start | bytes 6291460
  151.0 31.2 %collective-permute-start.5 = (f32[256,512]{1,0:T(8,128)S(1)}, f32[256,512]{1,0:T(8,128)S(1)}, u32[]{:S(2)}, u32[]{:S(2)}) collective-permute-start(f32[256,512]{1,0:T(8,128)S(1)} %pad_maximum_fusion), channel_id=1, source_target_pairs={{0,1},{1,0},{2,3},{3,2},{4,5},{5,4},{6,7},{7,6},{8,9},{9,8},{10,11... | collective-permute-start | bytes 1572872 | tf_op jit(solution)/shard_map/ppermute | solution.py:22
  155.9 9.3 %copy-start.5 = (bf16[8,128,256]{2,1,0:T(8,128)(2,1)}, bf16[8,128,256]{2,1,0:T(8,128)(2,1)S(1)}, u32[]{:S(2)}) copy-start(bf16[8,128,256]{2,1,0:T(8,128)(2,1)S(1)} %collective-permute-done.11.after) | copy-start | bytes 1572868
  155.9 11.3 %collective-permute-start.13 = (bf16[4,128,256]{2,1,0:T(8,128)(2,1)S(1)}, bf16[4,128,256]{2,1,0:T(8,128)(2,1)S(1)}, u32[]{:S(2)}, u32[]{:S(2)}) collective-permute-start(bf16[4,128,256]{2,1,0:T(8,128)(2,1)S(1)} %slice.8), channel_id=1, source_target_pairs={{0,16},{16,32},{32,48},{48,0},{1,17},{17,33},{33,49},{49,1},{2,18}... | collective-permute-start | bytes 786440 | tf_op jit(solution)/shard_map/ppermute | solution.py:22
  161.2 20.9 %copy-start.6 = (bf16[8,128,256]{2,1,0:T(8,128)(2,1)}, bf16[8,128,256]{2,1,0:T(8,128)(2,1)S(1)}, u32[]{:S(2)}) copy-start(bf16[8,128,256]{2,1,0:T(8,128)(2,1)S(1)} %collective-permute-done.12.before) | copy-start | bytes 1572868
  161.2 11.0 %collective-permute-start.14 = (bf16[4,128,256]{2,1,0:T(8,128)(2,1)S(1)}, bf16[4,128,256]{2,1,0:T(8,128)(2,1)S(1)}, u32[]{:S(2)}, u32[]{:S(2)}) collective-permute-start(bf16[4,128,256]{2,1,0:T(8,128)(2,1)S(1)} %slice.9), channel_id=1, source_target_pairs={{0,48},{16,0},{32,16},{48,32},{1,49},{17,1},{33,17},{49,33},{2,50}... | collective-permute-start | bytes 786440 | tf_op jit(solution)/shard_map/ppermute | solution.py:22
  167.3 14.9 %copy-start.10 = (bf16[4,128,256]{2,1,0:T(8,128)(2,1)}, bf16[4,128,256]{2,1,0:T(8,128)(2,1)S(1)}, u32[]{:S(2)}) copy-start(bf16[4,128,256]{2,1,0:T(8,128)(2,1)S(1)} %collective-permute-done.13.low) | copy-start | bytes 786436
  172.2 10.0 %copy-start.11 = (bf16[4,128,256]{2,1,0:T(8,128)(2,1)}, bf16[4,128,256]{2,1,0:T(8,128)(2,1)S(1)}, u32[]{:S(2)}) copy-start(bf16[4,128,256]{2,1,0:T(8,128)(2,1)S(1)} %collective-permute-done.14.high) | copy-start | bytes 786436
  182.1 0.8 copy-start.9
Sparse Core Ops, SparseCore 0:
  10.5 99.0 all-gather.1
where the time goes:
time: 201 us; the launch traced here: 197 us
  starting transfers between devices  68.5 us (34%)
  waiting for transfers between devices  41.9 us (21%)
  blocking collectives  30.3 us (15%)
  Pallas kernels  28.3 us (14%)
  between operations  14.4 us (7%)
  matrix products  7.25 us (4%)
  local copies, waits for them, and re-layouts  4.47 us (2%)
    ppermute x11, starting transfers between devices, shift(): lax.ppermute(array, axis, [(i, (i + step) % size) for i in range(size)])  38.2 us
    all_to_all x1, blocking collectives, exchange(): return lax.all_to_all(array, axes, 0, 0, tiled=True)  30.3 us
    ppermute x11, waiting for transfers between devices, shift(): lax.ppermute(array, axis, [(i, (i + step) % size) for i in range(size)])  24.8 us
    ppermute x4, starting transfers between devices, on_device(): lax.ppermute(sent, ('yl', 'yh'), [(a * yh + h, (a + k) % yl * yh + 1 - h)...  16.6 us
    ppermute x4, waiting for transfers between devices, on_device(): lax.ppermute(sent, ('yl', 'yh'), [(a * yh + h, (a + k) % yl * yh + 1 - h)...  15.7 us
    pallas_call x5, Pallas kernels, half_rows(): pl.pallas_call(half_kernel, grid_spec=pltpu.PrefetchScalarGridSpec(num_sc...  14.5 us
    all_to_all x2, starting transfers between devices, exchange(): return lax.all_to_all(array, axes, 0, 0, tiled=True)  13.8 us
    pallas_call x1, Pallas kernels, attention(): pl.pallas_call(functools.partial(attention_kernel, part, yl), grid=(block...  7.43 us
  transfers between devices with their start and end apart: 18, of which 9 were waited for; matrix products, arithmetic and copies ran while one was open for 6% of the time, Pallas kernels for 11%

commit v1 on v0

--- a/solution.py
+++ b/solution.py
@@ -39,7 +39,7 @@
 
 
 def half_kernel(choice, states, gain, *rest):
-    out = rest[-1]
+    outs = rest[1:]
     rows, width = states.shape
     depth = 128
     squares = jnp.zeros((rows, depth), jnp.float32)
@@ -48,32 +48,45 @@
         squares += wide * wide
     scale = lax.rsqrt(jnp.sum(squares, axis=-1, keepdims=True) / width + norm_epsilon)
     pair = choice[1] == 0
-    for j in range(out.shape[1] // depth):
+    for j in range(width // depth // 2):
         low = slice(2 * j * depth, (2 * j + 1) * depth)
         high = slice((2 * j + 1) * depth, (2 * j + 2) * depth)
-        kept = jnp.where(pair, states[:, low], states[:, high]).astype(jnp.float32)
-        kept_gain = jnp.where(pair, gain[:, low], gain[:, high])
-        out[:, j * depth : (j + 1) * depth] = (kept * scale * kept_gain).astype(out.dtype)
-
-
-def half_rows(states, gain, choice, steps, rows, blocks=None, base=None, first=0):
-    width = states.shape[1]
-    blocks = blocks or steps
+        blocks = [
+            (states[:, at].astype(jnp.float32) * scale * gain[:, at]).astype(jnp.bfloat16)
+            for at in (low, high)
+        ]
+        lanes = slice(j * depth, (j + 1) * depth)
+        outs[0][:, lanes] = jnp.where(pair, blocks[0], blocks[1])
+        if len(outs) > 1:
+            outs[1][:, lanes] = jnp.where(pair, blocks[1], blocks[0])
+
+
+def half_rows(states, gain, choice, base):
+    total, width = states.shape
+    rows = 32
+    steps = total // 2 // rows
     held = () if base is None else (base,)
+    place = pl.BlockSpec((rows, width // 2), lambda i, c: (c[0] * steps + i, 0))
+    shapes = [jax.ShapeDtypeStruct((total, width // 2), jnp.bfloat16)]
+    places = [place]
+    if base is None:
+        held = (gain,)
+        shapes.append(jax.ShapeDtypeStruct((total // 2, width // 2), jnp.bfloat16))
+        places.append(pl.BlockSpec((rows, width // 2), lambda i, c: (i, 0)))
     return pl.pallas_call(
         half_kernel,
         grid_spec=pltpu.PrefetchScalarGridSpec(
             num_scalar_prefetch=1,
             grid=(steps,),
             in_specs=[
-                pl.BlockSpec((rows, width), lambda i, c: (c[0] + first + i, 0)),
+                pl.BlockSpec((rows, width), lambda i, c: (c[0] * steps + i, 0)),
                 pl.BlockSpec((1, width), lambda i, c: (0, 0)),
-                *(pl.BlockSpec(memory_space=pl.ANY) for _ in held),
+                pl.BlockSpec(memory_space=pl.ANY),
             ],
-            out_specs=pl.BlockSpec((rows, width // 2), lambda i, c: (first + i, 0)),
+            out_specs=places,
         ),
-        out_shape=jax.ShapeDtypeStruct((blocks * rows, width // 2), jnp.bfloat16),
-        input_output_aliases={3: 0} if held else {},
+        out_shape=shapes,
+        input_output_aliases={} if base is None else {3: 0},
         name="half_rows",
     )(choice, states, gain, *held)
 
@@ -168,7 +181,7 @@
 
 
 def attention_kernel(
-    part, yl, where, owners, counts, gate, query, back, q_gain, own, after, before, low, high, out
+    core, owners, counts, gate, query, near, far, q_gain, own, after, before, low, high, out
 ):
     block = pl.program_id(0)
     rows, width = query.shape
@@ -179,13 +192,11 @@
     slots = owners.shape[1]
     scale = head ** (-0.5)
     gain = q_gain[...]
-    shares = []
-    for j in range(rows // part):
-        index = block * (rows // part) + j
-        core = lax.rem(index // yl + where[1], 2)
-        near = lax.rem(where[0] + yl - lax.rem(index, yl), yl)
-        shares.append(back[pl.ds(pl.multiple_of((core * yl + near) * part, part), part), :])
-    total = query[...] + jnp.concatenate(shares, axis=0)
+    span = near.shape[0]
+    first = block * rows
+    inside = lax.rem(first, span)
+    at = pl.ds(pl.multiple_of(inside, rows), rows)
+    total = query[...] + jnp.where(first // span == core[0], near[at, :], far[at, :])
     parts = []
     for h in range(heads):
         parts.append(head_norm(total[:, h * head : (h + 1) * head], gain).astype(jnp.bfloat16))
@@ -222,30 +233,31 @@
         weights = jnp.exp(scores[j] - top).astype(jnp.bfloat16)
         denominator += jnp.sum(weights.astype(jnp.float32), axis=1, keepdims=True)
         numerator += jnp.dot(weights, values[j], preferred_element_type=jnp.float32)
-    factor = jnp.where(live, jnp.tanh(jnp.full((1, head), gate[0], jnp.float32)), 0.0)
+    factor = jnp.where(live, gate[0], 0.0)
     attended = (numerator / denominator * factor).astype(out.dtype)
     for h in range(heads):
         out[:, h * head : (h + 1) * head] = attended[h * rows : (h + 1) * rows]
 
 
-def attention(where, owners, counts, gate_value, query, back, q_gain, pieces, part, yl):
+def attention(core, owners, counts, gate_value, query, near, far, q_gain, pieces):
     blocks = owners.shape[0]
     tokens, width = query.shape
     rows = tokens // blocks
     return pl.pallas_call(
-        functools.partial(attention_kernel, part, yl),
+        attention_kernel,
         grid=(blocks,),
         in_specs=[
             *(scalar,) * 4,
             pl.BlockSpec((rows, width), lambda b: (b, 0)),
-            whole(back.shape),
+            whole(near.shape),
+            whole(far.shape),
             whole(q_gain.shape),
             *(whole(p.shape) for p in pieces),
         ],
         out_specs=pl.BlockSpec((rows, width), lambda b: (b, 0)),
         out_shape=jax.ShapeDtypeStruct((tokens, width), jnp.bfloat16),
         name="attention",
-    )(where, owners, counts, gate_value, query, back, q_gain, *pieces)
+    )(core, owners, counts, gate_value, query, near, far, q_gain, *pieces)
 
 
 def on_device(
@@ -263,7 +275,6 @@
 ):
     head = q_gain.shape[0]
     tokens = vision.shape[1]
-    rows = text_states.shape[0]
     width = text_states.shape[1]
     yl, co, x, z, yh = (lax.axis_size(a) for a in IMG + FSDP)
     first = lax.axis_index("yh") == 0
@@ -282,28 +293,17 @@
     )
     pair_weight = (both, *(shift(both, "x", k) for k in range(1, x)))
 
-    part = rows // (yl * co)
-    place = lax.axis_index("co") * yl + lax.axis_index("yl")
+    gate = jnp.tanh(gate_value)
+
+    core = lax.axis_index("co")
     mine = lax.axis_index("yh")
     gain = text_gain[None]
-    sent = half_rows(text_states, gain, jnp.stack((place, 1 - mine)).astype(jnp.int32), 1, part)
-    came = [
-        lax.ppermute(
-            sent,
-            ("yl", "yh"),
-            [(a * yh + h, (a + k) % yl * yh + 1 - h) for a in range(yl) for h in range(yh)],
-        )
-        for k in range(yl)
-    ]
-    guest = jnp.concatenate(came, axis=0)
+    choice = jnp.stack((core, mine)).astype(jnp.int32)
+    text_half, sent = half_rows(text_states, gain, choice, None)
+    guest = shift(sent, "yh", 1)
     guest_other = shift(guest, "co", 1)
-    text_half = None
-    choice = jnp.stack((0 * mine, mine)).astype(jnp.int32)
-    pieces = 4
-    blocks = yl * co
-    for k in range(pieces):
-        steps = blocks // pieces
-        text_half = half_rows(text_states, gain, choice, steps, part, blocks, text_half, k * steps)
+    choice = jnp.stack((1 - core, mine)).astype(jnp.int32)
+    (text_half,) = half_rows(text_states, gain, choice, text_half)
 
     there = shift(here, "co", 1)
     partial = partial_sums(
@@ -326,27 +326,21 @@
     low = shift(after[:half], "x", 1)
     high = shift(before[half:], "x", -1)
 
-    guest_query = jnp.concatenate(
-        (
-            jnp.dot(guest, q_half, preferred_element_type=jnp.float32),
-            jnp.dot(guest_other, q_half, preferred_element_type=jnp.float32),
-        ),
-        axis=0,
-    )
-    back = shift(guest_query, "yh", 1)
+    guest_near = jnp.dot(guest, q_half, preferred_element_type=jnp.float32)
+    guest_far = jnp.dot(guest_other, q_half, preferred_element_type=jnp.float32)
+    back_near = shift(guest_near, "yh", 1)
+    back_far = shift(guest_far, "yh", 1)
     query = jnp.dot(text_half, q_half, preferred_element_type=jnp.float32)
-    where = jnp.stack((lax.axis_index("yl"), lax.axis_index("co"))).astype(jnp.int32)
     return attention(
-        where,
+        core.astype(jnp.int32)[None],
         owners,
         counts,
-        gate_value,
+        gate,
         query,
-        back,
+        back_near,
+        back_far,
         q_gain[None],
         (own, after, before, low, high),
-        part,
-        yl,
     )
 
 

time: 201 us -> 213 us (1.060)
  the two profiles are of different devices: /device:TPU:6 before, /device:TPU:80 now
where the time goes in v1:
time: 213 us; the launch traced here: 212 us
  waiting for transfers between devices  72.5 us (34%)
  starting transfers between devices  59.5 us (28%)
  blocking collectives  29.3 us (14%)
  Pallas kernels  23.7 us (11%)
  between operations  14.4 us (7%)
  matrix products  7.1 us (3%)
  local copies, waits for them, and re-layouts  4.03 us (2%)
    ppermute x13, waiting for transfers between devices, shift(): lax.ppermute(array, axis, [(i, (i + step) % size) for i in range(size)])  52.3 us
    ppermute x13, starting transfers between devices, shift(): lax.ppermute(array, axis, [(i, (i + step) % size) for i in range(size)])  49.5 us
    all_to_all x1, blocking collectives, exchange(): return lax.all_to_all(array, axes, 0, 0, tiled=True)  29.3 us
    all_to_all x2, waiting for transfers between devices, exchange(): return lax.all_to_all(array, axes, 0, 0, tiled=True)  19.5 us
    all_to_all x2, starting transfers between devices, exchange(): return lax.all_to_all(array, axes, 0, 0, tiled=True)  10 us
    pallas_call x2, Pallas kernels, half_rows(): pl.pallas_call(half_kernel, grid_spec=pltpu.PrefetchScalarGridSpec(num_sc...  9.9 us
    pallas_call x1, Pallas kernels, attention(): pl.pallas_call(attention_kernel, grid=(blocks,), in_specs=[*(scalar,) * 4...  7.42 us
  transfers between devices with their start and end apart: 16, of which 8 were waited for; matrix products, arithmetic and copies ran while one was open for 5% of the time, Pallas kernels for 8%

profile of v1, /device:TPU:80, one launch (start us, length us, event | category | flops | bytes accessed | tf_op | source)
XLA Modules:
  0.0 211.8 jit_solution(11703619723585401657)
XLA Ops:
  6.5 0.0 all-gather.2.cloned.1.call-start
  6.5 0.7 all-gather.2.cloned.1.call-update
  7.3 1.8 columns.1
  9.0 29.3 %all_to_all.15 = bf16[32,8,1024]{2,1,0:T(8,128)(2,1)S(1)} all-to-all(bf16[32,8,1024]{2,1,0:T(8,128)(2,1)} %bitcast.23), channel_id=1, replica_groups=mesh['yl'=4,'co'=2,'x'=4,'z'=8,'yh'=2] {'yl','z'}, dimensions={0} | all-to-all | bytes 1048576 | tf_op jit(solution)/shard_map/all_to_all | solution.py:26
  38.3 1.9 collective-permute-start.4
  40.2 0.8 constant_dynamic-update-slice_fusion.1
  41.0 0.8 constant_dynamic-update-slice_fusion
  41.8 5.0 %collective-permute-start.5 = (bf16[128,256]{1,0:T(8,128)(2,1)S(1)}, bf16[128,256]{1,0:T(8,128)(2,1)S(1)}, u32[]{:S(2)}, u32[]{:S(2)}) collective-permute-start(bf16[128,256]{1,0:T(8,128)(2,1)S(1)} %constant_dynamic-update-slice_fusion), channel_id=1, source_target_pairs={{0,1},{1,0},{2,3},{3,2},{4,5},{5,4},{6,7},{7,6},{8,9},{9,8},{10,11... | collective-permute-start | bytes 196616 | tf_op jit(solution)/shard_map/ppermute | solution.py:22
  46.8 6.7 %collective-permute-done.5 = bf16[128,256]{1,0:T(8,128)(2,1)S(1)} collective-permute-done((bf16[128,256]{1,0:T(8,128)(2,1)S(1)}, bf16[128,256]{1,0:T(8,128)(2,1)S(1)}, u32[]{:S(2)}, u32[]{:S(2)}) %collective-permute-start.5) | collective-permute-done | bytes 65568 | tf_op jit(solution)/shard_map/ppermute | solution.py:22
  53.5 0.0 copy-start.8
  53.5 3.4 %collective-permute-start.6 = (bf16[256,256]{1,0:T(8,128)(2,1)S(1)}, bf16[256,256]{1,0:T(8,128)(2,1)S(1)}, u32[]{:S(2)}, u32[]{:S(2)}) collective-permute-start(bf16[256,256]{1,0:T(8,128)(2,1)S(1)} %maximum_select_fusion.rest_0_), channel_id=1, source_target_pairs={{0,16},{16,32},{32,48},{48,0},{1,17},{17,33},{33,49},{49,1},{2,18}... | collective-permute-start | bytes 393224 | tf_op jit(solution)/shard_map/ppermute | solution.py:22
  56.9 4.6 %collective-permute-start.7 = (bf16[256,256]{1,0:T(8,128)(2,1)S(1)}, bf16[256,256]{1,0:T(8,128)(2,1)S(1)}, u32[]{:S(2)}, u32[]{:S(2)}) collective-permute-start(bf16[256,256]{1,0:T(8,128)(2,1)S(1)} %maximum_select_fusion.rest_0_), channel_id=1, source_target_pairs={{0,32},{16,48},{32,0},{48,16},{1,33},{17,49},{33,1},{49,17},{2,34}... | collective-permute-start | bytes 393224 | tf_op jit(solution)/shard_map/ppermute | solution.py:22
  61.6 3.3 %collective-permute-start.8 = (bf16[256,256]{1,0:T(8,128)(2,1)S(1)}, bf16[256,256]{1,0:T(8,128)(2,1)S(1)}, u32[]{:S(2)}, u32[]{:S(2)}) collective-permute-start(bf16[256,256]{1,0:T(8,128)(2,1)S(1)} %maximum_select_fusion.rest_0_), channel_id=1, source_target_pairs={{0,48},{16,0},{32,16},{48,32},{1,49},{17,1},{33,17},{49,33},{2,50}... | collective-permute-start | bytes 393224 | tf_op jit(solution)/shard_map/ppermute | solution.py:22
  64.9 0.0 collective-permute-done.6.rest_1_
  64.9 0.0 copy-start.13
  64.9 0.3 collective-permute-done.7.rest_2_
  65.3 3.1 %collective-permute-done.8.rest_3_ = bf16[256,256]{1,0:T(8,128)(2,1)S(1)} collective-permute-done((bf16[256,256]{1,0:T(8,128)(2,1)S(1)}, bf16[256,256]{1,0:T(8,128)(2,1)S(1)}, u32[]{:S(2)}, u32[]{:S(2)}) %collective-permute-start.8) | collective-permute-done | bytes 131104 | tf_op jit(solution)/shard_map/ppermute | solution.py:22
  68.4 0.0 collective-permute-done.4
  68.4 0.0 copy-done.1
  68.4 0.0 copy-done.8
  68.5 0.0 copy-done.13
  68.5 0.0 copy-done.14
  68.5 0.6 copy-done.15
  69.1 0.2 copy-done.7
  69.3 2.6 %partial_sums.1 = f32[8,2,4,8,256]{4,3,2,1,0:T(8,128)} custom-call(s32[1]{0:T(128)} %bitcast.5.spot, bf16[256,1024]{1,0:T(8,128)(2,1)} %bitcast.22, bf16[256,1024]{1,0:T(8,128)(2,1)} %bitcast.24, bf16[256,256]{1,0:T(8,128)(2,1)} %copy-done.8, bf16[256,256]{1,0:T(8,128)(2,1)} %copy-done.13, bf16[256,256]{1,0:T(8,128)(2,1)} %copy-done.14, ...), custom_call_target="tpu_custom_call" | custom-call | tf_op jit(solution)/shard_map/partial_sums/pallas_call | solution.py:137
  71.9 3.8 %all-to-all-start.1 = ((f32[8,2,4,8,256]{4,3,2,1,0:T(8,128)}), f32[8,2,4,8,256]{4,3,2,1,0:T(8,128)S(1)}, u32[]{:S(2)}, u32[]{:S(2)}) async-start(f32[8,2,4,8,256]{4,3,2,1,0:T(8,128)} %partial_sums.1), calls=%async_computation.1 | async-start | bytes 1048576 | tf_op jit(solution)/shard_map/all_to_all | solution.py:26
  75.8 0.6 pad_add_fusion.1.choice
  76.3 5.1 %half_rows.2 = (bf16[256,4096]{1,0:T(8,128)(2,1)}, bf16[128,4096]{1,0:T(8,128)(2,1)}) custom-call(s32[2]{0:T(128)} %pad_add_fusion.1.choice, bf16[256,8192]{1,0:T(8,128)(2,1)} %states.3, f32[1,8192]{1,0:T(1,128)} %bitcast.25, f32[1,8192]{1,0:T(1,128)} %bitcast.26), custom_call_target="tpu_custom_call" | custom-call | tf_op jit(solution)/shard_map/half_rows/pallas_call | solution.py:76
  81.4 5.3 %collective-permute-start = (bf16[128,4096]{1,0:T(8,128)(2,1)}, bf16[128,4096]{1,0:T(8,128)(2,1)S(1)}, u32[]{:S(2)}, u32[]{:S(2)}) collective-permute-start(bf16[128,4096]{1,0:T(8,128)(2,1)} %get-tuple-element.8), channel_id=1, source_target_pairs={{0,1},{1,0},{2,3},{3,2},{4,5},{5,4},{6,7},{7,6},{8,9},{9,8},{10,11... | collective-permute-start | bytes 3145736 | tf_op jit(solution)/shard_map/ppermute | solution.py:22
  86.7 10.1 %all-to-all-done.1.parts = f32[8,2,4,8,256]{4,3,2,1,0:T(8,128)S(1)} async-done(((f32[8,2,4,8,256]{4,3,2,1,0:T(8,128)}), f32[8,2,4,8,256]{4,3,2,1,0:T(8,128)S(1)}, u32[]{:S(2)}, u32[]{:S(2)}) %all-to-all-start.1) | async-done | bytes 524320 | tf_op jit(solution)/shard_map/all_to_all | solution.py:26
  96.8 0.8 copy-done.2
  97.7 2.0 key_value_pairs.1
  99.7 6.2 %all-to-all-start.2 = ((bf16[16,8,8,256]{3,2,1,0:T(8,128)(2,1)}), bf16[16,8,8,256]{3,2,1,0:T(8,128)(2,1)S(1)}, u32[]{:S(2)}, u32[]{:S(2)}) async-start(bf16[16,8,8,256]{3,2,1,0:T(8,128)(2,1)} %key_value_pairs.1), calls=%async_computation.2 | async-start | bytes 1048576 | tf_op jit(solution)/shard_map/all_to_all | solution.py:26
  105.9 32.6 %collective-permute-done = bf16[128,4096]{1,0:T(8,128)(2,1)S(1)} collective-permute-done((bf16[128,4096]{1,0:T(8,128)(2,1)}, bf16[128,4096]{1,0:T(8,128)(2,1)S(1)}, u32[]{:S(2)}, u32[]{:S(2)}) %collective-permute-start) | collective-permute-done | bytes 1048608 | tf_op jit(solution)/shard_map/ppermute | solution.py:22
  138.6 1.9 collective-permute-start.2
  140.5 9.3 %all-to-all-done.2 = bf16[16,8,8,256]{3,2,1,0:T(8,128)(2,1)S(1)} async-done(((bf16[16,8,8,256]{3,2,1,0:T(8,128)(2,1)}), bf16[16,8,8,256]{3,2,1,0:T(8,128)(2,1)S(1)}, u32[]{:S(2)}, u32[]{:S(2)}) %all-to-all-start.2) | async-done | bytes 524320 | tf_op jit(solution)/shard_map/all_to_all | solution.py:26
  149.8 0.0 copy-start.3
  149.9 4.2 %collective-permute-start.9 = (bf16[8,128,256]{2,1,0:T(8,128)(2,1)S(1)}, bf16[8,128,256]{2,1,0:T(8,128)(2,1)S(1)}, u32[]{:S(2)}, u32[]{:S(2)}) collective-permute-start(bf16[8,128,256]{2,1,0:T(8,128)(2,1)S(1)} %copy_bitcast_fusion.own), channel_id=1, source_target_pairs={{0,16},{16,32},{32,48},{48,0},{1,17},{17,33},{33,49},{49,1},{2,18}... | collective-permute-start | bytes 1572872 | tf_op jit(solution)/shard_map/ppermute | solution.py:22
  154.1 2.8 %collective-permute-start.10 = (bf16[8,128,256]{2,1,0:T(8,128)(2,1)S(1)}, bf16[8,128,256]{2,1,0:T(8,128)(2,1)S(1)}, u32[]{:S(2)}, u32[]{:S(2)}) collective-permute-start(bf16[8,128,256]{2,1,0:T(8,128)(2,1)S(1)} %copy_bitcast_fusion.own), channel_id=1, source_target_pairs={{0,48},{16,0},{32,16},{48,32},{1,49},{17,1},{33,17},{49,33},{2,50}... | collective-permute-start | bytes 1572872 | tf_op jit(solution)/shard_map/ppermute | solution.py:22
  157.6 0.6 pad_add_fusion.choice
  158.2 4.8 %half_rows.3 = bf16[256,4096]{1,0:T(8,128)(2,1)} custom-call(s32[2]{0:T(128)} %pad_add_fusion.choice, bf16[256,8192]{1,0:T(8,128)(2,1)} %states.3, f32[1,8192]{1,0:T(1,128)} %bitcast.27, bf16[256,4096]{1,0:T(8,128)(2,1)} %get-tuple-element.7.rest_0_), custom_call_target="tpu_custom_call", output_to_operand_aliasing={{}: (3, {})} | custom-call | tf_op jit(solution)/shard_map/half_rows/pallas_call | solution.py:76
  163.0 0.0 copy-done.3
  163.0 3.5 %collective-permute-done.9.after = bf16[8,128,256]{2,1,0:T(8,128)(2,1)S(1)} collective-permute-done((bf16[8,128,256]{2,1,0:T(8,128)(2,1)S(1)}, bf16[8,128,256]{2,1,0:T(8,128)(2,1)S(1)}, u32[]{:S(2)}, u32[]{:S(2)}) %collective-permute-start.9) | collective-permute-done | bytes 524320 | tf_op jit(solution)/shard_map/ppermute | solution.py:22
  166.5 3.0 %collective-permute-start.11 = (bf16[4,128,256]{2,1,0:T(8,128)(2,1)S(1)}, bf16[4,128,256]{2,1,0:T(8,128)(2,1)S(1)}, u32[]{:S(2)}, u32[]{:S(2)}) collective-permute-start(bf16[4,128,256]{2,1,0:T(8,128)(2,1)S(1)} %slice.8), channel_id=1, source_target_pairs={{0,16},{16,32},{32,48},{48,0},{1,17},{17,33},{33,49},{49,1},{2,18}... | collective-permute-start | bytes 786440 | tf_op jit(solution)/shard_map/ppermute | solution.py:22
  169.6 0.0 collective-permute-done.10.before
  169.6 0.0 copy-start.6
  169.6 4.0 %collective-permute-start.12 = (bf16[4,128,256]{2,1,0:T(8,128)(2,1)S(1)}, bf16[4,128,256]{2,1,0:T(8,128)(2,1)S(1)}, u32[]{:S(2)}, u32[]{:S(2)}) collective-permute-start(bf16[4,128,256]{2,1,0:T(8,128)(2,1)S(1)} %slice.9), channel_id=1, source_target_pairs={{0,48},{16,0},{32,16},{48,32},{1,49},{17,1},{33,17},{49,33},{2,50}... | collective-permute-start | bytes 786440 | tf_op jit(solution)/shard_map/ppermute | solution.py:22
  173.7 0.0 all-gather.2.cloned.1.call-done
  173.7 0.0 copy-start
  173.7 0.0 copy-start.4
  173.7 3.1 %fusion.1 = f32[128,512]{1,0:T(8,128)S(1)} fusion(bf16[128,4096]{1,0:T(8,128)(2,1)S(1)} %collective-permute-done, bf16[4096,512]{1,0:T(8,128)(2,1)} %all-gather.2.cloned.1.call-done), kind=kOutput, calls=%fused_computation.7 | convolution fusion | flops 536870912 | bytes 5505024 | tf_op jit(solution)/shard_map/dot_general | solution.py:329
  176.8 5.8 %collective-permute-start.1 = (f32[128,512]{1,0:T(8,128)S(1)}, f32[128,512]{1,0:T(8,128)S(1)}, u32[]{:S(2)}, u32[]{:S(2)}) collective-permute-start(f32[128,512]{1,0:T(8,128)S(1)} %fusion.1), channel_id=1, source_target_pairs={{0,1},{1,0},{2,3},{3,2},{4,5},{5,4},{6,7},{7,6},{8,9},{9,8},{10,11... | collective-permute-start | bytes 786440 | tf_op jit(solution)/shard_map/ppermute | solution.py:22
  182.6 0.0 collective-permute-done.2
  182.6 0.0 copy-done
  182.6 2.0 fusion.2
  184.6 4.1 %collective-permute-start.3 = (f32[128,512]{1,0:T(8,128)S(1)}, f32[128,512]{1,0:T(8,128)S(1)}, u32[]{:S(2)}, u32[]{:S(2)}) collective-permute-start(f32[128,512]{1,0:T(8,128)S(1)} %fusion.2), channel_id=1, source_target_pairs={{0,1},{1,0},{2,3},{3,2},{4,5},{5,4},{6,7},{7,6},{8,9},{9,8},{10,11... | collective-permute-start | bytes 786440 | tf_op jit(solution)/shard_map/ppermute | solution.py:22
  188.7 2.0 fusion.query
  190.8 0.0 collective-permute-done.11.low
  190.8 0.0 collective-permute-done.12.high
  190.8 0.0 collective-permute-done.1.near
  190.8 6.0 %collective-permute-done.3.far = f32[128,512]{1,0:T(8,128)S(1)} collective-permute-done((f32[128,512]{1,0:T(8,128)S(1)}, f32[128,512]{1,0:T(8,128)S(1)}, u32[]{:S(2)}, u32[]{:S(2)}) %collective-permute-start.3) | collective-permute-done | bytes 262176 | tf_op jit(solution)/shard_map/ppermute | solution.py:22
  196.8 0.0 copy-done.11
  196.8 0.7 copy-done.12
  197.5 7.4 %attention.1 = bf16[256,512]{1,0:T(8,128)(2,1)} custom-call(s32[1]{0:T(128)} %bitcast.odd.core, s32[4,4]{1,0:T(4,128)} %owners.1, s32[4]{0:T(128)} %counts.1, f32[1]{0:T(128)S(6)} %tanh.3.gate, f32[256,512]{1,0:T(8,128)} %fusion.query, f32[128,512]{1,0:T(8,128)} %copy-done.11, f32[128,512]{1,0:T(8,128)} %copy-done.12, f32[1,128]{1,0:T(1,128)} %bitcast.30, ...), custom_call_target="tpu_custom_call" | custom-call | tf_op jit(solution)/shard_map/attention/pallas_call | solution.py:246
  (19 shorter events, 0.1 us)
Async XLA Ops:
  6.5 167.1 %all-gather.2.cloned.1.call-start = ((), (), s32[]{:S(2)}) async-start(), calls=%async_computation.3 | async-start | bytes 4325376 | tf_op jit(solution)/shard_map/all_gather | solution.py:282
  38.3 30.1 %copy-start.1 = (bf16[32,8,1024]{2,1,0:T(8,128)(2,1)}, bf16[32,8,1024]{2,1,0:T(8,128)(2,1)S(1)}, u32[]{:S(2)}) copy-start(bf16[32,8,1024]{2,1,0:T(8,128)(2,1)S(1)} %all_to_all.15) | copy-start | bytes 1572868
  38.3 30.1 %collective-permute-start.4 = (bf16[32,8,1024]{2,1,0:T(8,128)(2,1)S(1)}, bf16[32,8,1024]{2,1,0:T(8,128)(2,1)S(1)}, u32[]{:S(2)}, u32[]{:S(2)}) collective-permute-start(bf16[32,8,1024]{2,1,0:T(8,128)(2,1)S(1)} %all_to_all.15), channel_id=1, source_target_pairs={{0,64},{64,0},{1,65},{65,1},{2,66},{66,2},{3,67},{67,3},{4,68},{68... | collective-permute-start | bytes 1572872 | tf_op jit(solution)/shard_map/ppermute | solution.py:22
  41.8 11.7 %collective-permute-start.5 = (bf16[128,256]{1,0:T(8,128)(2,1)S(1)}, bf16[128,256]{1,0:T(8,128)(2,1)S(1)}, u32[]{:S(2)}, u32[]{:S(2)}) collective-permute-start(bf16[128,256]{1,0:T(8,128)(2,1)S(1)} %constant_dynamic-update-slice_fusion), channel_id=1, source_target_pairs={{0,1},{1,0},{2,3},{3,2},{4,5},{5,4},{6,7},{7,6},{8,9},{9,8},{10,11... | collective-permute-start | bytes 196616 | tf_op jit(solution)/shard_map/ppermute | solution.py:22
  53.5 14.9 %copy-start.8 = (bf16[256,256]{1,0:T(8,128)(2,1)}, bf16[256,256]{1,0:T(8,128)(2,1)S(1)}, u32[]{:S(2)}) copy-start(bf16[256,256]{1,0:T(8,128)(2,1)S(1)} %maximum_select_fusion.rest_0_) | copy-start | bytes 393220
  53.5 11.4 %collective-permute-start.6 = (bf16[256,256]{1,0:T(8,128)(2,1)S(1)}, bf16[256,256]{1,0:T(8,128)(2,1)S(1)}, u32[]{:S(2)}, u32[]{:S(2)}) collective-permute-start(bf16[256,256]{1,0:T(8,128)(2,1)S(1)} %maximum_select_fusion.rest_0_), channel_id=1, source_target_pairs={{0,16},{16,32},{32,48},{48,0},{1,17},{17,33},{33,49},{49,1},{2,18}... | collective-permute-start | bytes 393224 | tf_op jit(solution)/shard_map/ppermute | solution.py:22
  56.9 8.4 %collective-permute-start.7 = (bf16[256,256]{1,0:T(8,128)(2,1)S(1)}, bf16[256,256]{1,0:T(8,128)(2,1)S(1)}, u32[]{:S(2)}, u32[]{:S(2)}) collective-permute-start(bf16[256,256]{1,0:T(8,128)(2,1)S(1)} %maximum_select_fusion.rest_0_), channel_id=1, source_target_pairs={{0,32},{16,48},{32,0},{48,16},{1,33},{17,49},{33,1},{49,17},{2,34}... | collective-permute-start | bytes 393224 | tf_op jit(solution)/shard_map/ppermute | solution.py:22
  61.6 6.9 %collective-permute-start.8 = (bf16[256,256]{1,0:T(8,128)(2,1)S(1)}, bf16[256,256]{1,0:T(8,128)(2,1)S(1)}, u32[]{:S(2)}, u32[]{:S(2)}) collective-permute-start(bf16[256,256]{1,0:T(8,128)(2,1)S(1)} %maximum_select_fusion.rest_0_), channel_id=1, source_target_pairs={{0,48},{16,0},{32,16},{48,32},{1,49},{17,1},{33,17},{49,33},{2,50}... | collective-permute-start | bytes 393224 | tf_op jit(solution)/shard_map/ppermute | solution.py:22
  64.9 3.5 %copy-start.13 = (bf16[256,256]{1,0:T(8,128)(2,1)}, bf16[256,256]{1,0:T(8,128)(2,1)S(1)}, u32[]{:S(2)}) copy-start(bf16[256,256]{1,0:T(8,128)(2,1)S(1)} %collective-permute-done.6.rest_1_) | copy-start | bytes 393220
  65.3 3.2 %copy-start.14 = (bf16[256,256]{1,0:T(8,128)(2,1)}, bf16[256,256]{1,0:T(8,128)(2,1)S(1)}, u32[]{:S(2)}) copy-start(bf16[256,256]{1,0:T(8,128)(2,1)S(1)} %collective-permute-done.7.rest_2_) | copy-start | bytes 393220
  68.4 0.7 copy-start.15
  68.4 0.9 copy-start.7
  71.9 24.9 %all-to-all-start.1 = ((f32[8,2,4,8,256]{4,3,2,1,0:T(8,128)}), f32[8,2,4,8,256]{4,3,2,1,0:T(8,128)S(1)}, u32[]{:S(2)}, u32[]{:S(2)}) async-start(f32[8,2,4,8,256]{4,3,2,1,0:T(8,128)} %partial_sums.1), calls=%async_computation.1 | async-start | bytes 1048576 | tf_op jit(solution)/shard_map/all_to_all | solution.py:26
  81.4 57.1 %collective-permute-start = (bf16[128,4096]{1,0:T(8,128)(2,1)}, bf16[128,4096]{1,0:T(8,128)(2,1)S(1)}, u32[]{:S(2)}, u32[]{:S(2)}) collective-permute-start(bf16[128,4096]{1,0:T(8,128)(2,1)} %get-tuple-element.8), channel_id=1, source_target_pairs={{0,1},{1,0},{2,3},{3,2},{4,5},{5,4},{6,7},{7,6},{8,9},{9,8},{10,11... | collective-permute-start | bytes 3145736 | tf_op jit(solution)/shard_map/ppermute | solution.py:22
  96.8 0.8 copy-start.2
  99.7 50.1 %all-to-all-start.2 = ((bf16[16,8,8,256]{3,2,1,0:T(8,128)(2,1)}), bf16[16,8,8,256]{3,2,1,0:T(8,128)(2,1)S(1)}, u32[]{:S(2)}, u32[]{:S(2)}) async-start(bf16[16,8,8,256]{3,2,1,0:T(8,128)(2,1)} %key_value_pairs.1), calls=%async_computation.2 | async-start | bytes 1048576 | tf_op jit(solution)/shard_map/all_to_all | solution.py:26
  138.6 44.0 %collective-permute-start.2 = (bf16[128,4096]{1,0:T(8,128)(2,1)S(1)}, bf16[128,4096]{1,0:T(8,128)(2,1)}, u32[]{:S(2)}, u32[]{:S(2)}) collective-permute-start(bf16[128,4096]{1,0:T(8,128)(2,1)S(1)} %collective-permute-done), channel_id=1, source_target_pairs={{0,64},{64,0},{1,65},{65,1},{2,66},{66,2},{3,67},{67,3},{4,68},{68... | collective-permute-start | bytes 3145736 | tf_op jit(solution)/shard_map/ppermute | solution.py:22
  149.8 13.2 %copy-start.3 = (bf16[8,128,256]{2,1,0:T(8,128)(2,1)}, bf16[8,128,256]{2,1,0:T(8,128)(2,1)S(1)}, u32[]{:S(2)}) copy-start(bf16[8,128,256]{2,1,0:T(8,128)(2,1)S(1)} %copy_bitcast_fusion.own) | copy-start | bytes 1572868
  149.9 16.7 %collective-permute-start.9 = (bf16[8,128,256]{2,1,0:T(8,128)(2,1)S(1)}, bf16[8,128,256]{2,1,0:T(8,128)(2,1)S(1)}, u32[]{:S(2)}, u32[]{:S(2)}) collective-permute-start(bf16[8,128,256]{2,1,0:T(8,128)(2,1)S(1)} %copy_bitcast_fusion.own), channel_id=1, source_target_pairs={{0,16},{16,32},{32,48},{48,0},{1,17},{17,33},{33,49},{49,1},{2,18}... | collective-permute-start | bytes 1572872 | tf_op jit(solution)/shard_map/ppermute | solution.py:22
  154.1 15.5 %collective-permute-start.10 = (bf16[8,128,256]{2,1,0:T(8,128)(2,1)S(1)}, bf16[8,128,256]{2,1,0:T(8,128)(2,1)S(1)}, u32[]{:S(2)}, u32[]{:S(2)}) collective-permute-start(bf16[8,128,256]{2,1,0:T(8,128)(2,1)S(1)} %copy_bitcast_fusion.own), channel_id=1, source_target_pairs={{0,48},{16,0},{32,16},{48,32},{1,49},{17,1},{33,17},{49,33},{2,50}... | collective-permute-start | bytes 1572872 | tf_op jit(solution)/shard_map/ppermute | solution.py:22
  166.5 18.1 %copy-start.5 = (bf16[8,128,256]{2,1,0:T(8,128)(2,1)}, bf16[8,128,256]{2,1,0:T(8,128)(2,1)S(1)}, u32[]{:S(2)}) copy-start(bf16[8,128,256]{2,1,0:T(8,128)(2,1)S(1)} %collective-permute-done.9.after) | copy-start | bytes 1572868
  166.5 24.2 %collective-permute-start.11 = (bf16[4,128,256]{2,1,0:T(8,128)(2,1)S(1)}, bf16[4,128,256]{2,1,0:T(8,128)(2,1)S(1)}, u32[]{:S(2)}, u32[]{:S(2)}) collective-permute-start(bf16[4,128,256]{2,1,0:T(8,128)(2,1)S(1)} %slice.8), channel_id=1, source_target_pairs={{0,16},{16,32},{32,48},{48,0},{1,17},{17,33},{33,49},{49,1},{2,18}... | collective-permute-start | bytes 786440 | tf_op jit(solution)/shard_map/ppermute | solution.py:22
  169.6 15.0 %copy-start.6 = (bf16[8,128,256]{2,1,0:T(8,128)(2,1)}, bf16[8,128,256]{2,1,0:T(8,128)(2,1)S(1)}, u32[]{:S(2)}) copy-start(bf16[8,128,256]{2,1,0:T(8,128)(2,1)S(1)} %collective-permute-done.10.before) | copy-start | bytes 1572868
  169.6 21.2 %collective-permute-start.12 = (bf16[4,128,256]{2,1,0:T(8,128)(2,1)S(1)}, bf16[4,128,256]{2,1,0:T(8,128)(2,1)S(1)}, u32[]{:S(2)}, u32[]{:S(2)}) collective-permute-start(bf16[4,128,256]{2,1,0:T(8,128)(2,1)S(1)} %slice.9), channel_id=1, source_target_pairs={{0,48},{16,0},{32,16},{48,32},{1,49},{17,1},{33,17},{49,33},{2,50}... | collective-permute-start | bytes 786440 | tf_op jit(solution)/shard_map/ppermute | solution.py:22
  173.7 8.9 %copy-start = (bf16[4096,512]{1,0:T(8,128)(2,1)S(1)}, bf16[4096,512]{1,0:T(8,128)(2,1)}, u32[]{:S(2)}) copy-start(bf16[4096,512]{1,0:T(8,128)(2,1)} %all-gather.2.cloned.1.call-done) | copy-start | bytes 12582916
  173.7 15.0 %copy-start.4 = (bf16[256,4096]{1,0:T(8,128)(2,1)S(1)}, bf16[256,4096]{1,0:T(8,128)(2,1)}, u32[]{:S(2)}) copy-start(bf16[256,4096]{1,0:T(8,128)(2,1)} %half_rows.3) | copy-start | bytes 6291460
  176.8 14.0 %collective-permute-start.1 = (f32[128,512]{1,0:T(8,128)S(1)}, f32[128,512]{1,0:T(8,128)S(1)}, u32[]{:S(2)}, u32[]{:S(2)}) collective-permute-start(f32[128,512]{1,0:T(8,128)S(1)} %fusion.1), channel_id=1, source_target_pairs={{0,1},{1,0},{2,3},{3,2},{4,5},{5,4},{6,7},{7,6},{8,9},{9,8},{10,11... | collective-permute-start | bytes 786440 | tf_op jit(solution)/shard_map/ppermute | solution.py:22
  184.6 12.2 %collective-permute-start.3 = (f32[128,512]{1,0:T(8,128)S(1)}, f32[128,512]{1,0:T(8,128)S(1)}, u32[]{:S(2)}, u32[]{:S(2)}) collective-permute-start(f32[128,512]{1,0:T(8,128)S(1)} %fusion.2), channel_id=1, source_target_pairs={{0,1},{1,0},{2,3},{3,2},{4,5},{5,4},{6,7},{7,6},{8,9},{9,8},{10,11... | collective-permute-start | bytes 786440 | tf_op jit(solution)/shard_map/ppermute | solution.py:22
  190.8 6.0 %copy-start.9 = (bf16[4,128,256]{2,1,0:T(8,128)(2,1)}, bf16[4,128,256]{2,1,0:T(8,128)(2,1)S(1)}, u32[]{:S(2)}) copy-start(bf16[4,128,256]{2,1,0:T(8,128)(2,1)S(1)} %collective-permute-done.11.low) | copy-start | bytes 786436
  190.8 6.0 %copy-start.10 = (bf16[4,128,256]{2,1,0:T(8,128)(2,1)}, bf16[4,128,256]{2,1,0:T(8,128)(2,1)S(1)}, u32[]{:S(2)}) copy-start(bf16[4,128,256]{2,1,0:T(8,128)(2,1)S(1)} %collective-permute-done.12.high) | copy-start | bytes 786436
  190.8 6.0 %copy-start.11 = (f32[128,512]{1,0:T(8,128)}, f32[128,512]{1,0:T(8,128)S(1)}, u32[]{:S(2)}) copy-start(f32[128,512]{1,0:T(8,128)S(1)} %collective-permute-done.1.near) | copy-start | bytes 786436
  196.8 0.7 copy-start.12
Sparse Core Ops, SparseCore 0:
  10.5 99.3 all-gather.1

commit v2 on v1

--- a/solution.py
+++ b/solution.py
@@ -38,30 +38,33 @@
 scalar = pl.BlockSpec(memory_space=pltpu.SMEM)
 
 
-def half_kernel(choice, states, gain, *rest):
+def half_kernel(x, z, choice, states, gain, *rest):
     outs = rest[1:]
     rows, width = states.shape
     depth = 128
+    span = width // (x * z)
     squares = jnp.zeros((rows, depth), jnp.float32)
     for j in range(width // depth):
         wide = states[:, j * depth : (j + 1) * depth].astype(jnp.float32)
         squares += wide * wide
     scale = lax.rsqrt(jnp.sum(squares, axis=-1, keepdims=True) / width + norm_epsilon)
-    pair = choice[1] == 0
-    for j in range(width // depth // 2):
-        low = slice(2 * j * depth, (2 * j + 1) * depth)
-        high = slice((2 * j + 1) * depth, (2 * j + 2) * depth)
-        blocks = [
-            (states[:, at].astype(jnp.float32) * scale * gain[:, at]).astype(jnp.bfloat16)
-            for at in (low, high)
-        ]
-        lanes = slice(j * depth, (j + 1) * depth)
-        outs[0][:, lanes] = jnp.where(pair, blocks[0], blocks[1])
-        if len(outs) > 1:
-            outs[1][:, lanes] = jnp.where(pair, blocks[1], blocks[0])
-
-
-def half_rows(states, gain, choice, base):
+    even = choice[1] == 0
+    for k in range(z):
+        for m in range(x // 2):
+            blocks = []
+            for p in range(2):
+                start = ((2 * m + p) * z + k) * span
+                at = slice(start, start + span)
+                wide = states[:, at].astype(jnp.float32)
+                blocks.append((wide * scale * gain[:, at]).astype(jnp.bfloat16))
+            start = (k * (x // 2) + m) * span
+            lanes = slice(start, start + span)
+            outs[0][:, lanes] = jnp.where(even, blocks[0], blocks[1])
+            if len(outs) > 1:
+                outs[1][:, lanes] = jnp.where(even, blocks[1], blocks[0])
+
+
+def half_rows(states, gain, choice, base, x, z):
     total, width = states.shape
     rows = 32
     steps = total // 2 // rows
@@ -74,7 +77,7 @@
         shapes.append(jax.ShapeDtypeStruct((total // 2, width // 2), jnp.bfloat16))
         places.append(pl.BlockSpec((rows, width // 2), lambda i, c: (i, 0)))
     return pl.pallas_call(
-        half_kernel,
+        functools.partial(half_kernel, x, z),
         grid_spec=pltpu.PrefetchScalarGridSpec(
             num_scalar_prefetch=1,
             grid=(steps,),
@@ -89,6 +92,27 @@
         input_output_aliases={} if base is None else {3: 0},
         name="half_rows",
     )(choice, states, gain, *held)
+
+
+def join_kernel(*refs):
+    *parts, out = refs
+    start = 0
+    for part in parts:
+        width = part.shape[1]
+        out[:, start : start + width] = part[...]
+        start += width
+
+
+def join(*parts):
+    shape = (parts[0].shape[0], sum(p.shape[1] for p in parts))
+    return pl.pallas_call(
+        join_kernel,
+        in_specs=[whole(p.shape) for p in parts],
+        out_specs=whole(shape),
+        grid=(1,),
+        out_shape=jax.ShapeDtypeStruct(shape, parts[0].dtype),
+        name="join",
+    )(*parts)
 
 
 def columns_kernel(x, vision, out):
@@ -132,11 +156,16 @@
                 out[k, c, a] = product[row : row + tokens]
 
 
-def partial_sums(here, there, spot, weights, z, yl, tokens):
-    shape = (z, 2, yl, tokens, weights[0].shape[1])
+def partial_sums(here, there, spot, weights, width, z, yl, tokens):
+    shape = (z, 2, yl, tokens, width)
     return pl.pallas_call(
         partial_kernel,
-        in_specs=[scalar, whole(here.shape), whole(there.shape), *(whole(w.shape) for w in weights)],
+        in_specs=[
+            scalar,
+            whole(here.shape),
+            whole(there.shape),
+            *(whole((w.shape[0], width)) for w in weights),
+        ],
         out_specs=whole(shape),
         grid=(1,),
         out_shape=jax.ShapeDtypeStruct(shape, jnp.float32),
@@ -277,40 +306,51 @@
     tokens = vision.shape[1]
     width = text_states.shape[1]
     yl, co, x, z, yh = (lax.axis_size(a) for a in IMG + FSDP)
-    first = lax.axis_index("yh") == 0
-
-    q_half = lax.all_gather(q_weight, ("x", "z"), axis=0, tiled=True)
+    place = lax.axis_index("x")
+    core = lax.axis_index("co")
+
+    def ordered(early, mine, other):
+        return jnp.where(
+            early,
+            jnp.concatenate((mine, other), axis=0),
+            jnp.concatenate((other, mine), axis=0),
+        )
+
+    joined = join(k_weight, v_weight, q_weight)
+    other = shift(joined, "yh", 1)
+    both = ordered(lax.axis_index("yh") == 0, joined, other)
+    far = shift(both, "x", 2)
+    near = both[:, : 2 * head]
+    pair_weight = (both, shift(near, "x", 1), far, shift(near, "x", 3))
+
+    rows_q = ordered(place < 2, both[:, 2 * head :], far[:, 2 * head :])
+    q_half = lax.all_gather(rows_q, "z", axis=0, tiled=True)
 
     columns = columns_of(vision.reshape(tokens, width), yl, x, z)
     here = exchange(columns.reshape(yl * z, tokens, width // z), ("yl", "z"))
 
-    joined = jnp.concatenate((k_weight, v_weight), axis=1)
-    other = shift(joined, "yh", 1)
-    both = jnp.where(
-        first,
-        jnp.concatenate((joined, other), axis=0),
-        jnp.concatenate((other, joined), axis=0),
-    )
-    pair_weight = (both, *(shift(both, "x", k) for k in range(1, x)))
-
     gate = jnp.tanh(gate_value)
 
-    core = lax.axis_index("co")
-    mine = lax.axis_index("yh")
+    mine = lax.rem(place, 2)
     gain = text_gain[None]
+
+    def partner(array):
+        return lax.ppermute(array, "x", [(i, i ^ 1) for i in range(x)])
+
     choice = jnp.stack((core, mine)).astype(jnp.int32)
-    text_half, sent = half_rows(text_states, gain, choice, None)
-    guest = shift(sent, "yh", 1)
+    text_half, sent = half_rows(text_states, gain, choice, None, x, z)
+    guest = partner(sent)
     guest_other = shift(guest, "co", 1)
     choice = jnp.stack((1 - core, mine)).astype(jnp.int32)
-    (text_half,) = half_rows(text_states, gain, choice, text_half)
+    (text_half,) = half_rows(text_states, gain, choice, text_half, x, z)
 
     there = shift(here, "co", 1)
     partial = partial_sums(
         here.reshape(yl * z * tokens, width // z),
         there.reshape(yl * z * tokens, width // z),
-        lax.axis_index("x").astype(jnp.int32)[None],
+        place.astype(jnp.int32)[None],
         pair_weight,
+        2 * head,
         z,
         yl,
         tokens,
@@ -328,8 +368,8 @@
 
     guest_near = jnp.dot(guest, q_half, preferred_element_type=jnp.float32)
     guest_far = jnp.dot(guest_other, q_half, preferred_element_type=jnp.float32)
-    back_near = shift(guest_near, "yh", 1)
-    back_far = shift(guest_far, "yh", 1)
+    back_near = partner(guest_near)
+    back_far = partner(guest_far)
     query = jnp.dot(text_half, q_half, preferred_element_type=jnp.float32)
     return attention(
         core.astype(jnp.int32)[None],

time: 213 us -> 204 us (0.958)
  waiting for transfers between devices: 72.5 us -> 66.6 us
  starting transfers between devices: 59.5 us -> 56.3 us
  other arithmetic: 1.19 us -> 3.34 us
    ppermute x13 -> x10, waiting for transfers between devices: 52.3 us -> 27.7 us  [shift(): lax.ppermute(array, axis, [(i, (i + step) % size) for i in range(size)])]
    all_to_all x2, waiting for transfers between devices: 19.5 us -> 33.5 us  [exchange(): return lax.all_to_all(array, axes, 0, 0, tiled=True)]
    ppermute x13 -> x10, starting transfers between devices: 49.5 us -> 35.8 us  [shift(): lax.ppermute(array, axis, [(i, (i + step) % size) for i in range(size)])]
    ppermute x0 -> x3, starting transfers between devices: none -> 9.35 us  [partner(): return lax.ppermute(array, 'x', [(i, i ^ 1) for i in range(x)])]
    ppermute x0 -> x3, waiting for transfers between devices: none -> 5.36 us  [partner(): return lax.ppermute(array, 'x', [(i, i ^ 1) for i in range(x)])]
    dot_general x1, matrix products: 3.06 us -> 0.78 us  [on_device(): guest_near = jnp.dot(guest, q_half, preferred_element_type=jnp.float32)]
    select_n x1 -> x2, other arithmetic: 0.03 us -> 2.16 us  [ordered(): jnp.where(early, jnp.concatenate((mine, other), axis=0), jnp.concatenate(...]
    pallas_call x2 -> x3, Pallas kernels: 9.9 us -> 11.5 us  [the longest x2 9.85 us: half_rows(): pl.pallas_call(functools.partial(half_kernel, x, z), grid_spec=pltpu.Pref...]
  transfers between devices with their start and end apart: 16 -> 16, of which waited for: 8 -> 9; matrix products, arithmetic and copies ran while one was open for 5% -> 4% of each run, Pallas kernels for 8% -> 8%
where the time goes in v2:
time: 204 us; the launch traced here: 203 us
  waiting for transfers between devices  66.6 us (33%)
  starting transfers between devices  56.3 us (28%)
  blocking collectives  28 us (14%)
  Pallas kernels  25.3 us (12%)
  between operations  14.4 us (7%)
  matrix products  6.19 us (3%)
  other arithmetic  3.34 us (2%)
  local copies, waits for them, and re-layouts  2.51 us (1%)
    ppermute x10, starting transfers between devices, shift(): lax.ppermute(array, axis, [(i, (i + step) % size) for i in range(size)])  35.8 us
    all_to_all x2, waiting for transfers between devices, exchange(): return lax.all_to_all(array, axes, 0, 0, tiled=True)  33.5 us
    all_to_all x1, blocking collectives, exchange(): return lax.all_to_all(array, axes, 0, 0, tiled=True)  28 us
    ppermute x10, waiting for transfers between devices, shift(): lax.ppermute(array, axis, [(i, (i + step) % size) for i in range(size)])  27.7 us
    all_to_all x2, starting transfers between devices, exchange(): return lax.all_to_all(array, axes, 0, 0, tiled=True)  11.1 us
    pallas_call x2, Pallas kernels, half_rows(): pl.pallas_call(functools.partial(half_kernel, x, z), grid_spec=pltpu.Pref...  9.85 us
    ppermute x3, starting transfers between devices, partner(): return lax.ppermute(array, 'x', [(i, i ^ 1) for i in range(x)])  9.35 us
    pallas_call x1, Pallas kernels, attention(): pl.pallas_call(attention_kernel, grid=(blocks,), in_specs=[*(scalar,) * 4...  7.42 us
  transfers between devices with their start and end apart: 16, of which 9 were waited for; matrix products, arithmetic and copies ran while one was open for 4% of the time, Pallas kernels for 8%

profile of v2, /device:TPU:80, one launch (start us, length us, event | category | flops | bytes accessed | tf_op | source)
XLA Modules:
  0.0 202.6 jit_solution(15192203590782965781)
XLA Ops:
  6.5 0.0 all-gather.2.cloned.1.call-start
  6.5 1.6 join.1
  8.2 5.9 %collective-permute-start = (bf16[128,768]{1,0:T(8,128)(2,1)}, bf16[128,768]{1,0:T(8,128)(2,1)S(1)}, u32[]{:S(2)}, u32[]{:S(2)}) collective-permute-start(bf16[128,768]{1,0:T(8,128)(2,1)} %join.1), channel_id=1, source_target_pairs={{0,1},{1,0},{2,3},{3,2},{4,5},{5,4},{6,7},{7,6},{8,9},{9,8},{10,11... | collective-permute-start | bytes 589832 | tf_op jit(solution)/shard_map/ppermute | solution.py:22
  14.1 11.0 %collective-permute-done = bf16[128,768]{1,0:T(8,128)(2,1)S(1)} collective-permute-done((bf16[128,768]{1,0:T(8,128)(2,1)}, bf16[128,768]{1,0:T(8,128)(2,1)S(1)}, u32[]{:S(2)}, u32[]{:S(2)}) %collective-permute-start) | collective-permute-done | bytes 196640 | tf_op jit(solution)/shard_map/ppermute | solution.py:22
  25.1 1.1 maximum_select_fusion.1.rest_0_
  26.2 0.0 copy-start.1
  26.2 4.9 %collective-permute-start.1 = (bf16[256,768]{1,0:T(8,128)(2,1)S(1)}, bf16[256,768]{1,0:T(8,128)(2,1)S(1)}, u32[]{:S(2)}, u32[]{:S(2)}) collective-permute-start(bf16[256,768]{1,0:T(8,128)(2,1)S(1)} %maximum_select_fusion.1.rest_0_), channel_id=1, source_target_pairs={{0,32},{16,48},{32,0},{48,16},{1,33},{17,49},{33,1},{49,17},{2,34}... | collective-permute-start | bytes 1179656 | tf_op jit(solution)/shard_map/ppermute | solution.py:22
  31.2 9.4 %collective-permute-done.1.rest_2_ = bf16[256,768]{1,0:T(8,128)(2,1)S(1)} collective-permute-done((bf16[256,768]{1,0:T(8,128)(2,1)S(1)}, bf16[256,768]{1,0:T(8,128)(2,1)S(1)}, u32[]{:S(2)}, u32[]{:S(2)}) %collective-permute-start.1) | collective-permute-done | bytes 393248 | tf_op jit(solution)/shard_map/ppermute | solution.py:22
  40.6 1.0 maximum_select_fusion
  41.6 0.0 all-gather.2.cloned.1.call-update
  41.6 1.8 columns.1
  43.4 28.0 %all_to_all.15 = bf16[32,8,1024]{2,1,0:T(8,128)(2,1)S(1)} all-to-all(bf16[32,8,1024]{2,1,0:T(8,128)(2,1)} %bitcast.22), channel_id=1, replica_groups=mesh['yl'=4,'co'=2,'x'=4,'z'=8,'yh'=2] {'yl','z'}, dimensions={0} | all-to-all | bytes 1048576 | tf_op jit(solution)/shard_map/all_to_all | solution.py:26
  71.4 1.9 collective-permute-start.6
  73.3 3.4 %collective-permute-start.7 = (bf16[256,256]{1,0:T(8,128)(2,1)S(1)}, bf16[256,256]{1,0:T(8,128)(2,1)S(1)}, u32[]{:S(2)}, u32[]{:S(2)}) collective-permute-start(bf16[256,256]{1,0:T(8,128)(2,1)S(1)} %slice.22), channel_id=1, source_target_pairs={{0,16},{16,32},{32,48},{48,0},{1,17},{17,33},{33,49},{49,1},{2,18}... | collective-permute-start | bytes 393224 | tf_op jit(solution)/shard_map/ppermute | solution.py:22
  76.7 3.7 %collective-permute-start.8 = (bf16[256,256]{1,0:T(8,128)(2,1)S(1)}, bf16[256,256]{1,0:T(8,128)(2,1)S(1)}, u32[]{:S(2)}, u32[]{:S(2)}) collective-permute-start(bf16[256,256]{1,0:T(8,128)(2,1)S(1)} %slice.22), channel_id=1, source_target_pairs={{0,48},{16,0},{32,16},{48,32},{1,49},{17,1},{33,17},{49,33},{2,50}... | collective-permute-start | bytes 393224 | tf_op jit(solution)/shard_map/ppermute | solution.py:22
  80.4 1.9 collective-permute-done.7.rest_1_
  82.3 1.9 collective-permute-done.8.rest_3_
  84.2 0.0 collective-permute-done.6
  84.2 0.0 copy-done.1
  84.2 0.0 copy-done.8
  84.2 0.0 copy-done.4
  84.3 0.0 copy-done.14
  84.3 0.6 copy-done.15
  84.9 0.2 copy-done.9
  85.1 2.6 %partial_sums.1 = f32[8,2,4,8,256]{4,3,2,1,0:T(8,128)} custom-call(s32[1]{0:T(128)} %bitcast.5.spot, bf16[256,1024]{1,0:T(8,128)(2,1)} %bitcast.23, bf16[256,1024]{1,0:T(8,128)(2,1)} %bitcast.24, bf16[256,768]{1,0:T(8,128)(2,1)} %copy-done.1, bf16[256,256]{1,0:T(8,128)(2,1)} %copy-done.14, bf16[256,768]{1,0:T(8,128)(2,1)} %copy-done.8, ...), custom_call_target="tpu_custom_call" | custom-call | tf_op jit(solution)/shard_map/partial_sums/pallas_call | solution.py:161
  87.7 4.5 %all-to-all-start.1 = ((f32[8,2,4,8,256]{4,3,2,1,0:T(8,128)}), f32[8,2,4,8,256]{4,3,2,1,0:T(8,128)S(1)}, u32[]{:S(2)}, u32[]{:S(2)}) async-start(f32[8,2,4,8,256]{4,3,2,1,0:T(8,128)} %partial_sums.1), calls=%async_computation.1 | async-start | bytes 1048576 | tf_op jit(solution)/shard_map/all_to_all | solution.py:26
  92.3 0.6 pad_add_fusion.1.choice
  92.8 5.0 %half_rows.2 = (bf16[256,4096]{1,0:T(8,128)(2,1)}, bf16[128,4096]{1,0:T(8,128)(2,1)}) custom-call(s32[2]{0:T(128)} %pad_add_fusion.1.choice, bf16[256,8192]{1,0:T(8,128)(2,1)} %states.3, f32[1,8192]{1,0:T(1,128)} %bitcast.25, f32[1,8192]{1,0:T(1,128)} %bitcast.26), custom_call_target="tpu_custom_call" | custom-call | tf_op jit(solution)/shard_map/half_rows/pallas_call | solution.py:79
  97.9 3.4 %collective-permute-start.2 = (bf16[128,4096]{1,0:T(8,128)(2,1)}, bf16[128,4096]{1,0:T(8,128)(2,1)S(1)}, u32[]{:S(2)}, u32[]{:S(2)}) collective-permute-start(bf16[128,4096]{1,0:T(8,128)(2,1)} %get-tuple-element.8), channel_id=1, source_target_pairs={{0,16},{16,0},{32,48},{48,32},{1,17},{17,1},{33,49},{49,33},{2,18}... | collective-permute-start | bytes 3145736 | tf_op jit(solution)/shard_map/ppermute | solution.py:338
  101.3 13.6 %all-to-all-done.1.parts = f32[8,2,4,8,256]{4,3,2,1,0:T(8,128)S(1)} async-done(((f32[8,2,4,8,256]{4,3,2,1,0:T(8,128)}), f32[8,2,4,8,256]{4,3,2,1,0:T(8,128)S(1)}, u32[]{:S(2)}, u32[]{:S(2)}) %all-to-all-start.1) | async-done | bytes 524320 | tf_op jit(solution)/shard_map/all_to_all | solution.py:26
  114.9 0.8 copy-done.2
  115.7 2.0 %key_value_pairs.1 = bf16[16,8,8,256]{3,2,1,0:T(8,128)(2,1)} custom-call(s32[1]{0:T(128)} %bitcast.odd.core, f32[8,2,4,8,256]{4,3,2,1,0:T(8,128)} %copy-done.2, f32[1,128]{1,0:T(1,128)} %bitcast.29), custom_call_target="tpu_custom_call" | custom-call | tf_op jit(solution)/shard_map/key_value_pairs/pallas_call | solution.py:202
  117.8 6.5 %all-to-all-start.2 = ((bf16[16,8,8,256]{3,2,1,0:T(8,128)(2,1)}), bf16[16,8,8,256]{3,2,1,0:T(8,128)(2,1)S(1)}, u32[]{:S(2)}, u32[]{:S(2)}) async-start(bf16[16,8,8,256]{3,2,1,0:T(8,128)(2,1)} %key_value_pairs.1), calls=%async_computation.2 | async-start | bytes 1048576 | tf_op jit(solution)/shard_map/all_to_all | solution.py:26
  124.3 0.0 collective-permute-done.2
  124.3 1.9 collective-permute-start.4
  126.3 19.8 %all-to-all-done.2 = bf16[16,8,8,256]{3,2,1,0:T(8,128)(2,1)S(1)} async-done(((bf16[16,8,8,256]{3,2,1,0:T(8,128)(2,1)}), bf16[16,8,8,256]{3,2,1,0:T(8,128)(2,1)S(1)}, u32[]{:S(2)}, u32[]{:S(2)}) %all-to-all-start.2) | async-done | bytes 524320 | tf_op jit(solution)/shard_map/all_to_all | solution.py:26
  146.1 0.0 copy-start.3
  146.1 3.4 %collective-permute-start.9 = (bf16[8,128,256]{2,1,0:T(8,128)(2,1)S(1)}, bf16[8,128,256]{2,1,0:T(8,128)(2,1)S(1)}, u32[]{:S(2)}, u32[]{:S(2)}) collective-permute-start(bf16[8,128,256]{2,1,0:T(8,128)(2,1)S(1)} %copy_bitcast_fusion.own), channel_id=1, source_target_pairs={{0,16},{16,32},{32,48},{48,0},{1,17},{17,33},{33,49},{49,1},{2,18}... | collective-permute-start | bytes 1572872 | tf_op jit(solution)/shard_map/ppermute | solution.py:22
  149.5 3.7 %collective-permute-start.10 = (bf16[8,128,256]{2,1,0:T(8,128)(2,1)S(1)}, bf16[8,128,256]{2,1,0:T(8,128)(2,1)S(1)}, u32[]{:S(2)}, u32[]{:S(2)}) collective-permute-start(bf16[8,128,256]{2,1,0:T(8,128)(2,1)S(1)} %copy_bitcast_fusion.own), channel_id=1, source_target_pairs={{0,48},{16,0},{32,16},{48,32},{1,49},{17,1},{33,17},{49,33},{2,50}... | collective-permute-start | bytes 1572872 | tf_op jit(solution)/shard_map/ppermute | solution.py:22
  153.9 0.6 pad_add_fusion.choice
  154.5 4.8 %half_rows.3 = bf16[256,4096]{1,0:T(8,128)(2,1)} custom-call(s32[2]{0:T(128)} %pad_add_fusion.choice, bf16[256,8192]{1,0:T(8,128)(2,1)} %states.3, f32[1,8192]{1,0:T(1,128)} %bitcast.27, bf16[256,4096]{1,0:T(8,128)(2,1)} %get-tuple-element.7.rest_0_), custom_call_target="tpu_custom_call", output_to_operand_aliasing={{}: (3, {})} | custom-call | tf_op jit(solution)/shard_map/half_rows/pallas_call | solution.py:79
  159.3 0.0 copy-done.3
  159.3 3.6 %collective-permute-done.9.after = bf16[8,128,256]{2,1,0:T(8,128)(2,1)S(1)} collective-permute-done((bf16[8,128,256]{2,1,0:T(8,128)(2,1)S(1)}, bf16[8,128,256]{2,1,0:T(8,128)(2,1)S(1)}, u32[]{:S(2)}, u32[]{:S(2)}) %collective-permute-start.9) | collective-permute-done | bytes 524320 | tf_op jit(solution)/shard_map/ppermute | solution.py:22
  162.9 2.1 %collective-permute-start.11 = (bf16[4,128,256]{2,1,0:T(8,128)(2,1)S(1)}, bf16[4,128,256]{2,1,0:T(8,128)(2,1)S(1)}, u32[]{:S(2)}, u32[]{:S(2)}) collective-permute-start(bf16[4,128,256]{2,1,0:T(8,128)(2,1)S(1)} %slice.23), channel_id=1, source_target_pairs={{0,16},{16,32},{32,48},{48,0},{1,17},{17,33},{33,49},{49,1},{2,18}... | collective-permute-start | bytes 786440 | tf_op jit(solution)/shard_map/ppermute | solution.py:22
  165.0 0.0 collective-permute-done.10.before
  165.0 0.0 copy-start.7
  165.0 5.0 %collective-permute-start.12 = (bf16[4,128,256]{2,1,0:T(8,128)(2,1)S(1)}, bf16[4,128,256]{2,1,0:T(8,128)(2,1)S(1)}, u32[]{:S(2)}, u32[]{:S(2)}) collective-permute-start(bf16[4,128,256]{2,1,0:T(8,128)(2,1)S(1)} %slice.24), channel_id=1, source_target_pairs={{0,48},{16,0},{32,16},{48,32},{1,49},{17,1},{33,17},{49,33},{2,50}... | collective-permute-start | bytes 786440 | tf_op jit(solution)/shard_map/ppermute | solution.py:22
  170.0 0.0 collective-permute-done.4
  170.0 0.0 all-gather.2.cloned.1.call-done
  170.0 0.0 copy-start
  170.0 0.0 copy-start.5
  170.1 3.4 %fusion.2 = f32[128,512]{1,0:T(8,128)S(1)} fusion(bf16[128,4096]{1,0:T(8,128)(2,1)} %collective-permute-done.4, bf16[4096,512]{1,0:T(8,128)(2,1)} %all-gather.2.cloned.1.call-done), kind=kOutput, calls=%fused_computation.7 | convolution fusion | flops 536870912 | bytes 5505024 | tf_op jit(solution)/shard_map/dot_general | solution.py:370
  173.4 2.1 %collective-permute-start.5 = (f32[128,512]{1,0:T(8,128)S(1)}, f32[128,512]{1,0:T(8,128)S(1)}, u32[]{:S(2)}, u32[]{:S(2)}) collective-permute-start(f32[128,512]{1,0:T(8,128)S(1)} %fusion.2), channel_id=1, source_target_pairs={{0,16},{16,0},{32,48},{48,32},{1,17},{17,1},{33,49},{49,33},{2,18}... | collective-permute-start | bytes 786440 | tf_op jit(solution)/shard_map/ppermute | solution.py:338
  175.5 0.8 fusion.1
  176.3 3.9 %collective-permute-start.3 = (f32[128,512]{1,0:T(8,128)S(1)}, f32[128,512]{1,0:T(8,128)S(1)}, u32[]{:S(2)}, u32[]{:S(2)}) collective-permute-start(f32[128,512]{1,0:T(8,128)S(1)} %fusion.1), channel_id=1, source_target_pairs={{0,16},{16,0},{32,48},{48,32},{1,17},{17,1},{33,49},{49,33},{2,18}... | collective-permute-start | bytes 786440 | tf_op jit(solution)/shard_map/ppermute | solution.py:338
  180.2 0.0 copy-done.5
  180.2 2.0 %fusion.query = f32[256,512]{1,0:T(8,128)} fusion(bf16[256,4096]{1,0:T(8,128)(2,1)S(1)} %copy-done.5, bf16[4096,512]{1,0:T(8,128)(2,1)S(1)} %copy-done), kind=kOutput, calls=%fused_computation.5 | convolution fusion | flops 1073741824 | bytes 6815744 | tf_op jit(solution)/shard_map/dot_general | solution.py:373
  182.3 0.0 collective-permute-done.11.low
  182.3 0.0 collective-permute-done.12.high
  182.3 2.3 %collective-permute-done.5.far = f32[128,512]{1,0:T(8,128)S(1)} collective-permute-done((f32[128,512]{1,0:T(8,128)S(1)}, f32[128,512]{1,0:T(8,128)S(1)}, u32[]{:S(2)}, u32[]{:S(2)}) %collective-permute-start.5) | collective-permute-done | bytes 262176 | tf_op jit(solution)/shard_map/ppermute | solution.py:338
  184.6 3.0 %collective-permute-done.3.near = f32[128,512]{1,0:T(8,128)S(1)} collective-permute-done((f32[128,512]{1,0:T(8,128)S(1)}, f32[128,512]{1,0:T(8,128)S(1)}, u32[]{:S(2)}, u32[]{:S(2)}) %collective-permute-start.3) | collective-permute-done | bytes 262176 | tf_op jit(solution)/shard_map/ppermute | solution.py:338
  187.7 0.0 copy-done.12
  187.7 0.7 copy-done.13
  188.4 7.4 %attention.1 = bf16[256,512]{1,0:T(8,128)(2,1)} custom-call(s32[1]{0:T(128)} %bitcast.odd.core, s32[4,4]{1,0:T(4,128)} %owners.1, s32[4]{0:T(128)} %counts.1, f32[1]{0:T(128)S(6)} %tanh.3.gate, f32[256,512]{1,0:T(8,128)} %fusion.query, f32[128,512]{1,0:T(8,128)} %copy-done.13, f32[128,512]{1,0:T(8,128)} %copy-done.12, f32[1,128]{1,0:T(1,128)} %bitcast.30, ...), custom_call_target="tpu_custom_call" | custom-call | tf_op jit(solution)/shard_map/attention/pallas_call | solution.py:275
  (22 shorter events, 0.1 us)
Async XLA Ops:
  6.5 163.5 %all-gather.2.cloned.1.call-start = ((), (), s32[]{:S(2)}) async-start(), calls=%async_computation.3 | async-start | bytes 4718592 | tf_op jit(solution)/shard_map/all_gather | solution.py:327
  8.2 16.9 %collective-permute-start = (bf16[128,768]{1,0:T(8,128)(2,1)}, bf16[128,768]{1,0:T(8,128)(2,1)S(1)}, u32[]{:S(2)}, u32[]{:S(2)}) collective-permute-start(bf16[128,768]{1,0:T(8,128)(2,1)} %join.1), channel_id=1, source_target_pairs={{0,1},{1,0},{2,3},{3,2},{4,5},{5,4},{6,7},{7,6},{8,9},{9,8},{10,11... | collective-permute-start | bytes 589832 | tf_op jit(solution)/shard_map/ppermute | solution.py:22
  26.2 58.0 %copy-start.1 = (bf16[256,768]{1,0:T(8,128)(2,1)}, bf16[256,768]{1,0:T(8,128)(2,1)S(1)}, u32[]{:S(2)}) copy-start(bf16[256,768]{1,0:T(8,128)(2,1)S(1)} %maximum_select_fusion.1.rest_0_) | copy-start | bytes 1179652
  26.2 14.3 %collective-permute-start.1 = (bf16[256,768]{1,0:T(8,128)(2,1)S(1)}, bf16[256,768]{1,0:T(8,128)(2,1)S(1)}, u32[]{:S(2)}, u32[]{:S(2)}) collective-permute-start(bf16[256,768]{1,0:T(8,128)(2,1)S(1)} %maximum_select_fusion.1.rest_0_), channel_id=1, source_target_pairs={{0,32},{16,48},{32,0},{48,16},{1,33},{17,49},{33,1},{49,17},{2,34}... | collective-permute-start | bytes 1179656 | tf_op jit(solution)/shard_map/ppermute | solution.py:22
  40.6 43.7 %copy-start.8 = (bf16[256,768]{1,0:T(8,128)(2,1)}, bf16[256,768]{1,0:T(8,128)(2,1)S(1)}, u32[]{:S(2)}) copy-start(bf16[256,768]{1,0:T(8,128)(2,1)S(1)} %collective-permute-done.1.rest_2_) | copy-start | bytes 1179652
  71.4 12.9 %copy-start.4 = (bf16[32,8,1024]{2,1,0:T(8,128)(2,1)}, bf16[32,8,1024]{2,1,0:T(8,128)(2,1)S(1)}, u32[]{:S(2)}) copy-start(bf16[32,8,1024]{2,1,0:T(8,128)(2,1)S(1)} %all_to_all.15) | copy-start | bytes 1572868
  71.4 12.9 %collective-permute-start.6 = (bf16[32,8,1024]{2,1,0:T(8,128)(2,1)S(1)}, bf16[32,8,1024]{2,1,0:T(8,128)(2,1)S(1)}, u32[]{:S(2)}, u32[]{:S(2)}) collective-permute-start(bf16[32,8,1024]{2,1,0:T(8,128)(2,1)S(1)} %all_to_all.15), channel_id=1, source_target_pairs={{0,64},{64,0},{1,65},{65,1},{2,66},{66,2},{3,67},{67,3},{4,68},{68... | collective-permute-start | bytes 1572872 | tf_op jit(solution)/shard_map/ppermute | solution.py:22
  73.3 9.0 %collective-permute-start.7 = (bf16[256,256]{1,0:T(8,128)(2,1)S(1)}, bf16[256,256]{1,0:T(8,128)(2,1)S(1)}, u32[]{:S(2)}, u32[]{:S(2)}) collective-permute-start(bf16[256,256]{1,0:T(8,128)(2,1)S(1)} %slice.22), channel_id=1, source_target_pairs={{0,16},{16,32},{32,48},{48,0},{1,17},{17,33},{33,49},{49,1},{2,18}... | collective-permute-start | bytes 393224 | tf_op jit(solution)/shard_map/ppermute | solution.py:22
  76.7 7.5 %collective-permute-start.8 = (bf16[256,256]{1,0:T(8,128)(2,1)S(1)}, bf16[256,256]{1,0:T(8,128)(2,1)S(1)}, u32[]{:S(2)}, u32[]{:S(2)}) collective-permute-start(bf16[256,256]{1,0:T(8,128)(2,1)S(1)} %slice.22), channel_id=1, source_target_pairs={{0,48},{16,0},{32,16},{48,32},{1,49},{17,1},{33,17},{49,33},{2,50}... | collective-permute-start | bytes 393224 | tf_op jit(solution)/shard_map/ppermute | solution.py:22
  82.3 2.0 copy-start.14
  84.2 0.7 copy-start.15
  84.2 0.9 copy-start.9
  87.7 27.2 %all-to-all-start.1 = ((f32[8,2,4,8,256]{4,3,2,1,0:T(8,128)}), f32[8,2,4,8,256]{4,3,2,1,0:T(8,128)S(1)}, u32[]{:S(2)}, u32[]{:S(2)}) async-start(f32[8,2,4,8,256]{4,3,2,1,0:T(8,128)} %partial_sums.1), calls=%async_computation.1 | async-start | bytes 1048576 | tf_op jit(solution)/shard_map/all_to_all | solution.py:26
  97.9 26.4 %collective-permute-start.2 = (bf16[128,4096]{1,0:T(8,128)(2,1)}, bf16[128,4096]{1,0:T(8,128)(2,1)S(1)}, u32[]{:S(2)}, u32[]{:S(2)}) collective-permute-start(bf16[128,4096]{1,0:T(8,128)(2,1)} %get-tuple-element.8), channel_id=1, source_target_pairs={{0,16},{16,0},{32,48},{48,32},{1,17},{17,1},{33,49},{49,33},{2,18}... | collective-permute-start | bytes 3145736 | tf_op jit(solution)/shard_map/ppermute | solution.py:338
  114.9 0.8 copy-start.2
  117.8 28.3 %all-to-all-start.2 = ((bf16[16,8,8,256]{3,2,1,0:T(8,128)(2,1)}), bf16[16,8,8,256]{3,2,1,0:T(8,128)(2,1)S(1)}, u32[]{:S(2)}, u32[]{:S(2)}) async-start(bf16[16,8,8,256]{3,2,1,0:T(8,128)(2,1)} %key_value_pairs.1), calls=%async_computation.2 | async-start | bytes 1048576 | tf_op jit(solution)/shard_map/all_to_all | solution.py:26
  124.3 45.7 %collective-permute-start.4 = (bf16[128,4096]{1,0:T(8,128)(2,1)S(1)}, bf16[128,4096]{1,0:T(8,128)(2,1)}, u32[]{:S(2)}, u32[]{:S(2)}) collective-permute-start(bf16[128,4096]{1,0:T(8,128)(2,1)S(1)} %collective-permute-done.2), channel_id=1, source_target_pairs={{0,64},{64,0},{1,65},{65,1},{2,66},{66,2},{3,67},{67,3},{4,68},{68... | collective-permute-start | bytes 3145736 | tf_op jit(solution)/shard_map/ppermute | solution.py:22
  146.1 13.2 %copy-start.3 = (bf16[8,128,256]{2,1,0:T(8,128)(2,1)}, bf16[8,128,256]{2,1,0:T(8,128)(2,1)S(1)}, u32[]{:S(2)}) copy-start(bf16[8,128,256]{2,1,0:T(8,128)(2,1)S(1)} %copy_bitcast_fusion.own) | copy-start | bytes 1572868
  146.1 16.7 %collective-permute-start.9 = (bf16[8,128,256]{2,1,0:T(8,128)(2,1)S(1)}, bf16[8,128,256]{2,1,0:T(8,128)(2,1)S(1)}, u32[]{:S(2)}, u32[]{:S(2)}) collective-permute-start(bf16[8,128,256]{2,1,0:T(8,128)(2,1)S(1)} %copy_bitcast_fusion.own), channel_id=1, source_target_pairs={{0,16},{16,32},{32,48},{48,0},{1,17},{17,33},{33,49},{49,1},{2,18}... | collective-permute-start | bytes 1572872 | tf_op jit(solution)/shard_map/ppermute | solution.py:22
  149.5 15.5 %collective-permute-start.10 = (bf16[8,128,256]{2,1,0:T(8,128)(2,1)S(1)}, bf16[8,128,256]{2,1,0:T(8,128)(2,1)S(1)}, u32[]{:S(2)}, u32[]{:S(2)}) collective-permute-start(bf16[8,128,256]{2,1,0:T(8,128)(2,1)S(1)} %copy_bitcast_fusion.own), channel_id=1, source_target_pairs={{0,48},{16,0},{32,16},{48,32},{1,49},{17,1},{33,17},{49,33},{2,50}... | collective-permute-start | bytes 1572872 | tf_op jit(solution)/shard_map/ppermute | solution.py:22
  162.9 13.4 %copy-start.6 = (bf16[8,128,256]{2,1,0:T(8,128)(2,1)}, bf16[8,128,256]{2,1,0:T(8,128)(2,1)S(1)}, u32[]{:S(2)}) copy-start(bf16[8,128,256]{2,1,0:T(8,128)(2,1)S(1)} %collective-permute-done.9.after) | copy-start | bytes 1572868
  162.9 19.4 %collective-permute-start.11 = (bf16[4,128,256]{2,1,0:T(8,128)(2,1)S(1)}, bf16[4,128,256]{2,1,0:T(8,128)(2,1)S(1)}, u32[]{:S(2)}, u32[]{:S(2)}) collective-permute-start(bf16[4,128,256]{2,1,0:T(8,128)(2,1)S(1)} %slice.23), channel_id=1, source_target_pairs={{0,16},{16,32},{32,48},{48,0},{1,17},{17,33},{33,49},{49,1},{2,18}... | collective-permute-start | bytes 786440 | tf_op jit(solution)/shard_map/ppermute | solution.py:22
  165.0 11.3 %copy-start.7 = (bf16[8,128,256]{2,1,0:T(8,128)(2,1)}, bf16[8,128,256]{2,1,0:T(8,128)(2,1)S(1)}, u32[]{:S(2)}) copy-start(bf16[8,128,256]{2,1,0:T(8,128)(2,1)S(1)} %collective-permute-done.10.before) | copy-start | bytes 1572868
  165.0 17.3 %collective-permute-start.12 = (bf16[4,128,256]{2,1,0:T(8,128)(2,1)S(1)}, bf16[4,128,256]{2,1,0:T(8,128)(2,1)S(1)}, u32[]{:S(2)}, u32[]{:S(2)}) collective-permute-start(bf16[4,128,256]{2,1,0:T(8,128)(2,1)S(1)} %slice.24), channel_id=1, source_target_pairs={{0,48},{16,0},{32,16},{48,32},{1,49},{17,1},{33,17},{49,33},{2,50}... | collective-permute-start | bytes 786440 | tf_op jit(solution)/shard_map/ppermute | solution.py:22
  170.0 5.5 %copy-start = (bf16[4096,512]{1,0:T(8,128)(2,1)S(1)}, bf16[4096,512]{1,0:T(8,128)(2,1)}, u32[]{:S(2)}) copy-start(bf16[4096,512]{1,0:T(8,128)(2,1)} %all-gather.2.cloned.1.call-done) | copy-start | bytes 12582916
  170.0 10.2 %copy-start.5 = (bf16[256,4096]{1,0:T(8,128)(2,1)S(1)}, bf16[256,4096]{1,0:T(8,128)(2,1)}, u32[]{:S(2)}) copy-start(bf16[256,4096]{1,0:T(8,128)(2,1)} %half_rows.3) | copy-start | bytes 6291460
  173.4 11.2 %collective-permute-start.5 = (f32[128,512]{1,0:T(8,128)S(1)}, f32[128,512]{1,0:T(8,128)S(1)}, u32[]{:S(2)}, u32[]{:S(2)}) collective-permute-start(f32[128,512]{1,0:T(8,128)S(1)} %fusion.2), channel_id=1, source_target_pairs={{0,16},{16,0},{32,48},{48,32},{1,17},{17,1},{33,49},{49,33},{2,18}... | collective-permute-start | bytes 786440 | tf_op jit(solution)/shard_map/ppermute | solution.py:338
  176.3 11.4 %collective-permute-start.3 = (f32[128,512]{1,0:T(8,128)S(1)}, f32[128,512]{1,0:T(8,128)S(1)}, u32[]{:S(2)}, u32[]{:S(2)}) collective-permute-start(f32[128,512]{1,0:T(8,128)S(1)} %fusion.1), channel_id=1, source_target_pairs={{0,16},{16,0},{32,48},{48,32},{1,17},{17,1},{33,49},{49,33},{2,18}... | collective-permute-start | bytes 786440 | tf_op jit(solution)/shard_map/ppermute | solution.py:338
  182.3 5.4 %copy-start.10 = (bf16[4,128,256]{2,1,0:T(8,128)(2,1)}, bf16[4,128,256]{2,1,0:T(8,128)(2,1)S(1)}, u32[]{:S(2)}) copy-start(bf16[4,128,256]{2,1,0:T(8,128)(2,1)S(1)} %collective-permute-done.11.low) | copy-start | bytes 786436
  182.3 5.4 %copy-start.11 = (bf16[4,128,256]{2,1,0:T(8,128)(2,1)}, bf16[4,128,256]{2,1,0:T(8,128)(2,1)S(1)}, u32[]{:S(2)}) copy-start(bf16[4,128,256]{2,1,0:T(8,128)(2,1)S(1)} %collective-permute-done.12.high) | copy-start | bytes 786436
  184.6 3.0 %copy-start.12 = (f32[128,512]{1,0:T(8,128)}, f32[128,512]{1,0:T(8,128)S(1)}, u32[]{:S(2)}) copy-start(f32[128,512]{1,0:T(8,128)S(1)} %collective-permute-done.5.far) | copy-start | bytes 786436
  187.7 0.7 copy-start.13
Sparse Core Ops, SparseCore 0:
  41.8 77.0 all-gather.1

commit v3 on v2

--- a/solution.py
+++ b/solution.py
@@ -38,46 +38,42 @@
 scalar = pl.BlockSpec(memory_space=pltpu.SMEM)
 
 
-def half_kernel(x, z, choice, states, gain, *rest):
+def text_kernel(x, choice, states, gain, *rest):
     outs = rest[1:]
     rows, width = states.shape
     depth = 128
-    span = width // (x * z)
     squares = jnp.zeros((rows, depth), jnp.float32)
     for j in range(width // depth):
         wide = states[:, j * depth : (j + 1) * depth].astype(jnp.float32)
         squares += wide * wide
     scale = lax.rsqrt(jnp.sum(squares, axis=-1, keepdims=True) / width + norm_epsilon)
-    even = choice[1] == 0
-    for k in range(z):
-        for m in range(x // 2):
-            blocks = []
-            for p in range(2):
-                start = ((2 * m + p) * z + k) * span
-                at = slice(start, start + span)
-                wide = states[:, at].astype(jnp.float32)
-                blocks.append((wide * scale * gain[:, at]).astype(jnp.bfloat16))
-            start = (k * (x // 2) + m) * span
-            lanes = slice(start, start + span)
-            outs[0][:, lanes] = jnp.where(even, blocks[0], blocks[1])
-            if len(outs) > 1:
-                outs[1][:, lanes] = jnp.where(even, blocks[1], blocks[0])
-
-
-def half_rows(states, gain, choice, base, x, z):
+    span = width // x
+    step = 2 * depth
+    for k in range(x if len(outs) > 1 else 1):
+        first = lax.rem(choice[1] + k, x) * span
+        for j in range(span // step):
+            at = pl.ds(pl.multiple_of(first + j * step, step), step)
+            block = (states[:, at].astype(jnp.float32) * scale * gain[:, at]).astype(jnp.bfloat16)
+            lanes = slice(j * step, (j + 1) * step)
+            if k == 0:
+                outs[0][:, lanes] = block
+            else:
+                outs[k][:, lanes] = block
+
+
+def text_rows(states, gain, choice, base, x):
     total, width = states.shape
     rows = 32
     steps = total // 2 // rows
-    held = () if base is None else (base,)
-    place = pl.BlockSpec((rows, width // 2), lambda i, c: (c[0] * steps + i, 0))
-    shapes = [jax.ShapeDtypeStruct((total, width // 2), jnp.bfloat16)]
+    span = width // x
+    place = pl.BlockSpec((rows, span), lambda i, c: (c[0] * steps + i, 0))
+    shapes = [jax.ShapeDtypeStruct((total, span), jnp.bfloat16)]
     places = [place]
     if base is None:
-        held = (gain,)
-        shapes.append(jax.ShapeDtypeStruct((total // 2, width // 2), jnp.bfloat16))
-        places.append(pl.BlockSpec((rows, width // 2), lambda i, c: (i, 0)))
-    return pl.pallas_call(
-        functools.partial(half_kernel, x, z),
+        shapes += [jax.ShapeDtypeStruct((total // 2, span), jnp.bfloat16)] * (x - 1)
+        places += [pl.BlockSpec((rows, span), lambda i, c: (i, 0))] * (x - 1)
+    return pl.pallas_call(
+        functools.partial(text_kernel, x),
         grid_spec=pltpu.PrefetchScalarGridSpec(
             num_scalar_prefetch=1,
             grid=(steps,),
@@ -90,8 +86,38 @@
         ),
         out_shape=shapes,
         input_output_aliases={} if base is None else {3: 0},
-        name="half_rows",
-    )(choice, states, gain, *held)
+        name="text_rows",
+    )(choice, states, gain, gain if base is None else base)
+
+
+def query_kernel(near, far, own, weight, query, *backs):
+    rows = near.shape[0] // len(backs)
+    columns = weight[...]
+    for c, guests in enumerate((near, far)):
+        product = jnp.dot(guests[...], columns, preferred_element_type=jnp.float32)
+        for k, back in enumerate(backs):
+            back[c * rows : (c + 1) * rows] = product[k * rows : (k + 1) * rows]
+    query[...] = jnp.dot(own[...], columns, preferred_element_type=jnp.float32)
+
+
+def query_products(near, far, own, weight, guests):
+    rows = own.shape[0]
+    depth, width = weight.shape
+    block = width // 2
+    column = pl.BlockSpec((rows, block), lambda n: (0, n))
+    return pl.pallas_call(
+        query_kernel,
+        grid=(2,),
+        in_specs=[
+            whole(near.shape),
+            whole(far.shape),
+            whole(own.shape),
+            pl.BlockSpec((depth, block), lambda n: (0, n)),
+        ],
+        out_specs=[column] * (1 + guests),
+        out_shape=[jax.ShapeDtypeStruct((rows, width), jnp.float32)] * (1 + guests),
+        name="query_products",
+    )(near, far, own, weight)
 
 
 def join_kernel(*refs):
@@ -210,7 +236,7 @@
 
 
 def attention_kernel(
-    core, owners, counts, gate, query, near, far, q_gain, own, after, before, low, high, out
+    core, owners, counts, gate, query, share_1, share_2, share_3, q_gain, own, after, before, low, high, out
 ):
     block = pl.program_id(0)
     rows, width = query.shape
@@ -221,11 +247,11 @@
     slots = owners.shape[1]
     scale = head ** (-0.5)
     gain = q_gain[...]
-    span = near.shape[0]
+    span = share_1.shape[0] // 2
     first = block * rows
-    inside = lax.rem(first, span)
-    at = pl.ds(pl.multiple_of(inside, rows), rows)
-    total = query[...] + jnp.where(first // span == core[0], near[at, :], far[at, :])
+    start = jnp.where(first // span == core[0], 0, span) + lax.rem(first, span)
+    at = pl.ds(pl.multiple_of(start, rows), rows)
+    total = query[...] + share_1[at, :] + share_2[at, :] + share_3[at, :]
     parts = []
     for h in range(heads):
         parts.append(head_norm(total[:, h * head : (h + 1) * head], gain).astype(jnp.bfloat16))
@@ -268,7 +294,7 @@
         out[:, h * head : (h + 1) * head] = attended[h * rows : (h + 1) * rows]
 
 
-def attention(core, owners, counts, gate_value, query, near, far, q_gain, pieces):
+def attention(core, owners, counts, gate_value, query, shares, q_gain, pieces):
     blocks = owners.shape[0]
     tokens, width = query.shape
     rows = tokens // blocks
@@ -278,15 +304,14 @@
         in_specs=[
             *(scalar,) * 4,
             pl.BlockSpec((rows, width), lambda b: (b, 0)),
-            whole(near.shape),
-            whole(far.shape),
+            *(whole(share.shape) for share in shares),
             whole(q_gain.shape),
             *(whole(p.shape) for p in pieces),
         ],
         out_specs=pl.BlockSpec((rows, width), lambda b: (b, 0)),
         out_shape=jax.ShapeDtypeStruct((tokens, width), jnp.bfloat16),
         name="attention",
-    )(core, owners, counts, gate_value, query, near, far, q_gain, *pieces)
+    )(core, owners, counts, gate_value, query, *shares, q_gain, *pieces)
 
 
 def on_device(
@@ -319,30 +344,24 @@
     joined = join(k_weight, v_weight, q_weight)
     other = shift(joined, "yh", 1)
     both = ordered(lax.axis_index("yh") == 0, joined, other)
-    far = shift(both, "x", 2)
     near = both[:, : 2 * head]
-    pair_weight = (both, shift(near, "x", 1), far, shift(near, "x", 3))
-
-    rows_q = ordered(place < 2, both[:, 2 * head :], far[:, 2 * head :])
-    q_half = lax.all_gather(rows_q, "z", axis=0, tiled=True)
+    pair_weight = (near, *(shift(near, "x", k) for k in range(1, x)))
+
+    q_part = lax.all_gather(both[:, 2 * head :], "z", axis=0, tiled=True)
 
     columns = columns_of(vision.reshape(tokens, width), yl, x, z)
     here = exchange(columns.reshape(yl * z, tokens, width // z), ("yl", "z"))
 
     gate = jnp.tanh(gate_value)
 
-    mine = lax.rem(place, 2)
     gain = text_gain[None]
-
-    def partner(array):
-        return lax.ppermute(array, "x", [(i, i ^ 1) for i in range(x)])
-
-    choice = jnp.stack((core, mine)).astype(jnp.int32)
-    text_half, sent = half_rows(text_states, gain, choice, None, x, z)
-    guest = partner(sent)
+    choice = jnp.stack((core, place)).astype(jnp.int32)
+    text_own, *sent = text_rows(text_states, gain, choice, None, x)
+    came = [shift(part, "x", k + 1) for k, part in enumerate(sent)]
+    guest = jnp.concatenate(came, axis=0)
     guest_other = shift(guest, "co", 1)
-    choice = jnp.stack((1 - core, mine)).astype(jnp.int32)
-    (text_half,) = half_rows(text_states, gain, choice, text_half, x, z)
+    choice = jnp.stack((1 - core, place)).astype(jnp.int32)
+    (text_own,) = text_rows(text_states, gain, choice, text_own, x)
 
     there = shift(here, "co", 1)
     partial = partial_sums(
@@ -366,19 +385,15 @@
     low = shift(after[:half], "x", 1)
     high = shift(before[half:], "x", -1)
 
-    guest_near = jnp.dot(guest, q_half, preferred_element_type=jnp.float32)
-    guest_far = jnp.dot(guest_other, q_half, preferred_element_type=jnp.float32)
-    back_near = partner(guest_near)
-    back_far = partner(guest_far)
-    query = jnp.dot(text_half, q_half, preferred_element_type=jnp.float32)
+    query, *backs = query_products(guest, guest_other, text_own, q_part, x - 1)
+    shares = [shift(part, "x", -(k + 1)) for k, part in enumerate(backs)]
     return attention(
         core.astype(jnp.int32)[None],
         owners,
         counts,
         gate,
         query,
-        back_near,
-        back_far,
+        shares,
         q_gain[None],
         (own, after, before, low, high),
     )

time: 204 us -> 217 us (1.064)
  the two profiles are of different devices: /device:TPU:80 before, /device:TPU:73 now
where the time goes in v3:
time: 217 us; the launch traced here: 216 us
  waiting for transfers between devices  67.3 us (31%)
  starting transfers between devices  65.7 us (30%)
  Pallas kernels  31.2 us (14%)
  blocking collectives  29.7 us (14%)
  between operations  14.5 us (7%)
  local copies, waits for them, and re-layouts  5.86 us (3%)
    ppermute x16, waiting for transfers between devices, shift(): lax.ppermute(array, axis, [(i, (i + step) % size) for i in range(size)])  51.9 us
    ppermute x16, starting transfers between devices, shift(): lax.ppermute(array, axis, [(i, (i + step) % size) for i in range(size)])  51.6 us
    all_to_all x1, blocking collectives, exchange(): return lax.all_to_all(array, axes, 0, 0, tiled=True)  29.7 us
    all_to_all x2, waiting for transfers between devices, exchange(): return lax.all_to_all(array, axes, 0, 0, tiled=True)  15.3 us
    all_to_all x2, starting transfers between devices, exchange(): return lax.all_to_all(array, axes, 0, 0, tiled=True)  14.1 us
    pallas_call x2, Pallas kernels, text_rows(): pl.pallas_call(functools.partial(text_kernel, x), grid_spec=pltpu.Prefetc...  9.46 us
    pallas_call x1, Pallas kernels, attention(): pl.pallas_call(attention_kernel, grid=(blocks,), in_specs=[*(scalar,) * 4...  7.77 us
    pallas_call x1, Pallas kernels, query_products(): pl.pallas_call(query_kernel, grid=(2,), in_specs=[whole(near.shape), whol...  6.07 us
  transfers between devices with their start and end apart: 19, of which 6 were waited for; matrix products, arithmetic and copies ran while one was open for 2% of the time, Pallas kernels for 10%

profile of v3, /device:TPU:73, one launch (start us, length us, event | category | flops | bytes accessed | tf_op | source)
XLA Modules:
  0.0 215.6 jit_solution(13158187472761395671)
XLA Ops:
  6.5 1.6 join.1
  8.2 6.7 %collective-permute-start.4 = (bf16[128,768]{1,0:T(8,128)(2,1)}, bf16[128,768]{1,0:T(8,128)(2,1)S(1)}, u32[]{:S(2)}, u32[]{:S(2)}) collective-permute-start(bf16[128,768]{1,0:T(8,128)(2,1)} %join.1), channel_id=1, source_target_pairs={{0,1},{1,0},{2,3},{3,2},{4,5},{5,4},{6,7},{7,6},{8,9},{9,8},{10,11... | collective-permute-start | bytes 589832 | tf_op jit(solution)/shard_map/ppermute | solution.py:22
  14.9 1.7 columns.1
  16.6 10.7 %all-to-all-start = ((bf16[32,8,1024]{2,1,0:T(8,128)(2,1)}), bf16[32,8,1024]{2,1,0:T(8,128)(2,1)S(1)}, u32[]{:S(2)}, u32[]{:S(2)}) async-start(bf16[32,8,1024]{2,1,0:T(8,128)(2,1)} %bitcast.16), calls=%async_computation | async-start | bytes 1048576 | tf_op jit(solution)/shard_map/all_to_all | solution.py:26
  27.3 0.0 all-gather.2.cloned.1.call-start
  27.4 0.0 collective-permute-done.4
  27.4 0.1 maximum_select_fusion
  27.5 0.7 slice.16
  28.2 0.0 all-gather.2.cloned.1.call-update
  28.2 15.3 %all-to-all-done = bf16[32,8,1024]{2,1,0:T(8,128)(2,1)S(1)} async-done(((bf16[32,8,1024]{2,1,0:T(8,128)(2,1)}), bf16[32,8,1024]{2,1,0:T(8,128)(2,1)S(1)}, u32[]{:S(2)}, u32[]{:S(2)}) %all-to-all-start) | async-done | bytes 524320 | tf_op jit(solution)/shard_map/all_to_all | solution.py:26
  43.5 3.8 %collective-permute-start.8 = (bf16[32,8,1024]{2,1,0:T(8,128)(2,1)S(1)}, bf16[32,8,1024]{2,1,0:T(8,128)(2,1)S(1)}, u32[]{:S(2)}, u32[]{:S(2)}) collective-permute-start(bf16[32,8,1024]{2,1,0:T(8,128)(2,1)S(1)} %all-to-all-done), channel_id=1, source_target_pairs={{0,64},{64,0},{1,65},{65,1},{2,66},{66,2},{3,67},{67,3},{4,68},{68... | collective-permute-start | bytes 1572872 | tf_op jit(solution)/shard_map/ppermute | solution.py:22
  47.3 0.6 pad_add_fusion.choice
  48.0 4.9 %text_rows.2 = (bf16[256,2048]{1,0:T(8,128)(2,1)}, bf16[128,2048]{1,0:T(8,128)(2,1)}, bf16[128,2048]{1,0:T(8,128)(2,1)}, bf16[128,2048]{1,0:T(8,128)(2,1)}) custom-call(s32[2]{0:T(128)} %pad_add_fusion.choice, bf16[256,8192]{1,0:T(8,128)(2,1)} %states.3, f32[1,8192]{1,0:T(1,128)} %bitcast.18, f32[1,8192]{1,0:T(1,128)} %bitcast.19), custom_call_target="tpu_custom_call" | custom-call | tf_op jit(solution)/shard_map/text_rows/pallas_call | solution.py:75
  52.9 0.0 copy-done.1
  52.9 3.1 %collective-permute-start = (bf16[128,2048]{1,0:T(8,128)(2,1)}, bf16[128,2048]{1,0:T(8,128)(2,1)}, u32[]{:S(2)}, u32[]{:S(2)}) collective-permute-start(bf16[128,2048]{1,0:T(8,128)(2,1)} %get-tuple-element.13), channel_id=1, source_target_pairs={{0,16},{16,32},{32,48},{48,0},{1,17},{17,33},{33,49},{49,1},{2,18}... | collective-permute-start | bytes 1572872 | tf_op jit(solution)/shard_map/ppermute | solution.py:22
  56.0 4.4 %collective-permute-start.10 = (bf16[256,256]{1,0:T(8,128)(2,1)S(1)}, bf16[256,256]{1,0:T(8,128)(2,1)S(1)}, u32[]{:S(2)}, u32[]{:S(2)}) collective-permute-start(bf16[256,256]{1,0:T(8,128)(2,1)S(1)} %slice.17.rest_0_), channel_id=1, source_target_pairs={{0,32},{16,48},{32,0},{48,16},{1,33},{17,49},{33,1},{49,17},{2,34}... | collective-permute-start | bytes 393224 | tf_op jit(solution)/shard_map/ppermute | solution.py:22
  60.4 2.4 %collective-permute-start.1 = (bf16[128,2048]{1,0:T(8,128)(2,1)}, bf16[128,2048]{1,0:T(8,128)(2,1)}, u32[]{:S(2)}, u32[]{:S(2)}) collective-permute-start(bf16[128,2048]{1,0:T(8,128)(2,1)} %get-tuple-element.14), channel_id=1, source_target_pairs={{0,32},{16,48},{32,0},{48,16},{1,33},{17,49},{33,1},{49,17},{2,34}... | collective-permute-start | bytes 1572872 | tf_op jit(solution)/shard_map/ppermute | solution.py:22
  62.8 3.4 %collective-permute-start.11 = (bf16[256,256]{1,0:T(8,128)(2,1)S(1)}, bf16[256,256]{1,0:T(8,128)(2,1)S(1)}, u32[]{:S(2)}, u32[]{:S(2)}) collective-permute-start(bf16[256,256]{1,0:T(8,128)(2,1)S(1)} %slice.17.rest_0_), channel_id=1, source_target_pairs={{0,48},{16,0},{32,16},{48,32},{1,49},{17,1},{33,17},{49,33},{2,50}... | collective-permute-start | bytes 393224 | tf_op jit(solution)/shard_map/ppermute | solution.py:22
  66.2 7.2 %collective-permute-done.10.rest_2_ = bf16[256,256]{1,0:T(8,128)(2,1)S(1)} collective-permute-done((bf16[256,256]{1,0:T(8,128)(2,1)S(1)}, bf16[256,256]{1,0:T(8,128)(2,1)S(1)}, u32[]{:S(2)}, u32[]{:S(2)}) %collective-permute-start.10) | collective-permute-done | bytes 131104 | tf_op jit(solution)/shard_map/ppermute | solution.py:22
  73.4 1.9 collective-permute-start.9
  75.4 3.3 %collective-permute-done.11.rest_3_ = bf16[256,256]{1,0:T(8,128)(2,1)S(1)} collective-permute-done((bf16[256,256]{1,0:T(8,128)(2,1)S(1)}, bf16[256,256]{1,0:T(8,128)(2,1)S(1)}, u32[]{:S(2)}, u32[]{:S(2)}) %collective-permute-start.11) | collective-permute-done | bytes 131104 | tf_op jit(solution)/shard_map/ppermute | solution.py:22
  78.6 9.2 %collective-permute-done.9.rest_1_ = bf16[256,256]{1,0:T(8,128)(2,1)S(1)} collective-permute-done((bf16[256,256]{1,0:T(8,128)(2,1)S(1)}, bf16[256,256]{1,0:T(8,128)(2,1)S(1)}, u32[]{:S(2)}, u32[]{:S(2)}) %collective-permute-start.9) | collective-permute-done | bytes 131104 | tf_op jit(solution)/shard_map/ppermute | solution.py:22
  87.9 0.0 collective-permute-done.8
  87.9 0.6 copy-done.16
  88.5 0.2 copy-done.7
  88.7 2.6 %partial_sums.1 = f32[8,2,4,8,256]{4,3,2,1,0:T(8,128)} custom-call(s32[1]{0:T(128)} %bitcast.1.spot, bf16[256,1024]{1,0:T(8,128)(2,1)} %bitcast.15, bf16[256,1024]{1,0:T(8,128)(2,1)} %bitcast.17, bf16[256,256]{1,0:T(8,128)(2,1)} %copy-done.11, bf16[256,256]{1,0:T(8,128)(2,1)} %copy-done.16, bf16[256,256]{1,0:T(8,128)(2,1)} %copy-done.14, ...), custom_call_target="tpu_custom_call" | custom-call | tf_op jit(solution)/shard_map/partial_sums/pallas_call | solution.py:187
  91.3 3.4 %all-to-all-start.1 = ((f32[8,2,4,8,256]{4,3,2,1,0:T(8,128)}), f32[8,2,4,8,256]{4,3,2,1,0:T(8,128)S(1)}, u32[]{:S(2)}, u32[]{:S(2)}) async-start(f32[8,2,4,8,256]{4,3,2,1,0:T(8,128)} %partial_sums.1), calls=%async_computation.1 | async-start | bytes 1048576 | tf_op jit(solution)/shard_map/all_to_all | solution.py:26
  94.7 1.9 collective-permute-start.2
  96.7 0.0 collective-permute-done
  96.7 1.1 constant_dynamic-update-slice_fusion.2
  97.8 0.0 collective-permute-done.1
  97.8 1.1 constant_dynamic-update-slice_fusion.1
  98.9 10.4 %collective-permute-done.2 = bf16[128,2048]{1,0:T(8,128)(2,1)S(1)} collective-permute-done((bf16[128,2048]{1,0:T(8,128)(2,1)}, bf16[128,2048]{1,0:T(8,128)(2,1)S(1)}, u32[]{:S(2)}, u32[]{:S(2)}) %collective-permute-start.2) | collective-permute-done | bytes 524320 | tf_op jit(solution)/shard_map/ppermute | solution.py:22
  109.4 3.8 %collective-permute-start.3 = (bf16[384,2048]{1,0:T(8,128)(2,1)S(1)}, bf16[384,2048]{1,0:T(8,128)(2,1)}, u32[]{:S(2)}, u32[]{:S(2)}) collective-permute-start(bf16[384,2048]{1,0:T(8,128)(2,1)S(1)} %constant_dynamic-update-slice_fusion.near), channel_id=1, source_target_pairs={{0,64},{64,0},{1,65},{65,1},{2,66},{66,2},{3,67},{67,3},{4,68},{68... | collective-permute-start | bytes 4718600 | tf_op jit(solution)/shard_map/ppermute | solution.py:22
  113.2 0.0 all-to-all-done.1.parts
  113.2 0.0 copy-start.3
  113.2 0.8 copy-done.3
  114.0 2.0 key_value_pairs.1
  115.9 29.7 %all_to_all.15 = bf16[16,8,8,256]{3,2,1,0:T(8,128)(2,1)S(1)} all-to-all(bf16[16,8,8,256]{3,2,1,0:T(8,128)(2,1)} %key_value_pairs.1), channel_id=1, replica_groups=mesh['yl'=4,'co'=2,'x'=4,'z'=8,'yh'=2] {'z','yh'}, dimensions={0} | all-to-all | bytes 1048576 | tf_op jit(solution)/shard_map/all_to_all | solution.py:26
  145.7 1.9 collective-permute-start.12
  147.6 4.6 %collective-permute-start.13 = (bf16[8,128,256]{2,1,0:T(8,128)(2,1)S(1)}, bf16[8,128,256]{2,1,0:T(8,128)(2,1)S(1)}, u32[]{:S(2)}, u32[]{:S(2)}) collective-permute-start(bf16[8,128,256]{2,1,0:T(8,128)(2,1)S(1)} %copy_bitcast_fusion.own), channel_id=1, source_target_pairs={{0,48},{16,0},{32,16},{48,32},{1,49},{17,1},{33,17},{49,33},{2,50}... | collective-permute-start | bytes 1572872 | tf_op jit(solution)/shard_map/ppermute | solution.py:22
  152.2 0.6 pad_add_fusion.1.choice
  152.8 4.6 %text_rows.3.own = bf16[256,2048]{1,0:T(8,128)(2,1)} custom-call(s32[2]{0:T(128)} %pad_add_fusion.1.choice, bf16[256,8192]{1,0:T(8,128)(2,1)} %states.3, f32[1,8192]{1,0:T(1,128)} %bitcast.20, bf16[256,2048]{1,0:T(8,128)(2,1)} %get-tuple-element.16.rest_0_), custom_call_target="tpu_custom_call", output_to_operand_aliasing={{}: (3, {})} | custom-call | tf_op jit(solution)/shard_map/text_rows/pallas_call | solution.py:75
  157.4 0.0 collective-permute-done.3.far
  157.4 0.0 all-gather.2.cloned.1.call-done.weight
  157.4 6.1 %query_products.1 = (f32[256,512]{1,0:T(8,128)}, f32[256,512]{1,0:T(8,128)}, f32[256,512]{1,0:T(8,128)}, f32[256,512]{1,0:T(8,128)}) custom-call(bf16[384,2048]{1,0:T(8,128)(2,1)} %copy-done, bf16[384,2048]{1,0:T(8,128)(2,1)} %collective-permute-done.3.far, bf16[256,2048]{1,0:T(8,128)(2,1)} %text_rows.3.own, ...), custom_call_target="tpu_custom_call" | custom-call | tf_op jit(solution)/shard_map/query_products/pallas_call | solution.py:108
  163.5 1.9 collective-permute-start.5
  165.4 2.5 %collective-permute-start.6 = (f32[256,512]{1,0:T(8,128)}, f32[256,512]{1,0:T(8,128)S(1)}, u32[]{:S(2)}, u32[]{:S(2)}) collective-permute-start(f32[256,512]{1,0:T(8,128)} %get-tuple-element.19), channel_id=1, source_target_pairs={{0,32},{16,48},{32,0},{48,16},{1,33},{17,49},{33,1},{49,17},{2,34}... | collective-permute-start | bytes 1572872 | tf_op jit(solution)/shard_map/ppermute | solution.py:22
  167.9 2.8 %collective-permute-start.7 = (f32[256,512]{1,0:T(8,128)}, f32[256,512]{1,0:T(8,128)S(1)}, u32[]{:S(2)}, u32[]{:S(2)}) collective-permute-start(f32[256,512]{1,0:T(8,128)} %get-tuple-element.20), channel_id=1, source_target_pairs={{0,16},{16,32},{32,48},{48,0},{1,17},{17,33},{33,49},{49,1},{2,18}... | collective-permute-start | bytes 1572872 | tf_op jit(solution)/shard_map/ppermute | solution.py:22
  170.7 0.0 collective-permute-done.12.after
  170.7 3.1 %collective-permute-start.14 = (bf16[4,128,256]{2,1,0:T(8,128)(2,1)S(1)}, bf16[4,128,256]{2,1,0:T(8,128)(2,1)S(1)}, u32[]{:S(2)}, u32[]{:S(2)}) collective-permute-start(bf16[4,128,256]{2,1,0:T(8,128)(2,1)S(1)} %slice.18), channel_id=1, source_target_pairs={{0,16},{16,32},{32,48},{48,0},{1,17},{17,33},{33,49},{49,1},{2,18}... | collective-permute-start | bytes 786440 | tf_op jit(solution)/shard_map/ppermute | solution.py:22
  173.8 0.0 collective-permute-done.13.before
  173.9 3.4 %collective-permute-start.15 = (bf16[4,128,256]{2,1,0:T(8,128)(2,1)S(1)}, bf16[4,128,256]{2,1,0:T(8,128)(2,1)S(1)}, u32[]{:S(2)}, u32[]{:S(2)}) collective-permute-start(bf16[4,128,256]{2,1,0:T(8,128)(2,1)S(1)} %slice.19), channel_id=1, source_target_pairs={{0,48},{16,0},{32,16},{48,32},{1,49},{17,1},{33,17},{49,33},{2,50}... | collective-permute-start | bytes 786440 | tf_op jit(solution)/shard_map/ppermute | solution.py:22
  178.0 21.7 %collective-permute-done.14.low = bf16[4,128,256]{2,1,0:T(8,128)(2,1)S(1)} collective-permute-done((bf16[4,128,256]{2,1,0:T(8,128)(2,1)S(1)}, bf16[4,128,256]{2,1,0:T(8,128)(2,1)S(1)}, u32[]{:S(2)}, u32[]{:S(2)}) %collective-permute-start.14) | collective-permute-done | bytes 262176 | tf_op jit(solution)/shard_map/ppermute | solution.py:22
  199.7 0.0 collective-permute-done.15.high
  199.7 0.0 collective-permute-done.5.share_1
  199.7 0.0 collective-permute-done.6.share_2
  199.7 0.0 collective-permute-done.7.share_3
  199.8 0.6 copy-done.12
  200.4 0.1 copy-done.13
  200.5 0.2 copy-done.8
  200.6 0.2 copy-done.9
  200.8 0.2 copy-done.10
  201.0 7.8 %attention.1 = bf16[256,512]{1,0:T(8,128)(2,1)} custom-call(s32[1]{0:T(128)} %bitcast.odd.core, s32[4,4]{1,0:T(4,128)} %owners.1, s32[4]{0:T(128)} %counts.1, f32[1]{0:T(128)S(6)} %tanh.3.gate, f32[256,512]{1,0:T(8,128)} %get-tuple-element.17.query, f32[256,512]{1,0:T(8,128)} %copy-done.8, f32[256,512]{1,0:T(8,128)} %copy-done.9, f32[256,512]{1,0:T(8,128)} %copy-done.10, ...), custom_call_target="tpu_custom_call" | custom-call | tf_op jit(solution)/shard_map/attention/pallas_call | solution.py:301
  (29 shorter events, 0.2 us)
Async XLA Ops:
  8.2 19.2 %copy-start.6 = (bf16[128,768]{1,0:T(8,128)(2,1)S(1)}, bf16[128,768]{1,0:T(8,128)(2,1)}, u32[]{:S(2)}) copy-start(bf16[128,768]{1,0:T(8,128)(2,1)} %join.1) | copy-start | bytes 589828
  8.2 19.2 %collective-permute-start.4 = (bf16[128,768]{1,0:T(8,128)(2,1)}, bf16[128,768]{1,0:T(8,128)(2,1)S(1)}, u32[]{:S(2)}, u32[]{:S(2)}) collective-permute-start(bf16[128,768]{1,0:T(8,128)(2,1)} %join.1), channel_id=1, source_target_pairs={{0,1},{1,0},{2,3},{3,2},{4,5},{5,4},{6,7},{7,6},{8,9},{9,8},{10,11... | collective-permute-start | bytes 589832 | tf_op jit(solution)/shard_map/ppermute | solution.py:22
  16.6 26.9 %all-to-all-start = ((bf16[32,8,1024]{2,1,0:T(8,128)(2,1)}), bf16[32,8,1024]{2,1,0:T(8,128)(2,1)S(1)}, u32[]{:S(2)}, u32[]{:S(2)}) async-start(bf16[32,8,1024]{2,1,0:T(8,128)(2,1)} %bitcast.16), calls=%async_computation | async-start | bytes 1048576 | tf_op jit(solution)/shard_map/all_to_all | solution.py:26
  27.3 130.1 %all-gather.2.cloned.1.call-start = ((), (), s32[]{:S(2)}) async-start(), calls=%async_computation.3 | async-start | bytes 2359296 | tf_op jit(solution)/shard_map/all_gather | solution.py:350
  43.5 9.4 %copy-start.1 = (bf16[32,8,1024]{2,1,0:T(8,128)(2,1)}, bf16[32,8,1024]{2,1,0:T(8,128)(2,1)S(1)}, u32[]{:S(2)}) copy-start(bf16[32,8,1024]{2,1,0:T(8,128)(2,1)S(1)} %all-to-all-done) | copy-start | bytes 1572868
  43.5 44.4 %collective-permute-start.8 = (bf16[32,8,1024]{2,1,0:T(8,128)(2,1)S(1)}, bf16[32,8,1024]{2,1,0:T(8,128)(2,1)S(1)}, u32[]{:S(2)}, u32[]{:S(2)}) collective-permute-start(bf16[32,8,1024]{2,1,0:T(8,128)(2,1)S(1)} %all-to-all-done), channel_id=1, source_target_pairs={{0,64},{64,0},{1,65},{65,1},{2,66},{66,2},{3,67},{67,3},{4,68},{68... | collective-permute-start | bytes 1572872 | tf_op jit(solution)/shard_map/ppermute | solution.py:22
  52.9 43.8 %collective-permute-start = (bf16[128,2048]{1,0:T(8,128)(2,1)}, bf16[128,2048]{1,0:T(8,128)(2,1)}, u32[]{:S(2)}, u32[]{:S(2)}) collective-permute-start(bf16[128,2048]{1,0:T(8,128)(2,1)} %get-tuple-element.13), channel_id=1, source_target_pairs={{0,16},{16,32},{32,48},{48,0},{1,17},{17,33},{33,49},{49,1},{2,18}... | collective-permute-start | bytes 1572872 | tf_op jit(solution)/shard_map/ppermute | solution.py:22
  56.0 31.9 %copy-start.11 = (bf16[256,256]{1,0:T(8,128)(2,1)}, bf16[256,256]{1,0:T(8,128)(2,1)S(1)}, u32[]{:S(2)}) copy-start(bf16[256,256]{1,0:T(8,128)(2,1)S(1)} %slice.17.rest_0_) | copy-start | bytes 393220
  56.0 17.4 %collective-permute-start.10 = (bf16[256,256]{1,0:T(8,128)(2,1)S(1)}, bf16[256,256]{1,0:T(8,128)(2,1)S(1)}, u32[]{:S(2)}, u32[]{:S(2)}) collective-permute-start(bf16[256,256]{1,0:T(8,128)(2,1)S(1)} %slice.17.rest_0_), channel_id=1, source_target_pairs={{0,32},{16,48},{32,0},{48,16},{1,33},{17,49},{33,1},{49,17},{2,34}... | collective-permute-start | bytes 393224 | tf_op jit(solution)/shard_map/ppermute | solution.py:22
  60.4 37.4 %collective-permute-start.1 = (bf16[128,2048]{1,0:T(8,128)(2,1)}, bf16[128,2048]{1,0:T(8,128)(2,1)}, u32[]{:S(2)}, u32[]{:S(2)}) collective-permute-start(bf16[128,2048]{1,0:T(8,128)(2,1)} %get-tuple-element.14), channel_id=1, source_target_pairs={{0,32},{16,48},{32,0},{48,16},{1,33},{17,49},{33,1},{49,17},{2,34}... | collective-permute-start | bytes 1572872 | tf_op jit(solution)/shard_map/ppermute | solution.py:22
  62.8 15.8 %collective-permute-start.11 = (bf16[256,256]{1,0:T(8,128)(2,1)S(1)}, bf16[256,256]{1,0:T(8,128)(2,1)S(1)}, u32[]{:S(2)}, u32[]{:S(2)}) collective-permute-start(bf16[256,256]{1,0:T(8,128)(2,1)S(1)} %slice.17.rest_0_), channel_id=1, source_target_pairs={{0,48},{16,0},{32,16},{48,32},{1,49},{17,1},{33,17},{49,33},{2,50}... | collective-permute-start | bytes 393224 | tf_op jit(solution)/shard_map/ppermute | solution.py:22
  73.4 14.4 %copy-start.14 = (bf16[256,256]{1,0:T(8,128)(2,1)}, bf16[256,256]{1,0:T(8,128)(2,1)S(1)}, u32[]{:S(2)}) copy-start(bf16[256,256]{1,0:T(8,128)(2,1)S(1)} %collective-permute-done.10.rest_2_) | copy-start | bytes 393220
  73.4 14.4 %collective-permute-start.9 = (bf16[256,256]{1,0:T(8,128)(2,1)S(1)}, bf16[256,256]{1,0:T(8,128)(2,1)S(1)}, u32[]{:S(2)}, u32[]{:S(2)}) collective-permute-start(bf16[256,256]{1,0:T(8,128)(2,1)S(1)} %slice.17.rest_0_), channel_id=1, source_target_pairs={{0,16},{16,32},{32,48},{48,0},{1,17},{17,33},{33,49},{49,1},{2,18}... | collective-permute-start | bytes 393224 | tf_op jit(solution)/shard_map/ppermute | solution.py:22
  78.6 9.3 %copy-start.15 = (bf16[256,256]{1,0:T(8,128)(2,1)}, bf16[256,256]{1,0:T(8,128)(2,1)S(1)}, u32[]{:S(2)}) copy-start(bf16[256,256]{1,0:T(8,128)(2,1)S(1)} %collective-permute-done.11.rest_3_) | copy-start | bytes 393220
  87.9 0.6 copy-start.16
  87.9 0.8 copy-start.7
  91.3 21.9 %all-to-all-start.1 = ((f32[8,2,4,8,256]{4,3,2,1,0:T(8,128)}), f32[8,2,4,8,256]{4,3,2,1,0:T(8,128)S(1)}, u32[]{:S(2)}, u32[]{:S(2)}) async-start(f32[8,2,4,8,256]{4,3,2,1,0:T(8,128)} %partial_sums.1), calls=%async_computation.1 | async-start | bytes 1048576 | tf_op jit(solution)/shard_map/all_to_all | solution.py:26
  94.7 14.6 %collective-permute-start.2 = (bf16[128,2048]{1,0:T(8,128)(2,1)}, bf16[128,2048]{1,0:T(8,128)(2,1)S(1)}, u32[]{:S(2)}, u32[]{:S(2)}) collective-permute-start(bf16[128,2048]{1,0:T(8,128)(2,1)} %get-tuple-element.15), channel_id=1, source_target_pairs={{0,48},{16,0},{32,16},{48,32},{1,49},{17,1},{33,17},{49,33},{2,50}... | collective-permute-start | bytes 1572872 | tf_op jit(solution)/shard_map/ppermute | solution.py:22
  109.3 36.3 %copy-start = (bf16[384,2048]{1,0:T(8,128)(2,1)}, bf16[384,2048]{1,0:T(8,128)(2,1)S(1)}, u32[]{:S(2)}) copy-start(bf16[384,2048]{1,0:T(8,128)(2,1)S(1)} %constant_dynamic-update-slice_fusion.near) | copy-start | bytes 4718596
  109.4 48.0 %collective-permute-start.3 = (bf16[384,2048]{1,0:T(8,128)(2,1)S(1)}, bf16[384,2048]{1,0:T(8,128)(2,1)}, u32[]{:S(2)}, u32[]{:S(2)}) collective-permute-start(bf16[384,2048]{1,0:T(8,128)(2,1)S(1)} %constant_dynamic-update-slice_fusion.near), channel_id=1, source_target_pairs={{0,64},{64,0},{1,65},{65,1},{2,66},{66,2},{3,67},{67,3},{4,68},{68... | collective-permute-start | bytes 4718600 | tf_op jit(solution)/shard_map/ppermute | solution.py:22
  113.2 0.8 copy-start.3
  145.7 11.7 %copy-start.2 = (bf16[8,128,256]{2,1,0:T(8,128)(2,1)}, bf16[8,128,256]{2,1,0:T(8,128)(2,1)S(1)}, u32[]{:S(2)}) copy-start(bf16[8,128,256]{2,1,0:T(8,128)(2,1)S(1)} %copy_bitcast_fusion.own) | copy-start | bytes 1572868
  145.7 25.0 %collective-permute-start.12 = (bf16[8,128,256]{2,1,0:T(8,128)(2,1)S(1)}, bf16[8,128,256]{2,1,0:T(8,128)(2,1)S(1)}, u32[]{:S(2)}, u32[]{:S(2)}) collective-permute-start(bf16[8,128,256]{2,1,0:T(8,128)(2,1)S(1)} %copy_bitcast_fusion.own), channel_id=1, source_target_pairs={{0,16},{16,32},{32,48},{48,0},{1,17},{17,33},{33,49},{49,1},{2,18}... | collective-permute-start | bytes 1572872 | tf_op jit(solution)/shard_map/ppermute | solution.py:22
  147.6 26.2 %collective-permute-start.13 = (bf16[8,128,256]{2,1,0:T(8,128)(2,1)S(1)}, bf16[8,128,256]{2,1,0:T(8,128)(2,1)S(1)}, u32[]{:S(2)}, u32[]{:S(2)}) collective-permute-start(bf16[8,128,256]{2,1,0:T(8,128)(2,1)S(1)} %copy_bitcast_fusion.own), channel_id=1, source_target_pairs={{0,48},{16,0},{32,16},{48,32},{1,49},{17,1},{33,17},{49,33},{2,50}... | collective-permute-start | bytes 1572872 | tf_op jit(solution)/shard_map/ppermute | solution.py:22
  163.5 36.2 %collective-permute-start.5 = (f32[256,512]{1,0:T(8,128)}, f32[256,512]{1,0:T(8,128)S(1)}, u32[]{:S(2)}, u32[]{:S(2)}) collective-permute-start(f32[256,512]{1,0:T(8,128)} %get-tuple-element.18), channel_id=1, source_target_pairs={{0,48},{16,0},{32,16},{48,32},{1,49},{17,1},{33,17},{49,33},{2,50}... | collective-permute-start | bytes 1572872 | tf_op jit(solution)/shard_map/ppermute | solution.py:22
  165.4 34.3 %collective-permute-start.6 = (f32[256,512]{1,0:T(8,128)}, f32[256,512]{1,0:T(8,128)S(1)}, u32[]{:S(2)}, u32[]{:S(2)}) collective-permute-start(f32[256,512]{1,0:T(8,128)} %get-tuple-element.19), channel_id=1, source_target_pairs={{0,32},{16,48},{32,0},{48,16},{1,33},{17,49},{33,1},{49,17},{2,34}... | collective-permute-start | bytes 1572872 | tf_op jit(solution)/shard_map/ppermute | solution.py:22
  167.9 31.9 %collective-permute-start.7 = (f32[256,512]{1,0:T(8,128)}, f32[256,512]{1,0:T(8,128)S(1)}, u32[]{:S(2)}, u32[]{:S(2)}) collective-permute-start(f32[256,512]{1,0:T(8,128)} %get-tuple-element.20), channel_id=1, source_target_pairs={{0,16},{16,32},{32,48},{48,0},{1,17},{17,33},{33,49},{49,1},{2,18}... | collective-permute-start | bytes 1572872 | tf_op jit(solution)/shard_map/ppermute | solution.py:22
  170.7 29.1 %copy-start.4 = (bf16[8,128,256]{2,1,0:T(8,128)(2,1)}, bf16[8,128,256]{2,1,0:T(8,128)(2,1)S(1)}, u32[]{:S(2)}) copy-start(bf16[8,128,256]{2,1,0:T(8,128)(2,1)S(1)} %collective-permute-done.12.after) | copy-start | bytes 1572868
  170.7 29.0 %collective-permute-start.14 = (bf16[4,128,256]{2,1,0:T(8,128)(2,1)S(1)}, bf16[4,128,256]{2,1,0:T(8,128)(2,1)S(1)}, u32[]{:S(2)}, u32[]{:S(2)}) collective-permute-start(bf16[4,128,256]{2,1,0:T(8,128)(2,1)S(1)} %slice.18), channel_id=1, source_target_pairs={{0,16},{16,32},{32,48},{48,0},{1,17},{17,33},{33,49},{49,1},{2,18}... | collective-permute-start | bytes 786440 | tf_op jit(solution)/shard_map/ppermute | solution.py:22
  173.8 25.9 %copy-start.5 = (bf16[8,128,256]{2,1,0:T(8,128)(2,1)}, bf16[8,128,256]{2,1,0:T(8,128)(2,1)S(1)}, u32[]{:S(2)}) copy-start(bf16[8,128,256]{2,1,0:T(8,128)(2,1)S(1)} %collective-permute-done.13.before) | copy-start | bytes 1572868
  173.9 25.8 %collective-permute-start.15 = (bf16[4,128,256]{2,1,0:T(8,128)(2,1)S(1)}, bf16[4,128,256]{2,1,0:T(8,128)(2,1)S(1)}, u32[]{:S(2)}, u32[]{:S(2)}) collective-permute-start(bf16[4,128,256]{2,1,0:T(8,128)(2,1)S(1)} %slice.19), channel_id=1, source_target_pairs={{0,48},{16,0},{32,16},{48,32},{1,49},{17,1},{33,17},{49,33},{2,50}... | collective-permute-start | bytes 786440 | tf_op jit(solution)/shard_map/ppermute | solution.py:22
  199.7 0.7 copy-start.12
  199.7 0.8 copy-start.13
  199.7 0.9 copy-start.8
  199.7 1.1 copy-start.9
  199.8 1.2 copy-start.10
Sparse Core Ops, SparseCore 0:
  30.2 39.2 all-gather.1

commit v4 on v2

--- a/solution.py
+++ b/solution.py
@@ -38,33 +38,29 @@
 scalar = pl.BlockSpec(memory_space=pltpu.SMEM)
 
 
-def half_kernel(x, z, choice, states, gain, *rest):
+def half_kernel(x, z, yh, choice, states, gain, *rest):
     outs = rest[1:]
     rows, width = states.shape
-    depth = 128
-    span = width // (x * z)
+    depth = width // (x * z * yh)
     squares = jnp.zeros((rows, depth), jnp.float32)
     for j in range(width // depth):
         wide = states[:, j * depth : (j + 1) * depth].astype(jnp.float32)
         squares += wide * wide
     scale = lax.rsqrt(jnp.sum(squares, axis=-1, keepdims=True) / width + norm_epsilon)
-    even = choice[1] == 0
-    for k in range(z):
-        for m in range(x // 2):
-            blocks = []
-            for p in range(2):
-                start = ((2 * m + p) * z + k) * span
-                at = slice(start, start + span)
-                wide = states[:, at].astype(jnp.float32)
-                blocks.append((wide * scale * gain[:, at]).astype(jnp.bfloat16))
-            start = (k * (x // 2) + m) * span
-            lanes = slice(start, start + span)
-            outs[0][:, lanes] = jnp.where(even, blocks[0], blocks[1])
-            if len(outs) > 1:
-                outs[1][:, lanes] = jnp.where(even, blocks[1], blocks[0])
-
-
-def half_rows(states, gain, choice, base, x, z):
+    for index, out in enumerate(outs):
+        home = choice[1] if index == 0 else choice[1] + 1 - 2 * lax.rem(choice[1], 2)
+        for k in range(z):
+            for m in range(x // 2):
+                for h in range(yh):
+                    place = (lax.rem(home + 2 * m, x) * z + k) * yh + lax.rem(choice[2] + h, yh)
+                    at = pl.ds(pl.multiple_of(place * depth, depth), depth)
+                    wide = states[:, at].astype(jnp.float32)
+                    start = ((k * (x // 2) + m) * yh + h) * depth
+                    block = wide * scale * gain[:, at]
+                    out[:, start : start + depth] = block.astype(out.dtype)
+
+
+def half_rows(states, gain, choice, base, x, z, yh):
     total, width = states.shape
     rows = 32
     steps = total // 2 // rows
@@ -77,7 +73,7 @@
         shapes.append(jax.ShapeDtypeStruct((total // 2, width // 2), jnp.bfloat16))
         places.append(pl.BlockSpec((rows, width // 2), lambda i, c: (i, 0)))
     return pl.pallas_call(
-        functools.partial(half_kernel, x, z),
+        functools.partial(half_kernel, x, z, yh),
         grid_spec=pltpu.PrefetchScalarGridSpec(
             num_scalar_prefetch=1,
             grid=(steps,),
@@ -115,6 +111,25 @@
     )(*parts)
 
 
+def pile_kernel(first, last, *refs):
+    *parts, out = refs
+    rows = parts[0].shape[0]
+    for k, part in enumerate(parts):
+        out[k * rows : (k + 1) * rows] = part[:, first:last]
+
+
+def pile(parts, first, last):
+    shape = (len(parts) * parts[0].shape[0], last - first)
+    return pl.pallas_call(
+        functools.partial(pile_kernel, first, last),
+        in_specs=[whole(p.shape) for p in parts],
+        out_specs=whole(shape),
+        grid=(1,),
+        out_shape=jax.ShapeDtypeStruct(shape, parts[0].dtype),
+        name="pile",
+    )(*parts)
+
+
 def columns_kernel(x, vision, out):
     copies, z, _, width = out.shape
     span = width // x
@@ -138,39 +153,42 @@
     )(vision)
 
 
-def partial_kernel(spot, here, there, *rest):
+def partial_kernel(x, spot, here, there, *rest):
     *weights, out = rest
-    z, _, yl, tokens, width = out.shape
-    x = len(weights)
+    z, _, yl, tokens, _ = out.shape
+    yh = len(weights) // x
     span = weights[0].shape[0]
+    columns = jnp.concatenate([w[...] for w in weights], axis=0)
+    starts = []
+    for k in range(x):
+        for h in range(yh):
+            place = lax.rem(spot[0] + x - k, x) * yh + lax.rem(spot[1] + h, yh)
+            starts.append(pl.multiple_of(place * span, span))
     for c, part in enumerate((here, there)):
-        product = jnp.zeros((part.shape[0], width), jnp.float32)
-        for k, weight in enumerate(weights):
-            start = pl.multiple_of(lax.rem(spot[0] + x - k, x) * span, span)
-            product += jnp.dot(
-                part[:, pl.ds(start, span)], weight[...], preferred_element_type=jnp.float32
-            )
+        rows = jnp.concatenate([part[:, pl.ds(start, span)] for start in starts], axis=1)
+        product = jnp.dot(rows, columns, preferred_element_type=jnp.float32)
         for a in range(yl):
             for k in range(z):
                 row = (a * z + k) * tokens
                 out[k, c, a] = product[row : row + tokens]
 
 
-def partial_sums(here, there, spot, weights, width, z, yl, tokens):
+def partial_sums(here, there, spot, weights, width, x, z, yl, tokens):
+    depth = here.shape[1] // len(weights)
     shape = (z, 2, yl, tokens, width)
     return pl.pallas_call(
-        partial_kernel,
+        functools.partial(partial_kernel, x),
         in_specs=[
             scalar,
             whole(here.shape),
             whole(there.shape),
-            *(whole((w.shape[0], width)) for w in weights),
+            *(pl.BlockSpec((depth, width), lambda _, r=r: (r, 0)) for _, r in weights),
         ],
         out_specs=whole(shape),
         grid=(1,),
         out_shape=jax.ShapeDtypeStruct(shape, jnp.float32),
         name="partial_sums",
-    )(spot, here, there, *weights)
+    )(spot, here, there, *(w for w, _ in weights))
 
 
 def pair_kernel(odd, parts, k_gain, out):
@@ -309,21 +327,31 @@
     place = lax.axis_index("x")
     core = lax.axis_index("co")
 
-    def ordered(early, mine, other):
-        return jnp.where(
-            early,
-            jnp.concatenate((mine, other), axis=0),
-            jnp.concatenate((other, mine), axis=0),
-        )
+    high_y = lax.axis_index("yh")
 
     joined = join(k_weight, v_weight, q_weight)
-    other = shift(joined, "yh", 1)
-    both = ordered(lax.axis_index("yh") == 0, joined, other)
-    far = shift(both, "x", 2)
-    near = both[:, : 2 * head]
-    pair_weight = (both, shift(near, "x", 1), far, shift(near, "x", 3))
-
-    rows_q = ordered(place < 2, both[:, 2 * head :], far[:, 2 * head :])
+    over = shift(joined, "yh", 1)
+    far = shift(joined, "x", 2)
+    both = lax.ppermute(
+        joined,
+        ("x", "yh"),
+        [(i * yh + h, (i + 2) % x * yh + 1 - h) for i in range(x) for h in range(yh)],
+    )
+    near = pile((joined, over), 0, 2 * head)
+    left = shift(near, "x", 1)
+    right = shift(near, "x", 3)
+    pair_weight = [
+        (joined, 0),
+        (over, 0),
+        (left, 0),
+        (left, 1),
+        (far, 0),
+        (both, 0),
+        (right, 0),
+        (right, 1),
+    ]
+
+    rows_q = pile((joined, over, far, both), 2 * head, joined.shape[1])
     q_half = lax.all_gather(rows_q, "z", axis=0, tiled=True)
 
     columns = columns_of(vision.reshape(tokens, width), yl, x, z)
@@ -331,26 +359,26 @@
 
     gate = jnp.tanh(gate_value)
 
-    mine = lax.rem(place, 2)
     gain = text_gain[None]
 
     def partner(array):
         return lax.ppermute(array, "x", [(i, i ^ 1) for i in range(x)])
 
-    choice = jnp.stack((core, mine)).astype(jnp.int32)
-    text_half, sent = half_rows(text_states, gain, choice, None, x, z)
+    choice = jnp.stack((core, place, high_y)).astype(jnp.int32)
+    text_half, sent = half_rows(text_states, gain, choice, None, x, z, yh)
     guest = partner(sent)
     guest_other = shift(guest, "co", 1)
-    choice = jnp.stack((1 - core, mine)).astype(jnp.int32)
-    (text_half,) = half_rows(text_states, gain, choice, text_half, x, z)
+    choice = jnp.stack((1 - core, place, high_y)).astype(jnp.int32)
+    (text_half,) = half_rows(text_states, gain, choice, text_half, x, z, yh)
 
     there = shift(here, "co", 1)
     partial = partial_sums(
         here.reshape(yl * z * tokens, width // z),
         there.reshape(yl * z * tokens, width // z),
-        place.astype(jnp.int32)[None],
+        jnp.stack((place, high_y)).astype(jnp.int32),
         pair_weight,
         2 * head,
+        x,
         z,
         yl,
         tokens,

time: 204 us -> 203 us (level)
  waiting for transfers between devices: 66.6 us -> 58.5 us
  Pallas kernels: 25.3 us -> 29.1 us
  blocking collectives: 28 us -> 30.6 us
    ppermute x10, waiting for transfers between devices: 27.7 us -> 8.9 us  [shift(): lax.ppermute(array, axis, [(i, (i + step) % size) for i in range(size)])]
    ppermute x0 -> x1, waiting for transfers between devices: none -> 10.6 us  [on_device(): lax.ppermute(joined, ('x', 'yh'), [(i * yh + h, (i + 2) % x * yh + 1 - h)...]
    pallas_call x3 -> x5, Pallas kernels: 12.5 us -> 16.3 us  [the longest x2 9.86 us: half_rows(): pl.pallas_call(functools.partial(half_kernel, x, z, yh), grid_spec=pltpu....]
    ppermute x0 -> x1, starting transfers between devices: none -> 3.76 us  [on_device(): lax.ppermute(joined, ('x', 'yh'), [(i * yh + h, (i + 2) % x * yh + 1 - h)...]
    all_to_all x1, blocking collectives: 28 us -> 30.6 us  [exchange(): return lax.all_to_all(array, axes, 0, 0, tiled=True)]
    dot_general x1, matrix products: 0.78 us -> 3.05 us  [on_device(): guest_near = jnp.dot(guest, q_half, preferred_element_type=jnp.float32)]
    select_n x2 -> x0, other arithmetic: 2.16 us -> none  [ordered(): jnp.where(early, jnp.concatenate((mine, other), axis=0), jnp.concatenate(...]
  transfers between devices with their start and end apart: 16 -> 17, of which waited for: 9 -> 10; matrix products, arithmetic and copies ran while one was open for 4% -> 4% of each run, Pallas kernels for 8% -> 9%
where the time goes in v4:
time: 203 us; the launch traced here: 202 us
  waiting for transfers between devices  58.5 us (29%)
  starting transfers between devices  57.7 us (28%)
  blocking collectives  30.6 us (15%)
  Pallas kernels  29.1 us (14%)
  between operations  14.4 us (7%)
  matrix products  7.09 us (3%)
  local copies, waits for them, and re-layouts  3.16 us (2%)
    ppermute x10, starting transfers between devices, shift(): lax.ppermute(array, axis, [(i, (i + step) % size) for i in range(size)])  36.3 us
    all_to_all x2, waiting for transfers between devices, exchange(): return lax.all_to_all(array, axes, 0, 0, tiled=True)  33.3 us
    all_to_all x1, blocking collectives, exchange(): return lax.all_to_all(array, axes, 0, 0, tiled=True)  30.6 us
    ppermute x1, waiting for transfers between devices, on_device(): lax.ppermute(joined, ('x', 'yh'), [(i * yh + h, (i + 2) % x * yh + 1 - h)...  10.6 us
    pallas_call x2, Pallas kernels, half_rows(): pl.pallas_call(functools.partial(half_kernel, x, z, yh), grid_spec=pltpu....  9.86 us
    all_to_all x2, starting transfers between devices, exchange(): return lax.all_to_all(array, axes, 0, 0, tiled=True)  9.62 us
    ppermute x10, waiting for transfers between devices, shift(): lax.ppermute(array, axis, [(i, (i + step) % size) for i in range(size)])  8.9 us
    ppermute x3, starting transfers between devices, partner(): return lax.ppermute(array, 'x', [(i, i ^ 1) for i in range(x)])  7.98 us
  transfers between devices with their start and end apart: 17, of which 10 were waited for; matrix products, arithmetic and copies ran while one was open for 4% of the time, Pallas kernels for 9%

profile of v4, /device:TPU:80, one launch (start us, length us, event | category | flops | bytes accessed | tf_op | source)
XLA Modules:
  0.0 202.3 jit_solution(16021192499987476024)
XLA Ops:
  6.5 0.0 all-gather.2.cloned.1.call-start
  6.5 1.6 join.1.refs_0_.rest_0_
  8.2 5.9 %collective-permute-start = (bf16[128,768]{1,0:T(8,128)(2,1)}, bf16[128,768]{1,0:T(8,128)(2,1)S(1)}, u32[]{:S(2)}, u32[]{:S(2)}) collective-permute-start(bf16[128,768]{1,0:T(8,128)(2,1)} %join.1.refs_0_.rest_0_), channel_id=1, source_target_pairs={{0,1},{1,0},{2,3},{3,2},{4,5},{5,4},{6,7},{7,6},{8,9},{9,8},{10,11... | collective-permute-start | bytes 589832 | tf_op jit(solution)/shard_map/ppermute | solution.py:22
  14.1 4.9 %collective-permute-start.1 = (bf16[128,768]{1,0:T(8,128)(2,1)}, bf16[128,768]{1,0:T(8,128)(2,1)S(1)}, u32[]{:S(2)}, u32[]{:S(2)}) collective-permute-start(bf16[128,768]{1,0:T(8,128)(2,1)} %join.1.refs_0_.rest_0_), channel_id=1, source_target_pairs={{0,32},{16,48},{32,0},{48,16},{1,33},{17,49},{33,1},{49,17},{2,34}... | collective-permute-start | bytes 589832 | tf_op jit(solution)/shard_map/ppermute | solution.py:22
  19.0 3.8 %collective-permute-start.2 = (bf16[128,768]{1,0:T(8,128)(2,1)}, bf16[128,768]{1,0:T(8,128)(2,1)S(1)}, u32[]{:S(2)}, u32[]{:S(2)}) collective-permute-start(bf16[128,768]{1,0:T(8,128)(2,1)} %join.1.refs_0_.rest_0_), channel_id=1, source_target_pairs={{0,33},{1,32},{16,49},{17,48},{32,1},{33,0},{48,17},{49,16},{2,35}... | collective-permute-start | bytes 589832 | tf_op jit(solution)/shard_map/ppermute | solution.py:335
  22.8 2.3 %collective-permute-done.refs_1_.rest_1_ = bf16[128,768]{1,0:T(8,128)(2,1)S(1)} collective-permute-done((bf16[128,768]{1,0:T(8,128)(2,1)}, bf16[128,768]{1,0:T(8,128)(2,1)S(1)}, u32[]{:S(2)}, u32[]{:S(2)}) %collective-permute-start) | collective-permute-done | bytes 196640 | tf_op jit(solution)/shard_map/ppermute | solution.py:22
  25.1 0.0 collective-permute-done.1.refs_2_.rest_4_
  25.1 10.6 %collective-permute-done.2.refs_3_.rest_5_ = bf16[128,768]{1,0:T(8,128)(2,1)S(1)} collective-permute-done((bf16[128,768]{1,0:T(8,128)(2,1)}, bf16[128,768]{1,0:T(8,128)(2,1)S(1)}, u32[]{:S(2)}, u32[]{:S(2)}) %collective-permute-start.2) | collective-permute-done | bytes 196640 | tf_op jit(solution)/shard_map/ppermute | solution.py:335
  35.7 0.0 copy-done.5
  35.7 0.0 copy-done.8
  35.7 0.7 copy-done.9
  36.4 2.1 %pile.2 = bf16[512,512]{1,0:T(8,128)(2,1)} custom-call(bf16[128,768]{1,0:T(8,128)(2,1)} %join.1.refs_0_.rest_0_, bf16[128,768]{1,0:T(8,128)(2,1)} %copy-done.5, bf16[128,768]{1,0:T(8,128)(2,1)} %copy-done.8, bf16[128,768]{1,0:T(8,128)(2,1)} %copy-done.9), custom_call_target="tpu_custom_call" | custom-call | tf_op jit(solution)/shard_map/pile/pallas_call | solution.py:123
  38.4 0.0 all-gather.2.cloned.1.call-update
  38.5 1.7 columns.1
  40.2 30.6 %all_to_all.15 = bf16[32,8,1024]{2,1,0:T(8,128)(2,1)S(1)} all-to-all(bf16[32,8,1024]{2,1,0:T(8,128)(2,1)} %bitcast.22), channel_id=1, replica_groups=mesh['yl'=4,'co'=2,'x'=4,'z'=8,'yh'=2] {'yl','z'}, dimensions={0} | all-to-all | bytes 1048576 | tf_op jit(solution)/shard_map/all_to_all | solution.py:26
  70.8 1.9 collective-permute-start.7
  72.7 1.7 pile.3
  74.4 2.3 %collective-permute-start.8 = (bf16[256,256]{1,0:T(8,128)(2,1)}, bf16[256,256]{1,0:T(8,128)(2,1)S(1)}, u32[]{:S(2)}, u32[]{:S(2)}) collective-permute-start(bf16[256,256]{1,0:T(8,128)(2,1)} %pile.3), channel_id=1, source_target_pairs={{0,16},{16,32},{32,48},{48,0},{1,17},{17,33},{33,49},{49,1},{2,18}... | collective-permute-start | bytes 393224 | tf_op jit(solution)/shard_map/ppermute | solution.py:22
  76.7 4.8 %collective-permute-start.9 = (bf16[256,256]{1,0:T(8,128)(2,1)}, bf16[256,256]{1,0:T(8,128)(2,1)S(1)}, u32[]{:S(2)}, u32[]{:S(2)}) collective-permute-start(bf16[256,256]{1,0:T(8,128)(2,1)} %pile.3), channel_id=1, source_target_pairs={{0,48},{16,0},{32,16},{48,32},{1,49},{17,1},{33,17},{49,33},{2,50}... | collective-permute-start | bytes 393224 | tf_op jit(solution)/shard_map/ppermute | solution.py:22
  81.5 0.6 pad_add_fusion.spot
  82.1 1.5 collective-permute-done.8.rest_2_.rest_3_
  83.6 1.3 collective-permute-done.9.rest_6_.rest_7_
  84.9 0.0 collective-permute-done.7
  84.9 0.0 copy-done.3
  84.9 0.0 copy-done.10
  84.9 0.6 copy-done.11
  85.6 0.2 copy-done.12
  85.8 2.6 %partial_sums.1 = f32[8,2,4,8,256]{4,3,2,1,0:T(8,128)} custom-call(s32[2]{0:T(128)} %pad_add_fusion.spot, bf16[256,1024]{1,0:T(8,128)(2,1)} %bitcast.23, bf16[256,1024]{1,0:T(8,128)(2,1)} %bitcast.24, bf16[128,768]{1,0:T(8,128)(2,1)} %join.1.refs_0_.rest_0_, bf16[128,768]{1,0:T(8,128)(2,1)} %copy-done.5, bf16[256,256]{1,0:T(8,128)(2,1)} %copy-done.10, ...), custom_call_target="tpu_custom_call" | custom-call | tf_op jit(solution)/shard_map/partial_sums/pallas_call | solution.py:179
  88.4 4.5 %all-to-all-start.1 = ((f32[8,2,4,8,256]{4,3,2,1,0:T(8,128)}), f32[8,2,4,8,256]{4,3,2,1,0:T(8,128)S(1)}, u32[]{:S(2)}, u32[]{:S(2)}) async-start(f32[8,2,4,8,256]{4,3,2,1,0:T(8,128)} %partial_sums.1), calls=%async_computation.1 | async-start | bytes 1048576 | tf_op jit(solution)/shard_map/all_to_all | solution.py:26
  92.9 0.6 add_add_fusion.1.choice
  93.5 5.1 %half_rows.2 = (bf16[256,4096]{1,0:T(8,128)(2,1)}, bf16[128,4096]{1,0:T(8,128)(2,1)}) custom-call(s32[3]{0:T(128)} %add_add_fusion.1.choice, bf16[256,8192]{1,0:T(8,128)(2,1)} %states.3, f32[1,8192]{1,0:T(1,128)} %bitcast.25, f32[1,8192]{1,0:T(1,128)} %bitcast.26), custom_call_target="tpu_custom_call" | custom-call | tf_op jit(solution)/shard_map/half_rows/pallas_call | solution.py:75
  98.6 2.0 collective-permute-start.3
  100.6 14.9 %all-to-all-done.1.parts = f32[8,2,4,8,256]{4,3,2,1,0:T(8,128)S(1)} async-done(((f32[8,2,4,8,256]{4,3,2,1,0:T(8,128)}), f32[8,2,4,8,256]{4,3,2,1,0:T(8,128)S(1)}, u32[]{:S(2)}, u32[]{:S(2)}) %all-to-all-start.1) | async-done | bytes 524320 | tf_op jit(solution)/shard_map/all_to_all | solution.py:26
  115.5 0.8 copy-done.1
  116.3 2.0 key_value_pairs.1
  118.3 5.1 %all-to-all-start.2 = ((bf16[16,8,8,256]{3,2,1,0:T(8,128)(2,1)}), bf16[16,8,8,256]{3,2,1,0:T(8,128)(2,1)S(1)}, u32[]{:S(2)}, u32[]{:S(2)}) async-start(bf16[16,8,8,256]{3,2,1,0:T(8,128)(2,1)} %key_value_pairs.1), calls=%async_computation.2 | async-start | bytes 1048576 | tf_op jit(solution)/shard_map/all_to_all | solution.py:26
  123.5 1.4 collective-permute-done.3
  124.9 1.9 collective-permute-start.5
  126.8 18.4 %all-to-all-done.2 = bf16[16,8,8,256]{3,2,1,0:T(8,128)(2,1)S(1)} async-done(((bf16[16,8,8,256]{3,2,1,0:T(8,128)(2,1)}), bf16[16,8,8,256]{3,2,1,0:T(8,128)(2,1)S(1)}, u32[]{:S(2)}, u32[]{:S(2)}) %all-to-all-start.2) | async-done | bytes 524320 | tf_op jit(solution)/shard_map/all_to_all | solution.py:26
  145.2 0.0 copy-start.2
  145.2 2.4 %collective-permute-start.10 = (bf16[8,128,256]{2,1,0:T(8,128)(2,1)S(1)}, bf16[8,128,256]{2,1,0:T(8,128)(2,1)S(1)}, u32[]{:S(2)}, u32[]{:S(2)}) collective-permute-start(bf16[8,128,256]{2,1,0:T(8,128)(2,1)S(1)} %copy_bitcast_fusion.own), channel_id=1, source_target_pairs={{0,16},{16,32},{32,48},{48,0},{1,17},{17,33},{33,49},{49,1},{2,18}... | collective-permute-start | bytes 1572872 | tf_op jit(solution)/shard_map/ppermute | solution.py:22
  147.6 5.1 %collective-permute-start.11 = (bf16[8,128,256]{2,1,0:T(8,128)(2,1)S(1)}, bf16[8,128,256]{2,1,0:T(8,128)(2,1)S(1)}, u32[]{:S(2)}, u32[]{:S(2)}) collective-permute-start(bf16[8,128,256]{2,1,0:T(8,128)(2,1)S(1)} %copy_bitcast_fusion.own), channel_id=1, source_target_pairs={{0,48},{16,0},{32,16},{48,32},{1,49},{17,1},{33,17},{49,33},{2,50}... | collective-permute-start | bytes 1572872 | tf_op jit(solution)/shard_map/ppermute | solution.py:22
  153.5 0.6 add_add_fusion.choice
  154.1 4.7 %half_rows.3 = bf16[256,4096]{1,0:T(8,128)(2,1)} custom-call(s32[3]{0:T(128)} %add_add_fusion.choice, bf16[256,8192]{1,0:T(8,128)(2,1)} %states.3, f32[1,8192]{1,0:T(1,128)} %bitcast.27, bf16[256,4096]{1,0:T(8,128)(2,1)} %get-tuple-element.7.rest_0_), custom_call_target="tpu_custom_call", output_to_operand_aliasing={{}: (3, {})} | custom-call | tf_op jit(solution)/shard_map/half_rows/pallas_call | solution.py:75
  158.8 0.0 copy-done.2
  158.8 3.8 %collective-permute-done.10.after = bf16[8,128,256]{2,1,0:T(8,128)(2,1)S(1)} collective-permute-done((bf16[8,128,256]{2,1,0:T(8,128)(2,1)S(1)}, bf16[8,128,256]{2,1,0:T(8,128)(2,1)S(1)}, u32[]{:S(2)}, u32[]{:S(2)}) %collective-permute-start.10) | collective-permute-done | bytes 524320 | tf_op jit(solution)/shard_map/ppermute | solution.py:22
  162.7 1.9 collective-permute-start.12
  164.6 0.0 collective-permute-done.11.before
  164.6 0.0 copy-start.7
  164.6 5.1 %collective-permute-start.13 = (bf16[4,128,256]{2,1,0:T(8,128)(2,1)S(1)}, bf16[4,128,256]{2,1,0:T(8,128)(2,1)S(1)}, u32[]{:S(2)}, u32[]{:S(2)}) collective-permute-start(bf16[4,128,256]{2,1,0:T(8,128)(2,1)S(1)} %slice.9), channel_id=1, source_target_pairs={{0,48},{16,0},{32,16},{48,32},{1,49},{17,1},{33,17},{49,33},{2,50}... | collective-permute-start | bytes 786440 | tf_op jit(solution)/shard_map/ppermute | solution.py:22
  169.8 0.0 all-gather.2.cloned.1.call-done
  169.8 0.0 copy-start
  169.8 3.1 %fusion.1 = f32[128,512]{1,0:T(8,128)S(1)} fusion(bf16[128,4096]{1,0:T(8,128)(2,1)S(1)} %collective-permute-done.3, bf16[4096,512]{1,0:T(8,128)(2,1)} %all-gather.2.cloned.1.call-done), kind=kOutput, calls=%fused_computation.5 | convolution fusion | flops 536870912 | bytes 5505024 | tf_op jit(solution)/shard_map/dot_general | solution.py:397
  172.9 2.1 %collective-permute-start.4 = (f32[128,512]{1,0:T(8,128)S(1)}, f32[128,512]{1,0:T(8,128)S(1)}, u32[]{:S(2)}, u32[]{:S(2)}) collective-permute-start(f32[128,512]{1,0:T(8,128)S(1)} %fusion.1), channel_id=1, source_target_pairs={{0,16},{16,0},{32,48},{48,32},{1,17},{17,1},{33,49},{49,33},{2,18}... | collective-permute-start | bytes 786440 | tf_op jit(solution)/shard_map/ppermute | solution.py:365
  174.9 0.0 collective-permute-done.5
  175.0 2.0 fusion.2
  177.0 3.9 %collective-permute-start.6 = (f32[128,512]{1,0:T(8,128)S(1)}, f32[128,512]{1,0:T(8,128)S(1)}, u32[]{:S(2)}, u32[]{:S(2)}) collective-permute-start(f32[128,512]{1,0:T(8,128)S(1)} %fusion.2), channel_id=1, source_target_pairs={{0,16},{16,0},{32,48},{48,32},{1,17},{17,1},{33,49},{49,33},{2,18}... | collective-permute-start | bytes 786440 | tf_op jit(solution)/shard_map/ppermute | solution.py:365
  180.9 2.0 %fusion.query = f32[256,512]{1,0:T(8,128)} fusion(bf16[256,4096]{1,0:T(8,128)(2,1)S(1)} %copy-done.4, bf16[4096,512]{1,0:T(8,128)(2,1)S(1)} %copy-done), kind=kOutput, calls=%fused_computation.4 | convolution fusion | flops 1073741824 | bytes 6815744 | tf_op jit(solution)/shard_map/dot_general | solution.py:401
  183.0 0.0 collective-permute-done.12.low
  183.0 0.0 collective-permute-done.13.high
  183.0 0.4 collective-permute-done.4.near
  183.4 4.0 %collective-permute-done.6.far = f32[128,512]{1,0:T(8,128)S(1)} collective-permute-done((f32[128,512]{1,0:T(8,128)S(1)}, f32[128,512]{1,0:T(8,128)S(1)}, u32[]{:S(2)}, u32[]{:S(2)}) %collective-permute-start.6) | collective-permute-done | bytes 262176 | tf_op jit(solution)/shard_map/ppermute | solution.py:365
  187.3 0.7 copy-done.16
  188.0 7.4 %attention.1 = bf16[256,512]{1,0:T(8,128)(2,1)} custom-call(s32[1]{0:T(128)} %bitcast.odd.core, s32[4,4]{1,0:T(4,128)} %owners.1, s32[4]{0:T(128)} %counts.1, f32[1]{0:T(128)S(6)} %tanh.3.gate, f32[256,512]{1,0:T(8,128)} %fusion.query, f32[128,512]{1,0:T(8,128)} %copy-done.15, f32[128,512]{1,0:T(8,128)} %copy-done.16, f32[1,128]{1,0:T(1,128)} %bitcast.30, ...), custom_call_target="tpu_custom_call" | custom-call | tf_op jit(solution)/shard_map/attention/pallas_call | solution.py:293
  (24 shorter events, 0.1 us)
Async XLA Ops:
  6.5 163.3 %all-gather.2.cloned.1.call-start = ((), (), s32[]{:S(2)}) async-start(), calls=%async_computation.3 | async-start | bytes 4718592 | tf_op jit(solution)/shard_map/all_gather | solution.py:355
  8.2 16.9 %collective-permute-start = (bf16[128,768]{1,0:T(8,128)(2,1)}, bf16[128,768]{1,0:T(8,128)(2,1)S(1)}, u32[]{:S(2)}, u32[]{:S(2)}) collective-permute-start(bf16[128,768]{1,0:T(8,128)(2,1)} %join.1.refs_0_.rest_0_), channel_id=1, source_target_pairs={{0,1},{1,0},{2,3},{3,2},{4,5},{5,4},{6,7},{7,6},{8,9},{9,8},{10,11... | collective-permute-start | bytes 589832 | tf_op jit(solution)/shard_map/ppermute | solution.py:22
  14.1 11.0 %collective-permute-start.1 = (bf16[128,768]{1,0:T(8,128)(2,1)}, bf16[128,768]{1,0:T(8,128)(2,1)S(1)}, u32[]{:S(2)}, u32[]{:S(2)}) collective-permute-start(bf16[128,768]{1,0:T(8,128)(2,1)} %join.1.refs_0_.rest_0_), channel_id=1, source_target_pairs={{0,32},{16,48},{32,0},{48,16},{1,33},{17,49},{33,1},{49,17},{2,34}... | collective-permute-start | bytes 589832 | tf_op jit(solution)/shard_map/ppermute | solution.py:22
  19.0 16.6 %collective-permute-start.2 = (bf16[128,768]{1,0:T(8,128)(2,1)}, bf16[128,768]{1,0:T(8,128)(2,1)S(1)}, u32[]{:S(2)}, u32[]{:S(2)}) collective-permute-start(bf16[128,768]{1,0:T(8,128)(2,1)} %join.1.refs_0_.rest_0_), channel_id=1, source_target_pairs={{0,33},{1,32},{16,49},{17,48},{32,1},{33,0},{48,17},{49,16},{2,35}... | collective-permute-start | bytes 589832 | tf_op jit(solution)/shard_map/ppermute | solution.py:335
  25.1 10.6 %copy-start.5 = (bf16[128,768]{1,0:T(8,128)(2,1)}, bf16[128,768]{1,0:T(8,128)(2,1)S(1)}, u32[]{:S(2)}) copy-start(bf16[128,768]{1,0:T(8,128)(2,1)S(1)} %collective-permute-done.refs_1_.rest_1_) | copy-start | bytes 589828
  25.1 10.6 %copy-start.8 = (bf16[128,768]{1,0:T(8,128)(2,1)}, bf16[128,768]{1,0:T(8,128)(2,1)S(1)}, u32[]{:S(2)}) copy-start(bf16[128,768]{1,0:T(8,128)(2,1)S(1)} %collective-permute-done.1.refs_2_.rest_4_) | copy-start | bytes 589828
  35.7 0.7 copy-start.9
  70.8 14.1 %copy-start.3 = (bf16[32,8,1024]{2,1,0:T(8,128)(2,1)}, bf16[32,8,1024]{2,1,0:T(8,128)(2,1)S(1)}, u32[]{:S(2)}) copy-start(bf16[32,8,1024]{2,1,0:T(8,128)(2,1)S(1)} %all_to_all.15) | copy-start | bytes 1572868
  70.8 14.1 %collective-permute-start.7 = (bf16[32,8,1024]{2,1,0:T(8,128)(2,1)S(1)}, bf16[32,8,1024]{2,1,0:T(8,128)(2,1)S(1)}, u32[]{:S(2)}, u32[]{:S(2)}) collective-permute-start(bf16[32,8,1024]{2,1,0:T(8,128)(2,1)S(1)} %all_to_all.15), channel_id=1, source_target_pairs={{0,64},{64,0},{1,65},{65,1},{2,66},{66,2},{3,67},{67,3},{4,68},{68... | collective-permute-start | bytes 1572872 | tf_op jit(solution)/shard_map/ppermute | solution.py:22
  74.4 9.2 %collective-permute-start.8 = (bf16[256,256]{1,0:T(8,128)(2,1)}, bf16[256,256]{1,0:T(8,128)(2,1)S(1)}, u32[]{:S(2)}, u32[]{:S(2)}) collective-permute-start(bf16[256,256]{1,0:T(8,128)(2,1)} %pile.3), channel_id=1, source_target_pairs={{0,16},{16,32},{32,48},{48,0},{1,17},{17,33},{33,49},{49,1},{2,18}... | collective-permute-start | bytes 393224 | tf_op jit(solution)/shard_map/ppermute | solution.py:22
  76.7 8.2 %collective-permute-start.9 = (bf16[256,256]{1,0:T(8,128)(2,1)}, bf16[256,256]{1,0:T(8,128)(2,1)S(1)}, u32[]{:S(2)}, u32[]{:S(2)}) collective-permute-start(bf16[256,256]{1,0:T(8,128)(2,1)} %pile.3), channel_id=1, source_target_pairs={{0,48},{16,0},{32,16},{48,32},{1,49},{17,1},{33,17},{49,33},{2,50}... | collective-permute-start | bytes 393224 | tf_op jit(solution)/shard_map/ppermute | solution.py:22
  83.6 1.3 copy-start.10
  84.9 0.7 copy-start.11
  84.9 0.9 copy-start.12
  88.4 27.1 %all-to-all-start.1 = ((f32[8,2,4,8,256]{4,3,2,1,0:T(8,128)}), f32[8,2,4,8,256]{4,3,2,1,0:T(8,128)S(1)}, u32[]{:S(2)}, u32[]{:S(2)}) async-start(f32[8,2,4,8,256]{4,3,2,1,0:T(8,128)} %partial_sums.1), calls=%async_computation.1 | async-start | bytes 1048576 | tf_op jit(solution)/shard_map/all_to_all | solution.py:26
  98.6 26.3 %collective-permute-start.3 = (bf16[128,4096]{1,0:T(8,128)(2,1)}, bf16[128,4096]{1,0:T(8,128)(2,1)S(1)}, u32[]{:S(2)}, u32[]{:S(2)}) collective-permute-start(bf16[128,4096]{1,0:T(8,128)(2,1)} %get-tuple-element.8), channel_id=1, source_target_pairs={{0,16},{16,0},{32,48},{48,32},{1,17},{17,1},{33,49},{49,33},{2,18}... | collective-permute-start | bytes 3145736 | tf_op jit(solution)/shard_map/ppermute | solution.py:365
  115.5 0.8 copy-start.1
  118.3 26.8 %all-to-all-start.2 = ((bf16[16,8,8,256]{3,2,1,0:T(8,128)(2,1)}), bf16[16,8,8,256]{3,2,1,0:T(8,128)(2,1)S(1)}, u32[]{:S(2)}, u32[]{:S(2)}) async-start(bf16[16,8,8,256]{3,2,1,0:T(8,128)(2,1)} %key_value_pairs.1), calls=%async_computation.2 | async-start | bytes 1048576 | tf_op jit(solution)/shard_map/all_to_all | solution.py:26
  124.9 50.1 %collective-permute-start.5 = (bf16[128,4096]{1,0:T(8,128)(2,1)S(1)}, bf16[128,4096]{1,0:T(8,128)(2,1)}, u32[]{:S(2)}, u32[]{:S(2)}) collective-permute-start(bf16[128,4096]{1,0:T(8,128)(2,1)S(1)} %collective-permute-done.3), channel_id=1, source_target_pairs={{0,64},{64,0},{1,65},{65,1},{2,66},{66,2},{3,67},{67,3},{4,68},{68... | collective-permute-start | bytes 3145736 | tf_op jit(solution)/shard_map/ppermute | solution.py:22
  145.2 13.7 %copy-start.2 = (bf16[8,128,256]{2,1,0:T(8,128)(2,1)}, bf16[8,128,256]{2,1,0:T(8,128)(2,1)S(1)}, u32[]{:S(2)}) copy-start(bf16[8,128,256]{2,1,0:T(8,128)(2,1)S(1)} %copy_bitcast_fusion.own) | copy-start | bytes 1572868
  145.2 17.4 %collective-permute-start.10 = (bf16[8,128,256]{2,1,0:T(8,128)(2,1)S(1)}, bf16[8,128,256]{2,1,0:T(8,128)(2,1)S(1)}, u32[]{:S(2)}, u32[]{:S(2)}) collective-permute-start(bf16[8,128,256]{2,1,0:T(8,128)(2,1)S(1)} %copy_bitcast_fusion.own), channel_id=1, source_target_pairs={{0,16},{16,32},{32,48},{48,0},{1,17},{17,33},{33,49},{49,1},{2,18}... | collective-permute-start | bytes 1572872 | tf_op jit(solution)/shard_map/ppermute | solution.py:22
  147.6 17.0 %collective-permute-start.11 = (bf16[8,128,256]{2,1,0:T(8,128)(2,1)S(1)}, bf16[8,128,256]{2,1,0:T(8,128)(2,1)S(1)}, u32[]{:S(2)}, u32[]{:S(2)}) collective-permute-start(bf16[8,128,256]{2,1,0:T(8,128)(2,1)S(1)} %copy_bitcast_fusion.own), channel_id=1, source_target_pairs={{0,48},{16,0},{32,16},{48,32},{1,49},{17,1},{33,17},{49,33},{2,50}... | collective-permute-start | bytes 1572872 | tf_op jit(solution)/shard_map/ppermute | solution.py:22
  162.6 14.3 %copy-start.6 = (bf16[8,128,256]{2,1,0:T(8,128)(2,1)}, bf16[8,128,256]{2,1,0:T(8,128)(2,1)S(1)}, u32[]{:S(2)}) copy-start(bf16[8,128,256]{2,1,0:T(8,128)(2,1)S(1)} %collective-permute-done.10.after) | copy-start | bytes 1572868
  162.7 20.3 %collective-permute-start.12 = (bf16[4,128,256]{2,1,0:T(8,128)(2,1)S(1)}, bf16[4,128,256]{2,1,0:T(8,128)(2,1)S(1)}, u32[]{:S(2)}, u32[]{:S(2)}) collective-permute-start(bf16[4,128,256]{2,1,0:T(8,128)(2,1)S(1)} %slice.8), channel_id=1, source_target_pairs={{0,16},{16,32},{32,48},{48,0},{1,17},{17,33},{33,49},{49,1},{2,18}... | collective-permute-start | bytes 786440 | tf_op jit(solution)/shard_map/ppermute | solution.py:22
  164.6 12.4 %copy-start.7 = (bf16[8,128,256]{2,1,0:T(8,128)(2,1)}, bf16[8,128,256]{2,1,0:T(8,128)(2,1)S(1)}, u32[]{:S(2)}) copy-start(bf16[8,128,256]{2,1,0:T(8,128)(2,1)S(1)} %collective-permute-done.11.before) | copy-start | bytes 1572868
  164.6 18.3 %collective-permute-start.13 = (bf16[4,128,256]{2,1,0:T(8,128)(2,1)S(1)}, bf16[4,128,256]{2,1,0:T(8,128)(2,1)S(1)}, u32[]{:S(2)}, u32[]{:S(2)}) collective-permute-start(bf16[4,128,256]{2,1,0:T(8,128)(2,1)S(1)} %slice.9), channel_id=1, source_target_pairs={{0,48},{16,0},{32,16},{48,32},{1,49},{17,1},{33,17},{49,33},{2,50}... | collective-permute-start | bytes 786440 | tf_op jit(solution)/shard_map/ppermute | solution.py:22
  169.8 5.2 %copy-start = (bf16[4096,512]{1,0:T(8,128)(2,1)S(1)}, bf16[4096,512]{1,0:T(8,128)(2,1)}, u32[]{:S(2)}) copy-start(bf16[4096,512]{1,0:T(8,128)(2,1)} %all-gather.2.cloned.1.call-done) | copy-start | bytes 12582916
  169.8 11.1 %copy-start.4 = (bf16[256,4096]{1,0:T(8,128)(2,1)S(1)}, bf16[256,4096]{1,0:T(8,128)(2,1)}, u32[]{:S(2)}) copy-start(bf16[256,4096]{1,0:T(8,128)(2,1)} %half_rows.3) | copy-start | bytes 6291460
  172.9 10.5 %collective-permute-start.4 = (f32[128,512]{1,0:T(8,128)S(1)}, f32[128,512]{1,0:T(8,128)S(1)}, u32[]{:S(2)}, u32[]{:S(2)}) collective-permute-start(f32[128,512]{1,0:T(8,128)S(1)} %fusion.1), channel_id=1, source_target_pairs={{0,16},{16,0},{32,48},{48,32},{1,17},{17,1},{33,49},{49,33},{2,18}... | collective-permute-start | bytes 786440 | tf_op jit(solution)/shard_map/ppermute | solution.py:365
  177.0 10.3 %collective-permute-start.6 = (f32[128,512]{1,0:T(8,128)S(1)}, f32[128,512]{1,0:T(8,128)S(1)}, u32[]{:S(2)}, u32[]{:S(2)}) collective-permute-start(f32[128,512]{1,0:T(8,128)S(1)} %fusion.2), channel_id=1, source_target_pairs={{0,16},{16,0},{32,48},{48,32},{1,17},{17,1},{33,49},{49,33},{2,18}... | collective-permute-start | bytes 786440 | tf_op jit(solution)/shard_map/ppermute | solution.py:365
  183.0 4.4 %copy-start.13 = (bf16[4,128,256]{2,1,0:T(8,128)(2,1)}, bf16[4,128,256]{2,1,0:T(8,128)(2,1)S(1)}, u32[]{:S(2)}) copy-start(bf16[4,128,256]{2,1,0:T(8,128)(2,1)S(1)} %collective-permute-done.12.low) | copy-start | bytes 786436
  183.0 4.4 %copy-start.14 = (bf16[4,128,256]{2,1,0:T(8,128)(2,1)}, bf16[4,128,256]{2,1,0:T(8,128)(2,1)S(1)}, u32[]{:S(2)}) copy-start(bf16[4,128,256]{2,1,0:T(8,128)(2,1)S(1)} %collective-permute-done.13.high) | copy-start | bytes 786436
  183.4 4.0 %copy-start.15 = (f32[128,512]{1,0:T(8,128)}, f32[128,512]{1,0:T(8,128)S(1)}, u32[]{:S(2)}) copy-start(f32[128,512]{1,0:T(8,128)S(1)} %collective-permute-done.4.near) | copy-start | bytes 786436
  187.3 0.7 copy-start.16
Sparse Core Ops, SparseCore 0:
  38.6 79.6 all-gather.1

commit v5 on v2

--- a/solution.py
+++ b/solution.py
@@ -210,12 +210,12 @@
 
 
 def attention_kernel(
-    core, owners, counts, gate, query, near, far, q_gain, own, after, before, low, high, out
+    core, owners, counts, gate, query, near, far, q_gain, *rest
 ):
+    *pieces, out = rest
     block = pl.program_id(0)
     rows, width = query.shape
-    images = own.shape[0]
-    half = low.shape[0]
+    images = pieces[0].shape[0]
     head = q_gain.shape[1]
     heads = width // head
     slots = owners.shape[1]
@@ -241,10 +241,7 @@
             valid = valid & (names[i] != names[j])
         live = live | valid
         image = jnp.clip(names[j], 0, images - 1)
-        lower = jnp.minimum(image, half - 1)
-        upper = jnp.maximum(image - half, 0)
-        across = jnp.where(image < half, low[lower], high[upper])
-        pairs = jnp.concatenate((own[image], after[image], before[image], across), axis=0)
+        pairs = jnp.concatenate([piece[image] for piece in pieces], axis=0)
         values.append(pairs[:, head:])
         score = (
             lax.dot_general(
@@ -360,11 +357,7 @@
     pair = pairs_of(odd, parts, k_gain[None], z * yh)
     own = exchange(pair, ("z", "yh"))
     own = own.transpose(1, 0, 2, 3).reshape(yl * co, z * yh * tokens, 2 * head)
-    after = shift(own, "x", 1)
-    before = shift(own, "x", -1)
-    half = yl * co // 2
-    low = shift(after[:half], "x", 1)
-    high = shift(before[half:], "x", -1)
+    pieces = [own, *(shift(own, "x", k) for k in range(1, x))]
 
     guest_near = jnp.dot(guest, q_half, preferred_element_type=jnp.float32)
     guest_far = jnp.dot(guest_other, q_half, preferred_element_type=jnp.float32)
@@ -380,7 +373,7 @@
         back_near,
         back_far,
         q_gain[None],
-        (own, after, before, low, high),
+        pieces,
     )
 
 

time: 204 us -> 201 us (0.985)
  starting transfers between devices: 56.3 us -> 52.6 us
    all_to_all x2, waiting for transfers between devices: 33.5 us -> 27.2 us  [exchange(): return lax.all_to_all(array, axes, 0, 0, tiled=True)]
    ppermute x3, waiting for transfers between devices: 5.36 us -> 10.2 us  [partner(): return lax.ppermute(array, 'x', [(i, i ^ 1) for i in range(x)])]
    ppermute x10 -> x9, starting transfers between devices: 35.8 us -> 32.3 us  [shift(): lax.ppermute(array, axis, [(i, (i + step) % size) for i in range(size)])]
    ppermute x10 -> x9, waiting for transfers between devices: 27.7 us -> 30.2 us  [shift(): lax.ppermute(array, axis, [(i, (i + step) % size) for i in range(size)])]
  transfers between devices with their start and end apart: 16 -> 15, of which waited for: 9 -> 10; matrix products, arithmetic and copies ran while one was open for 4% -> 4% of each run, Pallas kernels for 8% -> 8%
where the time goes in v5:
time: 201 us; the launch traced here: 200 us
  waiting for transfers between devices  67.6 us (34%)
  starting transfers between devices  52.6 us (26%)
  blocking collectives  28 us (14%)
  Pallas kernels  25.2 us (13%)
  between operations  14.3 us (7%)
  matrix products  7.48 us (4%)
  other arithmetic  3.35 us (2%)
    ppermute x9, starting transfers between devices, shift(): lax.ppermute(array, axis, [(i, (i + step) % size) for i in range(size)])  32.3 us
    ppermute x9, waiting for transfers between devices, shift(): lax.ppermute(array, axis, [(i, (i + step) % size) for i in range(size)])  30.2 us
    all_to_all x1, blocking collectives, exchange(): return lax.all_to_all(array, axes, 0, 0, tiled=True)  28 us
    all_to_all x2, waiting for transfers between devices, exchange(): return lax.all_to_all(array, axes, 0, 0, tiled=True)  27.2 us
    all_to_all x2, starting transfers between devices, exchange(): return lax.all_to_all(array, axes, 0, 0, tiled=True)  11.1 us
    ppermute x3, waiting for transfers between devices, partner(): return lax.ppermute(array, 'x', [(i, i ^ 1) for i in range(x)])  10.2 us
    pallas_call x2, Pallas kernels, half_rows(): pl.pallas_call(functools.partial(half_kernel, x, z), grid_spec=pltpu.Pref...  9.87 us
    ppermute x3, starting transfers between devices, partner(): return lax.ppermute(array, 'x', [(i, i ^ 1) for i in range(x)])  9.23 us
  transfers between devices with their start and end apart: 15, of which 10 were waited for; matrix products, arithmetic and copies ran while one was open for 4% of the time, Pallas kernels for 8%

profile of v5, /device:TPU:80, one launch (start us, length us, event | category | flops | bytes accessed | tf_op | source)
XLA Modules:
  0.0 200.3 jit_solution(9674667101646402395)
XLA Ops:
  6.5 0.0 all-gather.2.cloned.1.call-start
  6.5 1.6 join.1
  8.2 5.9 %collective-permute-start = (bf16[128,768]{1,0:T(8,128)(2,1)}, bf16[128,768]{1,0:T(8,128)(2,1)S(1)}, u32[]{:S(2)}, u32[]{:S(2)}) collective-permute-start(bf16[128,768]{1,0:T(8,128)(2,1)} %join.1), channel_id=1, source_target_pairs={{0,1},{1,0},{2,3},{3,2},{4,5},{5,4},{6,7},{7,6},{8,9},{9,8},{10,11... | collective-permute-start | bytes 589832 | tf_op jit(solution)/shard_map/ppermute | solution.py:22
  14.1 11.0 %collective-permute-done = bf16[128,768]{1,0:T(8,128)(2,1)S(1)} collective-permute-done((bf16[128,768]{1,0:T(8,128)(2,1)}, bf16[128,768]{1,0:T(8,128)(2,1)S(1)}, u32[]{:S(2)}, u32[]{:S(2)}) %collective-permute-start) | collective-permute-done | bytes 196640 | tf_op jit(solution)/shard_map/ppermute | solution.py:22
  25.1 1.1 maximum_select_fusion.1.rest_0_
  26.2 0.0 copy-start.1
  26.2 4.9 %collective-permute-start.1 = (bf16[256,768]{1,0:T(8,128)(2,1)S(1)}, bf16[256,768]{1,0:T(8,128)(2,1)S(1)}, u32[]{:S(2)}, u32[]{:S(2)}) collective-permute-start(bf16[256,768]{1,0:T(8,128)(2,1)S(1)} %maximum_select_fusion.1.rest_0_), channel_id=1, source_target_pairs={{0,32},{16,48},{32,0},{48,16},{1,33},{17,49},{33,1},{49,17},{2,34}... | collective-permute-start | bytes 1179656 | tf_op jit(solution)/shard_map/ppermute | solution.py:22
  31.2 9.4 %collective-permute-done.1.rest_2_ = bf16[256,768]{1,0:T(8,128)(2,1)S(1)} collective-permute-done((bf16[256,768]{1,0:T(8,128)(2,1)S(1)}, bf16[256,768]{1,0:T(8,128)(2,1)S(1)}, u32[]{:S(2)}, u32[]{:S(2)}) %collective-permute-start.1) | collective-permute-done | bytes 393248 | tf_op jit(solution)/shard_map/ppermute | solution.py:22
  40.6 0.0 copy-start.6
  40.6 1.1 maximum_select_fusion
  41.7 0.0 all-gather.2.cloned.1.call-update
  41.7 1.8 columns.1
  43.4 28.0 %all_to_all.15 = bf16[32,8,1024]{2,1,0:T(8,128)(2,1)S(1)} all-to-all(bf16[32,8,1024]{2,1,0:T(8,128)(2,1)} %bitcast.22), channel_id=1, replica_groups=mesh['yl'=4,'co'=2,'x'=4,'z'=8,'yh'=2] {'yl','z'}, dimensions={0} | all-to-all | bytes 1048576 | tf_op jit(solution)/shard_map/all_to_all | solution.py:26
  71.4 0.0 copy-start.4
  71.4 1.9 collective-permute-start.6
  73.3 3.4 %collective-permute-start.7 = (bf16[256,256]{1,0:T(8,128)(2,1)S(1)}, bf16[256,256]{1,0:T(8,128)(2,1)S(1)}, u32[]{:S(2)}, u32[]{:S(2)}) collective-permute-start(bf16[256,256]{1,0:T(8,128)(2,1)S(1)} %slice.14), channel_id=1, source_target_pairs={{0,16},{16,32},{32,48},{48,0},{1,17},{17,33},{33,49},{49,1},{2,18}... | collective-permute-start | bytes 393224 | tf_op jit(solution)/shard_map/ppermute | solution.py:22
  76.8 3.7 %collective-permute-start.8 = (bf16[256,256]{1,0:T(8,128)(2,1)S(1)}, bf16[256,256]{1,0:T(8,128)(2,1)S(1)}, u32[]{:S(2)}, u32[]{:S(2)}) collective-permute-start(bf16[256,256]{1,0:T(8,128)(2,1)S(1)} %slice.14), channel_id=1, source_target_pairs={{0,48},{16,0},{32,16},{48,32},{1,49},{17,1},{33,17},{49,33},{2,50}... | collective-permute-start | bytes 393224 | tf_op jit(solution)/shard_map/ppermute | solution.py:22
  80.4 1.9 collective-permute-done.7.rest_1_
  82.4 0.0 copy-start.10
  82.4 1.9 collective-permute-done.8.rest_3_
  84.3 0.0 collective-permute-done.6
  84.3 0.0 copy-done.1
  84.3 0.0 copy-done.6
  84.3 0.0 copy-done.4
  84.3 0.0 copy-done.10
  84.3 0.6 copy-done.11
  84.9 0.2 copy-done.8
  85.1 2.6 %partial_sums.1 = f32[8,2,4,8,256]{4,3,2,1,0:T(8,128)} custom-call(s32[1]{0:T(128)} %bitcast.5.spot, bf16[256,1024]{1,0:T(8,128)(2,1)} %bitcast.23, bf16[256,1024]{1,0:T(8,128)(2,1)} %bitcast.24, bf16[256,768]{1,0:T(8,128)(2,1)} %copy-done.1, bf16[256,256]{1,0:T(8,128)(2,1)} %copy-done.10, bf16[256,768]{1,0:T(8,128)(2,1)} %copy-done.6, ...), custom_call_target="tpu_custom_call" | custom-call | tf_op jit(solution)/shard_map/partial_sums/pallas_call | solution.py:161
  87.7 4.5 %all-to-all-start.1 = ((f32[8,2,4,8,256]{4,3,2,1,0:T(8,128)}), f32[8,2,4,8,256]{4,3,2,1,0:T(8,128)S(1)}, u32[]{:S(2)}, u32[]{:S(2)}) async-start(f32[8,2,4,8,256]{4,3,2,1,0:T(8,128)} %partial_sums.1), calls=%async_computation.1 | async-start | bytes 1048576 | tf_op jit(solution)/shard_map/all_to_all | solution.py:26
  92.2 0.6 pad_add_fusion.1.choice
  92.8 5.1 %half_rows.2 = (bf16[256,4096]{1,0:T(8,128)(2,1)}, bf16[128,4096]{1,0:T(8,128)(2,1)}) custom-call(s32[2]{0:T(128)} %pad_add_fusion.1.choice, bf16[256,8192]{1,0:T(8,128)(2,1)} %states.3, f32[1,8192]{1,0:T(1,128)} %bitcast.25, f32[1,8192]{1,0:T(1,128)} %bitcast.26), custom_call_target="tpu_custom_call" | custom-call | tf_op jit(solution)/shard_map/half_rows/pallas_call | solution.py:79
  97.9 3.4 %collective-permute-start.2 = (bf16[128,4096]{1,0:T(8,128)(2,1)}, bf16[128,4096]{1,0:T(8,128)(2,1)}, u32[]{:S(2)}, u32[]{:S(2)}) collective-permute-start(bf16[128,4096]{1,0:T(8,128)(2,1)} %get-tuple-element.8), channel_id=1, source_target_pairs={{0,16},{16,0},{32,48},{48,32},{1,17},{17,1},{33,49},{49,33},{2,18}... | collective-permute-start | bytes 3145736 | tf_op jit(solution)/shard_map/ppermute | solution.py:335
  101.3 13.6 %all-to-all-done.1.parts = f32[8,2,4,8,256]{4,3,2,1,0:T(8,128)S(1)} async-done(((f32[8,2,4,8,256]{4,3,2,1,0:T(8,128)}), f32[8,2,4,8,256]{4,3,2,1,0:T(8,128)S(1)}, u32[]{:S(2)}, u32[]{:S(2)}) %all-to-all-start.1) | async-done | bytes 524320 | tf_op jit(solution)/shard_map/all_to_all | solution.py:26
  114.9 0.8 copy-done.2
  115.7 2.0 key_value_pairs.1
  117.6 6.6 %all-to-all-start.2 = ((bf16[16,8,8,256]{3,2,1,0:T(8,128)(2,1)}), bf16[16,8,8,256]{3,2,1,0:T(8,128)(2,1)S(1)}, u32[]{:S(2)}, u32[]{:S(2)}) async-start(bf16[16,8,8,256]{3,2,1,0:T(8,128)(2,1)} %key_value_pairs.1), calls=%async_computation.2 | async-start | bytes 1048576 | tf_op jit(solution)/shard_map/all_to_all | solution.py:26
  124.2 0.2 collective-permute-done.2
  124.4 1.9 collective-permute-start.4
  127.0 0.6 pad_add_fusion.choice
  127.6 4.8 %half_rows.3 = bf16[256,4096]{1,0:T(8,128)(2,1)} custom-call(s32[2]{0:T(128)} %pad_add_fusion.choice, bf16[256,8192]{1,0:T(8,128)(2,1)} %states.3, f32[1,8192]{1,0:T(1,128)} %bitcast.27, bf16[256,4096]{1,0:T(8,128)(2,1)} %get-tuple-element.7.rest_0_), custom_call_target="tpu_custom_call", output_to_operand_aliasing={{}: (3, {})} | custom-call | tf_op jit(solution)/shard_map/half_rows/pallas_call | solution.py:79
  132.4 13.6 %all-to-all-done.2 = bf16[16,8,8,256]{3,2,1,0:T(8,128)(2,1)S(1)} async-done(((bf16[16,8,8,256]{3,2,1,0:T(8,128)(2,1)}), bf16[16,8,8,256]{3,2,1,0:T(8,128)(2,1)S(1)}, u32[]{:S(2)}, u32[]{:S(2)}) %all-to-all-start.2) | async-done | bytes 524320 | tf_op jit(solution)/shard_map/all_to_all | solution.py:26
  146.0 0.0 copy-start.3
  146.0 4.8 %collective-permute-start.10 = (bf16[8,128,256]{2,1,0:T(8,128)(2,1)S(1)}, bf16[8,128,256]{2,1,0:T(8,128)(2,1)S(1)}, u32[]{:S(2)}, u32[]{:S(2)}) collective-permute-start(bf16[8,128,256]{2,1,0:T(8,128)(2,1)S(1)} %copy_bitcast_fusion.rest_0_), channel_id=1, source_target_pairs={{0,32},{16,48},{32,0},{48,16},{1,33},{17,49},{33,1},{49,17},{2,34}... | collective-permute-start | bytes 1572872 | tf_op jit(solution)/shard_map/ppermute | solution.py:22
  150.8 3.3 %collective-permute-start.11 = (bf16[8,128,256]{2,1,0:T(8,128)(2,1)S(1)}, bf16[8,128,256]{2,1,0:T(8,128)(2,1)}, u32[]{:S(2)}, u32[]{:S(2)}) collective-permute-start(bf16[8,128,256]{2,1,0:T(8,128)(2,1)S(1)} %copy_bitcast_fusion.rest_0_), channel_id=1, source_target_pairs={{0,48},{16,0},{32,16},{48,32},{1,49},{17,1},{33,17},{49,33},{2,50}... | collective-permute-start | bytes 1572872 | tf_op jit(solution)/shard_map/ppermute | solution.py:22
  154.1 2.5 %collective-permute-start.9 = (bf16[8,128,256]{2,1,0:T(8,128)(2,1)S(1)}, bf16[8,128,256]{2,1,0:T(8,128)(2,1)}, u32[]{:S(2)}, u32[]{:S(2)}) collective-permute-start(bf16[8,128,256]{2,1,0:T(8,128)(2,1)S(1)} %copy_bitcast_fusion.rest_0_), channel_id=1, source_target_pairs={{0,16},{16,32},{32,48},{48,0},{1,17},{17,33},{33,49},{49,1},{2,18}... | collective-permute-start | bytes 1572872 | tf_op jit(solution)/shard_map/ppermute | solution.py:22
  156.6 0.0 collective-permute-done.4
  156.6 0.0 all-gather.2.cloned.1.call-done
  156.7 0.0 copy-start
  156.7 3.4 %fusion.2 = f32[128,512]{1,0:T(8,128)S(1)} fusion(bf16[128,4096]{1,0:T(8,128)(2,1)} %collective-permute-done.4, bf16[4096,512]{1,0:T(8,128)(2,1)} %all-gather.2.cloned.1.call-done), kind=kOutput, calls=%fused_computation.7 | convolution fusion | flops 536870912 | bytes 5505024 | tf_op jit(solution)/shard_map/dot_general | solution.py:363
  160.1 3.1 %collective-permute-start.5 = (f32[128,512]{1,0:T(8,128)S(1)}, f32[128,512]{1,0:T(8,128)S(1)}, u32[]{:S(2)}, u32[]{:S(2)}) collective-permute-start(f32[128,512]{1,0:T(8,128)S(1)} %fusion.2), channel_id=1, source_target_pairs={{0,16},{16,0},{32,48},{48,32},{1,17},{17,1},{33,49},{49,33},{2,18}... | collective-permute-start | bytes 786440 | tf_op jit(solution)/shard_map/ppermute | solution.py:335
  163.1 0.0 copy-done
  163.2 2.0 fusion.1
  165.2 0.0 copy-done.3
  165.2 2.8 %collective-permute-start.3 = (f32[128,512]{1,0:T(8,128)S(1)}, f32[128,512]{1,0:T(8,128)}, u32[]{:S(2)}, u32[]{:S(2)}) collective-permute-start(f32[128,512]{1,0:T(8,128)S(1)} %fusion.1), channel_id=1, source_target_pairs={{0,16},{16,0},{32,48},{48,32},{1,17},{17,1},{33,49},{49,33},{2,18}... | collective-permute-start | bytes 786440 | tf_op jit(solution)/shard_map/ppermute | solution.py:335
  167.9 0.0 copy-done.5
  168.0 2.1 %fusion.query = f32[256,512]{1,0:T(8,128)} fusion(bf16[256,4096]{1,0:T(8,128)(2,1)S(1)} %copy-done.5, bf16[4096,512]{1,0:T(8,128)(2,1)S(1)} %copy-done), kind=kOutput, calls=%fused_computation.5 | convolution fusion | flops 1073741824 | bytes 6815744 | tf_op jit(solution)/shard_map/dot_general | solution.py:366
  170.1 0.0 collective-permute-done.10.rest_2_
  170.1 6.0 %collective-permute-done.11.rest_3_ = bf16[8,128,256]{2,1,0:T(8,128)(2,1)} collective-permute-done((bf16[8,128,256]{2,1,0:T(8,128)(2,1)S(1)}, bf16[8,128,256]{2,1,0:T(8,128)(2,1)}, u32[]{:S(2)}, u32[]{:S(2)}) %collective-permute-start.11) | collective-permute-done | bytes 524320 | tf_op jit(solution)/shard_map/ppermute | solution.py:22
  176.1 0.0 collective-permute-done.9.rest_1_
  176.1 5.5 %collective-permute-done.5.far = f32[128,512]{1,0:T(8,128)S(1)} collective-permute-done((f32[128,512]{1,0:T(8,128)S(1)}, f32[128,512]{1,0:T(8,128)S(1)}, u32[]{:S(2)}, u32[]{:S(2)}) %collective-permute-start.5) | collective-permute-done | bytes 262176 | tf_op jit(solution)/shard_map/ppermute | solution.py:335
  181.6 4.5 %collective-permute-done.3.near = f32[128,512]{1,0:T(8,128)} collective-permute-done((f32[128,512]{1,0:T(8,128)S(1)}, f32[128,512]{1,0:T(8,128)}, u32[]{:S(2)}, u32[]{:S(2)}) %collective-permute-start.3) | collective-permute-done | bytes 262176 | tf_op jit(solution)/shard_map/ppermute | solution.py:335
  186.1 0.0 copy-done.7
  186.1 0.0 copy-done.9
  186.1 7.4 %attention.1 = bf16[256,512]{1,0:T(8,128)(2,1)} custom-call(s32[1]{0:T(128)} %bitcast.odd.core, s32[4,4]{1,0:T(4,128)} %owners.1, s32[4]{0:T(128)} %counts.1, f32[1]{0:T(128)S(6)} %tanh.3.gate, f32[256,512]{1,0:T(8,128)} %fusion.query, f32[128,512]{1,0:T(8,128)} %collective-permute-done.3.near, f32[128,512]{1,0:T(8,128)} %copy-done.9, f32[1,128]{1,0:T(1,128)} %bitcast.30, ...), custom_call_target="tpu_custom_call" | custom-call | tf_op jit(solution)/shard_map/attention/pallas_call | solution.py:272
  (10 shorter events, 0.1 us)
Async XLA Ops:
  6.5 150.1 %all-gather.2.cloned.1.call-start = ((), (), s32[]{:S(2)}) async-start(), calls=%async_computation.3 | async-start | bytes 4718592 | tf_op jit(solution)/shard_map/all_gather | solution.py:324
  8.2 16.9 %collective-permute-start = (bf16[128,768]{1,0:T(8,128)(2,1)}, bf16[128,768]{1,0:T(8,128)(2,1)S(1)}, u32[]{:S(2)}, u32[]{:S(2)}) collective-permute-start(bf16[128,768]{1,0:T(8,128)(2,1)} %join.1), channel_id=1, source_target_pairs={{0,1},{1,0},{2,3},{3,2},{4,5},{5,4},{6,7},{7,6},{8,9},{9,8},{10,11... | collective-permute-start | bytes 589832 | tf_op jit(solution)/shard_map/ppermute | solution.py:22
  26.2 58.1 %copy-start.1 = (bf16[256,768]{1,0:T(8,128)(2,1)}, bf16[256,768]{1,0:T(8,128)(2,1)S(1)}, u32[]{:S(2)}) copy-start(bf16[256,768]{1,0:T(8,128)(2,1)S(1)} %maximum_select_fusion.1.rest_0_) | copy-start | bytes 1179652
  26.2 14.3 %collective-permute-start.1 = (bf16[256,768]{1,0:T(8,128)(2,1)S(1)}, bf16[256,768]{1,0:T(8,128)(2,1)S(1)}, u32[]{:S(2)}, u32[]{:S(2)}) collective-permute-start(bf16[256,768]{1,0:T(8,128)(2,1)S(1)} %maximum_select_fusion.1.rest_0_), channel_id=1, source_target_pairs={{0,32},{16,48},{32,0},{48,16},{1,33},{17,49},{33,1},{49,17},{2,34}... | collective-permute-start | bytes 1179656 | tf_op jit(solution)/shard_map/ppermute | solution.py:22
  40.6 43.7 %copy-start.6 = (bf16[256,768]{1,0:T(8,128)(2,1)}, bf16[256,768]{1,0:T(8,128)(2,1)S(1)}, u32[]{:S(2)}) copy-start(bf16[256,768]{1,0:T(8,128)(2,1)S(1)} %collective-permute-done.1.rest_2_) | copy-start | bytes 1179652
  71.4 12.9 %copy-start.4 = (bf16[32,8,1024]{2,1,0:T(8,128)(2,1)}, bf16[32,8,1024]{2,1,0:T(8,128)(2,1)S(1)}, u32[]{:S(2)}) copy-start(bf16[32,8,1024]{2,1,0:T(8,128)(2,1)S(1)} %all_to_all.15) | copy-start | bytes 1572868
  71.4 12.9 %collective-permute-start.6 = (bf16[32,8,1024]{2,1,0:T(8,128)(2,1)S(1)}, bf16[32,8,1024]{2,1,0:T(8,128)(2,1)S(1)}, u32[]{:S(2)}, u32[]{:S(2)}) collective-permute-start(bf16[32,8,1024]{2,1,0:T(8,128)(2,1)S(1)} %all_to_all.15), channel_id=1, source_target_pairs={{0,64},{64,0},{1,65},{65,1},{2,66},{66,2},{3,67},{67,3},{4,68},{68... | collective-permute-start | bytes 1572872 | tf_op jit(solution)/shard_map/ppermute | solution.py:22
  73.3 9.0 %collective-permute-start.7 = (bf16[256,256]{1,0:T(8,128)(2,1)S(1)}, bf16[256,256]{1,0:T(8,128)(2,1)S(1)}, u32[]{:S(2)}, u32[]{:S(2)}) collective-permute-start(bf16[256,256]{1,0:T(8,128)(2,1)S(1)} %slice.14), channel_id=1, source_target_pairs={{0,16},{16,32},{32,48},{48,0},{1,17},{17,33},{33,49},{49,1},{2,18}... | collective-permute-start | bytes 393224 | tf_op jit(solution)/shard_map/ppermute | solution.py:22
  76.8 7.5 %collective-permute-start.8 = (bf16[256,256]{1,0:T(8,128)(2,1)S(1)}, bf16[256,256]{1,0:T(8,128)(2,1)S(1)}, u32[]{:S(2)}, u32[]{:S(2)}) collective-permute-start(bf16[256,256]{1,0:T(8,128)(2,1)S(1)} %slice.14), channel_id=1, source_target_pairs={{0,48},{16,0},{32,16},{48,32},{1,49},{17,1},{33,17},{49,33},{2,50}... | collective-permute-start | bytes 393224 | tf_op jit(solution)/shard_map/ppermute | solution.py:22
  82.4 2.0 copy-start.10
  84.3 0.7 copy-start.11
  84.3 0.8 copy-start.8
  87.7 27.2 %all-to-all-start.1 = ((f32[8,2,4,8,256]{4,3,2,1,0:T(8,128)}), f32[8,2,4,8,256]{4,3,2,1,0:T(8,128)S(1)}, u32[]{:S(2)}, u32[]{:S(2)}) async-start(f32[8,2,4,8,256]{4,3,2,1,0:T(8,128)} %partial_sums.1), calls=%async_computation.1 | async-start | bytes 1048576 | tf_op jit(solution)/shard_map/all_to_all | solution.py:26
  97.9 26.5 %collective-permute-start.2 = (bf16[128,4096]{1,0:T(8,128)(2,1)}, bf16[128,4096]{1,0:T(8,128)(2,1)}, u32[]{:S(2)}, u32[]{:S(2)}) collective-permute-start(bf16[128,4096]{1,0:T(8,128)(2,1)} %get-tuple-element.8), channel_id=1, source_target_pairs={{0,16},{16,0},{32,48},{48,32},{1,17},{17,1},{33,49},{49,33},{2,18}... | collective-permute-start | bytes 3145736 | tf_op jit(solution)/shard_map/ppermute | solution.py:335
  114.9 0.8 copy-start.2
  117.6 28.3 %all-to-all-start.2 = ((bf16[16,8,8,256]{3,2,1,0:T(8,128)(2,1)}), bf16[16,8,8,256]{3,2,1,0:T(8,128)(2,1)S(1)}, u32[]{:S(2)}, u32[]{:S(2)}) async-start(bf16[16,8,8,256]{3,2,1,0:T(8,128)(2,1)} %key_value_pairs.1), calls=%async_computation.2 | async-start | bytes 1048576 | tf_op jit(solution)/shard_map/all_to_all | solution.py:26
  124.4 32.2 %collective-permute-start.4 = (bf16[128,4096]{1,0:T(8,128)(2,1)}, bf16[128,4096]{1,0:T(8,128)(2,1)}, u32[]{:S(2)}, u32[]{:S(2)}) collective-permute-start(bf16[128,4096]{1,0:T(8,128)(2,1)} %collective-permute-done.2), channel_id=1, source_target_pairs={{0,64},{64,0},{1,65},{65,1},{2,66},{66,2},{3,67},{67,3},{4,68},{68... | collective-permute-start | bytes 3145736 | tf_op jit(solution)/shard_map/ppermute | solution.py:22
  146.0 22.0 %copy-start.5 = (bf16[256,4096]{1,0:T(8,128)(2,1)S(1)}, bf16[256,4096]{1,0:T(8,128)(2,1)}, u32[]{:S(2)}) copy-start(bf16[256,4096]{1,0:T(8,128)(2,1)} %half_rows.3) | copy-start | bytes 6291460
  146.0 19.2 %copy-start.3 = (bf16[8,128,256]{2,1,0:T(8,128)(2,1)}, bf16[8,128,256]{2,1,0:T(8,128)(2,1)S(1)}, u32[]{:S(2)}) copy-start(bf16[8,128,256]{2,1,0:T(8,128)(2,1)S(1)} %copy_bitcast_fusion.rest_0_) | copy-start | bytes 1572868
  146.0 24.1 %collective-permute-start.10 = (bf16[8,128,256]{2,1,0:T(8,128)(2,1)S(1)}, bf16[8,128,256]{2,1,0:T(8,128)(2,1)S(1)}, u32[]{:S(2)}, u32[]{:S(2)}) collective-permute-start(bf16[8,128,256]{2,1,0:T(8,128)(2,1)S(1)} %copy_bitcast_fusion.rest_0_), channel_id=1, source_target_pairs={{0,32},{16,48},{32,0},{48,16},{1,33},{17,49},{33,1},{49,17},{2,34}... | collective-permute-start | bytes 1572872 | tf_op jit(solution)/shard_map/ppermute | solution.py:22
  150.8 25.3 %collective-permute-start.11 = (bf16[8,128,256]{2,1,0:T(8,128)(2,1)S(1)}, bf16[8,128,256]{2,1,0:T(8,128)(2,1)}, u32[]{:S(2)}, u32[]{:S(2)}) collective-permute-start(bf16[8,128,256]{2,1,0:T(8,128)(2,1)S(1)} %copy_bitcast_fusion.rest_0_), channel_id=1, source_target_pairs={{0,48},{16,0},{32,16},{48,32},{1,49},{17,1},{33,17},{49,33},{2,50}... | collective-permute-start | bytes 1572872 | tf_op jit(solution)/shard_map/ppermute | solution.py:22
  154.1 22.0 %collective-permute-start.9 = (bf16[8,128,256]{2,1,0:T(8,128)(2,1)S(1)}, bf16[8,128,256]{2,1,0:T(8,128)(2,1)}, u32[]{:S(2)}, u32[]{:S(2)}) collective-permute-start(bf16[8,128,256]{2,1,0:T(8,128)(2,1)S(1)} %copy_bitcast_fusion.rest_0_), channel_id=1, source_target_pairs={{0,16},{16,32},{32,48},{48,0},{1,17},{17,33},{33,49},{49,1},{2,18}... | collective-permute-start | bytes 1572872 | tf_op jit(solution)/shard_map/ppermute | solution.py:22
  156.7 6.5 %copy-start = (bf16[4096,512]{1,0:T(8,128)(2,1)S(1)}, bf16[4096,512]{1,0:T(8,128)(2,1)}, u32[]{:S(2)}) copy-start(bf16[4096,512]{1,0:T(8,128)(2,1)} %all-gather.2.cloned.1.call-done) | copy-start | bytes 12582916
  160.1 21.5 %collective-permute-start.5 = (f32[128,512]{1,0:T(8,128)S(1)}, f32[128,512]{1,0:T(8,128)S(1)}, u32[]{:S(2)}, u32[]{:S(2)}) collective-permute-start(f32[128,512]{1,0:T(8,128)S(1)} %fusion.2), channel_id=1, source_target_pairs={{0,16},{16,0},{32,48},{48,32},{1,17},{17,1},{33,49},{49,33},{2,18}... | collective-permute-start | bytes 786440 | tf_op jit(solution)/shard_map/ppermute | solution.py:335
  165.2 20.9 %collective-permute-start.3 = (f32[128,512]{1,0:T(8,128)S(1)}, f32[128,512]{1,0:T(8,128)}, u32[]{:S(2)}, u32[]{:S(2)}) collective-permute-start(f32[128,512]{1,0:T(8,128)S(1)} %fusion.1), channel_id=1, source_target_pairs={{0,16},{16,0},{32,48},{48,32},{1,17},{17,1},{33,49},{49,33},{2,18}... | collective-permute-start | bytes 786440 | tf_op jit(solution)/shard_map/ppermute | solution.py:335
  170.1 16.0 %copy-start.7 = (bf16[8,128,256]{2,1,0:T(8,128)(2,1)}, bf16[8,128,256]{2,1,0:T(8,128)(2,1)S(1)}, u32[]{:S(2)}) copy-start(bf16[8,128,256]{2,1,0:T(8,128)(2,1)S(1)} %collective-permute-done.10.rest_2_) | copy-start | bytes 1572868
  181.6 4.5 %copy-start.9 = (f32[128,512]{1,0:T(8,128)}, f32[128,512]{1,0:T(8,128)S(1)}, u32[]{:S(2)}) copy-start(f32[128,512]{1,0:T(8,128)S(1)} %collective-permute-done.5.far) | copy-start | bytes 786436
Sparse Core Ops, SparseCore 0:
  41.8 77.0 all-gather.1

commit v6 on v5

--- a/solution.py
+++ b/solution.py
@@ -31,11 +31,16 @@
     return values * lax.rsqrt(mean_square + norm_epsilon) * gain
 
 
+def near_core(*arrays):
+    return [pltpu.with_memory_space_constraint(array, pltpu.VMEM) for array in arrays]
+
+
 def whole(shape):
     return pl.BlockSpec(shape, lambda *_: (0,) * len(shape))
 
 
 scalar = pl.BlockSpec(memory_space=pltpu.SMEM)
+resident = pl.BlockSpec(memory_space=pltpu.VMEM)
 
 
 def half_kernel(x, z, choice, states, gain, *rest):
@@ -138,7 +143,7 @@
     )(vision)
 
 
-def partial_kernel(spot, here, there, *rest):
+def partial_kernel(here, there, *rest):
     *weights, out = rest
     z, _, yl, tokens, width = out.shape
     x = len(weights)
@@ -146,7 +151,7 @@
     for c, part in enumerate((here, there)):
         product = jnp.zeros((part.shape[0], width), jnp.float32)
         for k, weight in enumerate(weights):
-            start = pl.multiple_of(lax.rem(spot[0] + x - k, x) * span, span)
+            start = pl.multiple_of(lax.rem(lax.axis_index("x") + x - k, x) * span, span)
             product += jnp.dot(
                 part[:, pl.ds(start, span)], weight[...], preferred_element_type=jnp.float32
             )
@@ -156,28 +161,27 @@
                 out[k, c, a] = product[row : row + tokens]
 
 
-def partial_sums(here, there, spot, weights, width, z, yl, tokens):
+def partial_sums(here, there, weights, width, z, yl, tokens):
     shape = (z, 2, yl, tokens, width)
     return pl.pallas_call(
         partial_kernel,
         in_specs=[
-            scalar,
-            whole(here.shape),
-            whole(there.shape),
+            resident,
+            resident,
             *(whole((w.shape[0], width)) for w in weights),
         ],
         out_specs=whole(shape),
         grid=(1,),
         out_shape=jax.ShapeDtypeStruct(shape, jnp.float32),
         name="partial_sums",
-    )(spot, here, there, *weights)
-
-
-def pair_kernel(odd, parts, k_gain, out):
+    )(*near_core(here, there), *weights)
+
+
+def pair_kernel(parts, k_gain, out):
     sources, cores, yl, tokens, width = parts.shape
     head = width // 2
     copies = out.shape[0]
-    swap = odd[0] != 0
+    swap = lax.axis_index("co") != 0
     total = parts[0]
     for s in range(1, sources):
         total = total + parts[s]
@@ -196,21 +200,21 @@
                 out[c, 2 * a + 1, :, lanes] = odd_core
 
 
-def pairs_of(odd, parts, k_gain, copies):
+def pairs_of(parts, k_gain, copies):
     _, cores, yl, tokens, width = parts.shape
     shape = (copies, cores * yl, tokens, width)
     return pl.pallas_call(
         pair_kernel,
-        in_specs=[scalar, whole(parts.shape), whole(k_gain.shape)],
+        in_specs=[resident, whole(k_gain.shape)],
         out_specs=whole(shape),
         grid=(1,),
         out_shape=jax.ShapeDtypeStruct(shape, jnp.bfloat16),
         name="key_value_pairs",
-    )(odd, parts, k_gain)
+    )(*near_core(parts), k_gain)
 
 
 def attention_kernel(
-    core, owners, counts, gate, query, near, far, q_gain, *rest
+    owners, counts, gate, query, near, far, q_gain, *rest
 ):
     *pieces, out = rest
     block = pl.program_id(0)
@@ -225,7 +229,7 @@
     first = block * rows
     inside = lax.rem(first, span)
     at = pl.ds(pl.multiple_of(inside, rows), rows)
-    total = query[...] + jnp.where(first // span == core[0], near[at, :], far[at, :])
+    total = query[...] + jnp.where(first // span == lax.axis_index("co"), near[at, :], far[at, :])
     parts = []
     for h in range(heads):
         parts.append(head_norm(total[:, h * head : (h + 1) * head], gain).astype(jnp.bfloat16))
@@ -265,7 +269,7 @@
         out[:, h * head : (h + 1) * head] = attended[h * rows : (h + 1) * rows]
 
 
-def attention(core, owners, counts, gate_value, query, near, far, q_gain, pieces):
+def attention(owners, counts, gate_value, query, near, far, q_gain, pieces):
     blocks = owners.shape[0]
     tokens, width = query.shape
     rows = tokens // blocks
@@ -273,17 +277,17 @@
         attention_kernel,
         grid=(blocks,),
         in_specs=[
-            *(scalar,) * 4,
+            *(scalar,) * 3,
             pl.BlockSpec((rows, width), lambda b: (b, 0)),
-            whole(near.shape),
-            whole(far.shape),
+            resident,
+            resident,
             whole(q_gain.shape),
-            *(whole(p.shape) for p in pieces),
+            *(resident for _ in pieces),
         ],
         out_specs=pl.BlockSpec((rows, width), lambda b: (b, 0)),
         out_shape=jax.ShapeDtypeStruct((tokens, width), jnp.bfloat16),
         name="attention",
-    )(core, owners, counts, gate_value, query, near, far, q_gain, *pieces)
+    )(owners, counts, gate_value, query, *near_core(near, far), q_gain, *near_core(*pieces))
 
 
 def on_device(
@@ -345,7 +349,6 @@
     partial = partial_sums(
         here.reshape(yl * z * tokens, width // z),
         there.reshape(yl * z * tokens, width // z),
-        place.astype(jnp.int32)[None],
         pair_weight,
         2 * head,
         z,
@@ -353,8 +356,7 @@
         tokens,
     )
     parts = exchange(partial, "z")
-    odd = lax.axis_index("co").astype(jnp.int32)[None]
-    pair = pairs_of(odd, parts, k_gain[None], z * yh)
+    pair = pairs_of(parts, k_gain[None], z * yh)
     own = exchange(pair, ("z", "yh"))
     own = own.transpose(1, 0, 2, 3).reshape(yl * co, z * yh * tokens, 2 * head)
     pieces = [own, *(shift(own, "x", k) for k in range(1, x))]
@@ -365,7 +367,6 @@
     back_far = partner(guest_far)
     query = jnp.dot(text_half, q_half, preferred_element_type=jnp.float32)
     return attention(
-        core.astype(jnp.int32)[None],
         owners,
         counts,
         gate,

time: 201 us -> 198 us (0.985)
  no operation moved by 1% of the time
where the time goes in v6:
time: 198 us; the launch traced here: 197 us
  waiting for transfers between devices  68.4 us (35%)
  starting transfers between devices  52.7 us (27%)
  blocking collectives  28 us (14%)
  Pallas kernels  23.8 us (12%)
  between operations  14.3 us (7%)
  matrix products  6.19 us (3%)
  other arithmetic  3.38 us (2%)
    ppermute x9, starting transfers between devices, shift(): lax.ppermute(array, axis, [(i, (i + step) % size) for i in range(size)])  32.2 us
    ppermute x9, waiting for transfers between devices, shift(): lax.ppermute(array, axis, [(i, (i + step) % size) for i in range(size)])  31.1 us
    all_to_all x1, blocking collectives, exchange(): return lax.all_to_all(array, axes, 0, 0, tiled=True)  28 us
    all_to_all x2, waiting for transfers between devices, exchange(): return lax.all_to_all(array, axes, 0, 0, tiled=True)  26.2 us
    ppermute x3, waiting for transfers between devices, partner(): return lax.ppermute(array, 'x', [(i, i ^ 1) for i in range(x)])  11.1 us
    all_to_all x2, starting transfers between devices, exchange(): return lax.all_to_all(array, axes, 0, 0, tiled=True)  11.1 us
    pallas_call x2, Pallas kernels, half_rows(): pl.pallas_call(functools.partial(half_kernel, x, z), grid_spec=pltpu.Pref...  9.84 us
    ppermute x3, starting transfers between devices, partner(): return lax.ppermute(array, 'x', [(i, i ^ 1) for i in range(x)])  9.37 us
  transfers between devices with their start and end apart: 15, of which 10 were waited for; matrix products, arithmetic and copies ran while one was open for 4% of the time, Pallas kernels for 8%

profile of v6, /device:TPU:80, one launch (start us, length us, event | category | flops | bytes accessed | tf_op | source)
XLA Modules:
  0.0 197.5 jit_solution(3696463928955328470)
XLA Ops:
  6.5 0.0 all-gather.2.cloned.1.call-start
  6.5 1.6 join.1
  8.2 5.9 %collective-permute-start = (bf16[128,768]{1,0:T(8,128)(2,1)}, bf16[128,768]{1,0:T(8,128)(2,1)S(1)}, u32[]{:S(2)}, u32[]{:S(2)}) collective-permute-start(bf16[128,768]{1,0:T(8,128)(2,1)} %join.1), channel_id=1, source_target_pairs={{0,1},{1,0},{2,3},{3,2},{4,5},{5,4},{6,7},{7,6},{8,9},{9,8},{10,11... | collective-permute-start | bytes 589832 | tf_op jit(solution)/shard_map/ppermute | solution.py:22
  14.1 11.0 %collective-permute-done = bf16[128,768]{1,0:T(8,128)(2,1)S(1)} collective-permute-done((bf16[128,768]{1,0:T(8,128)(2,1)}, bf16[128,768]{1,0:T(8,128)(2,1)S(1)}, u32[]{:S(2)}, u32[]{:S(2)}) %collective-permute-start) | collective-permute-done | bytes 196640 | tf_op jit(solution)/shard_map/ppermute | solution.py:22
  25.1 1.1 maximum_select_fusion.1.rest_0_
  26.2 0.0 copy-start.1
  26.2 4.9 %collective-permute-start.1 = (bf16[256,768]{1,0:T(8,128)(2,1)S(1)}, bf16[256,768]{1,0:T(8,128)(2,1)S(1)}, u32[]{:S(2)}, u32[]{:S(2)}) collective-permute-start(bf16[256,768]{1,0:T(8,128)(2,1)S(1)} %maximum_select_fusion.1.rest_0_), channel_id=1, source_target_pairs={{0,32},{16,48},{32,0},{48,16},{1,33},{17,49},{33,1},{49,17},{2,34}... | collective-permute-start | bytes 1179656 | tf_op jit(solution)/shard_map/ppermute | solution.py:22
  31.2 9.4 %collective-permute-done.1.rest_2_ = bf16[256,768]{1,0:T(8,128)(2,1)S(1)} collective-permute-done((bf16[256,768]{1,0:T(8,128)(2,1)S(1)}, bf16[256,768]{1,0:T(8,128)(2,1)S(1)}, u32[]{:S(2)}, u32[]{:S(2)}) %collective-permute-start.1) | collective-permute-done | bytes 393248 | tf_op jit(solution)/shard_map/ppermute | solution.py:22
  40.6 0.0 copy-start.3
  40.6 1.0 maximum_select_fusion
  41.6 0.0 all-gather.2.cloned.1.call-update
  41.6 1.7 columns.1
  43.3 28.0 %all_to_all.15 = bf16[32,8,1024]{2,1,0:T(8,128)(2,1)S(1)} all-to-all(bf16[32,8,1024]{2,1,0:T(8,128)(2,1)} %bitcast.23), channel_id=1, replica_groups=mesh['yl'=4,'co'=2,'x'=4,'z'=8,'yh'=2] {'yl','z'}, dimensions={0} | all-to-all | bytes 1048576 | tf_op jit(solution)/shard_map/all_to_all | solution.py:26
  71.3 1.9 collective-permute-start.6
  73.2 3.4 %collective-permute-start.7 = (bf16[256,256]{1,0:T(8,128)(2,1)S(1)}, bf16[256,256]{1,0:T(8,128)(2,1)S(1)}, u32[]{:S(2)}, u32[]{:S(2)}) collective-permute-start(bf16[256,256]{1,0:T(8,128)(2,1)S(1)} %slice.14), channel_id=1, source_target_pairs={{0,16},{16,32},{32,48},{48,0},{1,17},{17,33},{33,49},{49,1},{2,18}... | collective-permute-start | bytes 393224 | tf_op jit(solution)/shard_map/ppermute | solution.py:22
  76.7 3.7 %collective-permute-start.8 = (bf16[256,256]{1,0:T(8,128)(2,1)S(1)}, bf16[256,256]{1,0:T(8,128)(2,1)S(1)}, u32[]{:S(2)}, u32[]{:S(2)}) collective-permute-start(bf16[256,256]{1,0:T(8,128)(2,1)S(1)} %slice.14), channel_id=1, source_target_pairs={{0,48},{16,0},{32,16},{48,32},{1,49},{17,1},{33,17},{49,33},{2,50}... | collective-permute-start | bytes 393224 | tf_op jit(solution)/shard_map/ppermute | solution.py:22
  80.3 1.9 collective-permute-done.7.rest_1_
  82.3 0.0 copy-start.4
  82.3 1.9 collective-permute-done.8.rest_3_
  84.2 0.0 copy-start.5
  84.2 0.0 collective-permute-done.6
  84.2 0.0 copy-done.1
  84.2 0.0 copy-done.3
  84.2 0.0 copy-done.4
  84.2 0.6 copy-done.5
  84.8 2.4 %partial_sums.1 = f32[8,2,4,8,256]{4,3,2,1,0:T(8,128)} custom-call(bf16[256,1024]{1,0:T(8,128)(2,1)S(1)} %bitcast.21, bf16[256,1024]{1,0:T(8,128)(2,1)S(1)} %bitcast.22, bf16[256,768]{1,0:T(8,128)(2,1)} %copy-done.1, bf16[256,256]{1,0:T(8,128)(2,1)} %copy-done.4, bf16[256,768]{1,0:T(8,128)(2,1)} %copy-done.3, bf16[256,256]{1,0:T(8,128)(2,1)} %copy-done.5), custom_call_target="tpu_custom_call" | custom-call | tf_op jit(solution)/shard_map/partial_sums/pallas_call | solution.py:166
  87.2 4.5 %all-to-all-start.1 = ((f32[8,2,4,8,256]{4,3,2,1,0:T(8,128)}), f32[8,2,4,8,256]{4,3,2,1,0:T(8,128)S(1)}, u32[]{:S(2)}, u32[]{:S(2)}) async-start(f32[8,2,4,8,256]{4,3,2,1,0:T(8,128)} %partial_sums.1), calls=%async_computation.1 | async-start | bytes 1048576 | tf_op jit(solution)/shard_map/all_to_all | solution.py:26
  91.8 0.6 pad_add_fusion.1.choice
  92.3 5.0 %half_rows.2 = (bf16[256,4096]{1,0:T(8,128)(2,1)}, bf16[128,4096]{1,0:T(8,128)(2,1)}) custom-call(s32[2]{0:T(128)} %pad_add_fusion.1.choice, bf16[256,8192]{1,0:T(8,128)(2,1)} %states.3, f32[1,8192]{1,0:T(1,128)} %bitcast.24, f32[1,8192]{1,0:T(1,128)} %bitcast.25), custom_call_target="tpu_custom_call" | custom-call | tf_op jit(solution)/shard_map/half_rows/pallas_call | solution.py:84
  97.4 3.4 %collective-permute-start.2 = (bf16[128,4096]{1,0:T(8,128)(2,1)}, bf16[128,4096]{1,0:T(8,128)(2,1)S(1)}, u32[]{:S(2)}, u32[]{:S(2)}) collective-permute-start(bf16[128,4096]{1,0:T(8,128)(2,1)} %get-tuple-element.8), channel_id=1, source_target_pairs={{0,16},{16,0},{32,48},{48,32},{1,17},{17,1},{33,49},{49,33},{2,18}... | collective-permute-start | bytes 3145736 | tf_op jit(solution)/shard_map/ppermute | solution.py:339
  100.8 13.6 %all-to-all-done.1.parts = f32[8,2,4,8,256]{4,3,2,1,0:T(8,128)S(1)} async-done(((f32[8,2,4,8,256]{4,3,2,1,0:T(8,128)}), f32[8,2,4,8,256]{4,3,2,1,0:T(8,128)S(1)}, u32[]{:S(2)}, u32[]{:S(2)}) %all-to-all-start.1) | async-done | bytes 524320 | tf_op jit(solution)/shard_map/all_to_all | solution.py:26
  114.4 1.6 key_value_pairs.1
  116.0 6.6 %all-to-all-start.2 = ((bf16[16,8,8,256]{3,2,1,0:T(8,128)(2,1)}), bf16[16,8,8,256]{3,2,1,0:T(8,128)(2,1)S(1)}, u32[]{:S(2)}, u32[]{:S(2)}) async-start(bf16[16,8,8,256]{3,2,1,0:T(8,128)(2,1)} %key_value_pairs.1), calls=%async_computation.2 | async-start | bytes 1048576 | tf_op jit(solution)/shard_map/all_to_all | solution.py:26
  122.6 1.1 collective-permute-done.2
  123.7 1.9 collective-permute-start.4
  126.3 0.7 pad_add_fusion.choice
  127.0 4.8 %half_rows.3 = bf16[256,4096]{1,0:T(8,128)(2,1)} custom-call(s32[2]{0:T(128)} %pad_add_fusion.choice, bf16[256,8192]{1,0:T(8,128)(2,1)} %states.3, f32[1,8192]{1,0:T(1,128)} %bitcast.26, bf16[256,4096]{1,0:T(8,128)(2,1)} %get-tuple-element.7.rest_0_), custom_call_target="tpu_custom_call", output_to_operand_aliasing={{}: (3, {})} | custom-call | tf_op jit(solution)/shard_map/half_rows/pallas_call | solution.py:84
  131.8 12.5 %all-to-all-done.2 = bf16[16,8,8,256]{3,2,1,0:T(8,128)(2,1)S(1)} async-done(((bf16[16,8,8,256]{3,2,1,0:T(8,128)(2,1)}), bf16[16,8,8,256]{3,2,1,0:T(8,128)(2,1)S(1)}, u32[]{:S(2)}, u32[]{:S(2)}) %all-to-all-start.2) | async-done | bytes 524320 | tf_op jit(solution)/shard_map/all_to_all | solution.py:26
  144.4 4.7 %collective-permute-start.10 = (bf16[8,128,256]{2,1,0:T(8,128)(2,1)S(1)}, bf16[8,128,256]{2,1,0:T(8,128)(2,1)S(1)}, u32[]{:S(2)}, u32[]{:S(2)}) collective-permute-start(bf16[8,128,256]{2,1,0:T(8,128)(2,1)S(1)} %copy_bitcast_fusion.rest_0_), channel_id=1, source_target_pairs={{0,32},{16,48},{32,0},{48,16},{1,33},{17,49},{33,1},{49,17},{2,34}... | collective-permute-start | bytes 1572872 | tf_op jit(solution)/shard_map/ppermute | solution.py:22
  149.1 3.2 %collective-permute-start.11 = (bf16[8,128,256]{2,1,0:T(8,128)(2,1)S(1)}, bf16[8,128,256]{2,1,0:T(8,128)(2,1)S(1)}, u32[]{:S(2)}, u32[]{:S(2)}) collective-permute-start(bf16[8,128,256]{2,1,0:T(8,128)(2,1)S(1)} %copy_bitcast_fusion.rest_0_), channel_id=1, source_target_pairs={{0,48},{16,0},{32,16},{48,32},{1,49},{17,1},{33,17},{49,33},{2,50}... | collective-permute-start | bytes 1572872 | tf_op jit(solution)/shard_map/ppermute | solution.py:22
  152.2 2.7 %collective-permute-start.9 = (bf16[8,128,256]{2,1,0:T(8,128)(2,1)S(1)}, bf16[8,128,256]{2,1,0:T(8,128)(2,1)S(1)}, u32[]{:S(2)}, u32[]{:S(2)}) collective-permute-start(bf16[8,128,256]{2,1,0:T(8,128)(2,1)S(1)} %copy_bitcast_fusion.rest_0_), channel_id=1, source_target_pairs={{0,16},{16,32},{32,48},{48,0},{1,17},{17,33},{33,49},{49,1},{2,18}... | collective-permute-start | bytes 1572872 | tf_op jit(solution)/shard_map/ppermute | solution.py:22
  154.9 0.0 collective-permute-done.4
  154.9 0.0 all-gather.2.cloned.1.call-done
  155.0 0.0 copy-start
  155.0 0.0 copy-start.2
  155.0 3.4 %fusion.2 = f32[128,512]{1,0:T(8,128)S(1)} fusion(bf16[128,4096]{1,0:T(8,128)(2,1)} %collective-permute-done.4, bf16[4096,512]{1,0:T(8,128)(2,1)} %all-gather.2.cloned.1.call-done), kind=kOutput, calls=%fused_computation.7 | convolution fusion | flops 536870912 | bytes 5505024 | tf_op jit(solution)/shard_map/dot_general | solution.py:365
  158.4 3.1 %collective-permute-start.5 = (f32[128,512]{1,0:T(8,128)S(1)}, f32[128,512]{1,0:T(8,128)S(1)}, u32[]{:S(2)}, u32[]{:S(2)}) collective-permute-start(f32[128,512]{1,0:T(8,128)S(1)} %fusion.2), channel_id=1, source_target_pairs={{0,16},{16,0},{32,48},{48,32},{1,17},{17,1},{33,49},{49,33},{2,18}... | collective-permute-start | bytes 786440 | tf_op jit(solution)/shard_map/ppermute | solution.py:339
  161.4 0.0 copy-done
  161.4 0.8 fusion.1
  162.2 2.9 %collective-permute-start.3 = (f32[128,512]{1,0:T(8,128)S(1)}, f32[128,512]{1,0:T(8,128)S(1)}, u32[]{:S(2)}, u32[]{:S(2)}) collective-permute-start(f32[128,512]{1,0:T(8,128)S(1)} %fusion.1), channel_id=1, source_target_pairs={{0,16},{16,0},{32,48},{48,32},{1,17},{17,1},{33,49},{49,33},{2,18}... | collective-permute-start | bytes 786440 | tf_op jit(solution)/shard_map/ppermute | solution.py:339
  165.2 0.0 copy-done.2
  165.2 2.0 %fusion.query = f32[256,512]{1,0:T(8,128)} fusion(bf16[256,4096]{1,0:T(8,128)(2,1)S(1)} %copy-done.2, bf16[4096,512]{1,0:T(8,128)(2,1)S(1)} %copy-done), kind=kOutput, calls=%fused_computation.5 | convolution fusion | flops 1073741824 | bytes 6815744 | tf_op jit(solution)/shard_map/dot_general | solution.py:368
  167.2 0.0 collective-permute-done.10.rest_2_
  167.2 6.9 %collective-permute-done.11.rest_3_ = bf16[8,128,256]{2,1,0:T(8,128)(2,1)S(1)} collective-permute-done((bf16[8,128,256]{2,1,0:T(8,128)(2,1)S(1)}, bf16[8,128,256]{2,1,0:T(8,128)(2,1)S(1)}, u32[]{:S(2)}, u32[]{:S(2)}) %collective-permute-start.11) | collective-permute-done | bytes 524320 | tf_op jit(solution)/shard_map/ppermute | solution.py:22
  174.1 0.0 collective-permute-done.9.rest_1_
  174.1 5.6 %collective-permute-done.5.far = f32[128,512]{1,0:T(8,128)S(1)} collective-permute-done((f32[128,512]{1,0:T(8,128)S(1)}, f32[128,512]{1,0:T(8,128)S(1)}, u32[]{:S(2)}, u32[]{:S(2)}) %collective-permute-start.5) | collective-permute-done | bytes 262176 | tf_op jit(solution)/shard_map/ppermute | solution.py:339
  179.7 4.4 %collective-permute-done.3.near = f32[128,512]{1,0:T(8,128)S(1)} collective-permute-done((f32[128,512]{1,0:T(8,128)S(1)}, f32[128,512]{1,0:T(8,128)S(1)}, u32[]{:S(2)}, u32[]{:S(2)}) %collective-permute-start.3) | collective-permute-done | bytes 262176 | tf_op jit(solution)/shard_map/ppermute | solution.py:339
  184.1 6.5 %attention.1 = bf16[256,512]{1,0:T(8,128)(2,1)} custom-call(s32[4,4]{1,0:T(4,128)} %owners.1, s32[4]{0:T(128)} %counts.1, f32[1]{0:T(128)S(6)} %tanh.3.gate, f32[256,512]{1,0:T(8,128)} %fusion.query, f32[128,512]{1,0:T(8,128)S(1)} %collective-permute-done.3.near, f32[128,512]{1,0:T(8,128)S(1)} %collective-permute-done.5.far, f32[1,128]{1,0:T(1,128)} %bitcast.29, ...), custom_call_target="tpu_custom_call" | custom-call | tf_op jit(solution)/shard_map/attention/pallas_call | solution.py:276
  (4 shorter events, 0.1 us)
Async XLA Ops:
  6.5 148.4 %all-gather.2.cloned.1.call-start = ((), (), s32[]{:S(2)}) async-start(), calls=%async_computation.3 | async-start | bytes 4718592 | tf_op jit(solution)/shard_map/all_gather | solution.py:328
  8.2 16.9 %collective-permute-start = (bf16[128,768]{1,0:T(8,128)(2,1)}, bf16[128,768]{1,0:T(8,128)(2,1)S(1)}, u32[]{:S(2)}, u32[]{:S(2)}) collective-permute-start(bf16[128,768]{1,0:T(8,128)(2,1)} %join.1), channel_id=1, source_target_pairs={{0,1},{1,0},{2,3},{3,2},{4,5},{5,4},{6,7},{7,6},{8,9},{9,8},{10,11... | collective-permute-start | bytes 589832 | tf_op jit(solution)/shard_map/ppermute | solution.py:22
  26.2 58.0 %copy-start.1 = (bf16[256,768]{1,0:T(8,128)(2,1)}, bf16[256,768]{1,0:T(8,128)(2,1)S(1)}, u32[]{:S(2)}) copy-start(bf16[256,768]{1,0:T(8,128)(2,1)S(1)} %maximum_select_fusion.1.rest_0_) | copy-start | bytes 1179652
  26.2 14.3 %collective-permute-start.1 = (bf16[256,768]{1,0:T(8,128)(2,1)S(1)}, bf16[256,768]{1,0:T(8,128)(2,1)S(1)}, u32[]{:S(2)}, u32[]{:S(2)}) collective-permute-start(bf16[256,768]{1,0:T(8,128)(2,1)S(1)} %maximum_select_fusion.1.rest_0_), channel_id=1, source_target_pairs={{0,32},{16,48},{32,0},{48,16},{1,33},{17,49},{33,1},{49,17},{2,34}... | collective-permute-start | bytes 1179656 | tf_op jit(solution)/shard_map/ppermute | solution.py:22
  40.6 43.6 %copy-start.3 = (bf16[256,768]{1,0:T(8,128)(2,1)}, bf16[256,768]{1,0:T(8,128)(2,1)S(1)}, u32[]{:S(2)}) copy-start(bf16[256,768]{1,0:T(8,128)(2,1)S(1)} %collective-permute-done.1.rest_2_) | copy-start | bytes 1179652
  71.3 12.9 %collective-permute-start.6 = (bf16[32,8,1024]{2,1,0:T(8,128)(2,1)S(1)}, bf16[32,8,1024]{2,1,0:T(8,128)(2,1)S(1)}, u32[]{:S(2)}, u32[]{:S(2)}) collective-permute-start(bf16[32,8,1024]{2,1,0:T(8,128)(2,1)S(1)} %all_to_all.15), channel_id=1, source_target_pairs={{0,64},{64,0},{1,65},{65,1},{2,66},{66,2},{3,67},{67,3},{4,68},{68... | collective-permute-start | bytes 1572872 | tf_op jit(solution)/shard_map/ppermute | solution.py:22
  73.2 9.0 %collective-permute-start.7 = (bf16[256,256]{1,0:T(8,128)(2,1)S(1)}, bf16[256,256]{1,0:T(8,128)(2,1)S(1)}, u32[]{:S(2)}, u32[]{:S(2)}) collective-permute-start(bf16[256,256]{1,0:T(8,128)(2,1)S(1)} %slice.14), channel_id=1, source_target_pairs={{0,16},{16,32},{32,48},{48,0},{1,17},{17,33},{33,49},{49,1},{2,18}... | collective-permute-start | bytes 393224 | tf_op jit(solution)/shard_map/ppermute | solution.py:22
  76.7 7.5 %collective-permute-start.8 = (bf16[256,256]{1,0:T(8,128)(2,1)S(1)}, bf16[256,256]{1,0:T(8,128)(2,1)S(1)}, u32[]{:S(2)}, u32[]{:S(2)}) collective-permute-start(bf16[256,256]{1,0:T(8,128)(2,1)S(1)} %slice.14), channel_id=1, source_target_pairs={{0,48},{16,0},{32,16},{48,32},{1,49},{17,1},{33,17},{49,33},{2,50}... | collective-permute-start | bytes 393224 | tf_op jit(solution)/shard_map/ppermute | solution.py:22
  82.3 1.9 copy-start.4
  84.2 0.7 copy-start.5
  87.2 27.2 %all-to-all-start.1 = ((f32[8,2,4,8,256]{4,3,2,1,0:T(8,128)}), f32[8,2,4,8,256]{4,3,2,1,0:T(8,128)S(1)}, u32[]{:S(2)}, u32[]{:S(2)}) async-start(f32[8,2,4,8,256]{4,3,2,1,0:T(8,128)} %partial_sums.1), calls=%async_computation.1 | async-start | bytes 1048576 | tf_op jit(solution)/shard_map/all_to_all | solution.py:26
  97.4 26.4 %collective-permute-start.2 = (bf16[128,4096]{1,0:T(8,128)(2,1)}, bf16[128,4096]{1,0:T(8,128)(2,1)S(1)}, u32[]{:S(2)}, u32[]{:S(2)}) collective-permute-start(bf16[128,4096]{1,0:T(8,128)(2,1)} %get-tuple-element.8), channel_id=1, source_target_pairs={{0,16},{16,0},{32,48},{48,32},{1,17},{17,1},{33,49},{49,33},{2,18}... | collective-permute-start | bytes 3145736 | tf_op jit(solution)/shard_map/ppermute | solution.py:339
  116.0 28.3 %all-to-all-start.2 = ((bf16[16,8,8,256]{3,2,1,0:T(8,128)(2,1)}), bf16[16,8,8,256]{3,2,1,0:T(8,128)(2,1)S(1)}, u32[]{:S(2)}, u32[]{:S(2)}) async-start(bf16[16,8,8,256]{3,2,1,0:T(8,128)(2,1)} %key_value_pairs.1), calls=%async_computation.2 | async-start | bytes 1048576 | tf_op jit(solution)/shard_map/all_to_all | solution.py:26
  123.7 31.2 %collective-permute-start.4 = (bf16[128,4096]{1,0:T(8,128)(2,1)S(1)}, bf16[128,4096]{1,0:T(8,128)(2,1)}, u32[]{:S(2)}, u32[]{:S(2)}) collective-permute-start(bf16[128,4096]{1,0:T(8,128)(2,1)S(1)} %collective-permute-done.2), channel_id=1, source_target_pairs={{0,64},{64,0},{1,65},{65,1},{2,66},{66,2},{3,67},{67,3},{4,68},{68... | collective-permute-start | bytes 3145736 | tf_op jit(solution)/shard_map/ppermute | solution.py:22
  144.4 22.8 %collective-permute-start.10 = (bf16[8,128,256]{2,1,0:T(8,128)(2,1)S(1)}, bf16[8,128,256]{2,1,0:T(8,128)(2,1)S(1)}, u32[]{:S(2)}, u32[]{:S(2)}) collective-permute-start(bf16[8,128,256]{2,1,0:T(8,128)(2,1)S(1)} %copy_bitcast_fusion.rest_0_), channel_id=1, source_target_pairs={{0,32},{16,48},{32,0},{48,16},{1,33},{17,49},{33,1},{49,17},{2,34}... | collective-permute-start | bytes 1572872 | tf_op jit(solution)/shard_map/ppermute | solution.py:22
  149.1 25.0 %collective-permute-start.11 = (bf16[8,128,256]{2,1,0:T(8,128)(2,1)S(1)}, bf16[8,128,256]{2,1,0:T(8,128)(2,1)S(1)}, u32[]{:S(2)}, u32[]{:S(2)}) collective-permute-start(bf16[8,128,256]{2,1,0:T(8,128)(2,1)S(1)} %copy_bitcast_fusion.rest_0_), channel_id=1, source_target_pairs={{0,48},{16,0},{32,16},{48,32},{1,49},{17,1},{33,17},{49,33},{2,50}... | collective-permute-start | bytes 1572872 | tf_op jit(solution)/shard_map/ppermute | solution.py:22
  152.2 21.9 %collective-permute-start.9 = (bf16[8,128,256]{2,1,0:T(8,128)(2,1)S(1)}, bf16[8,128,256]{2,1,0:T(8,128)(2,1)S(1)}, u32[]{:S(2)}, u32[]{:S(2)}) collective-permute-start(bf16[8,128,256]{2,1,0:T(8,128)(2,1)S(1)} %copy_bitcast_fusion.rest_0_), channel_id=1, source_target_pairs={{0,16},{16,32},{32,48},{48,0},{1,17},{17,33},{33,49},{49,1},{2,18}... | collective-permute-start | bytes 1572872 | tf_op jit(solution)/shard_map/ppermute | solution.py:22
  155.0 6.5 %copy-start = (bf16[4096,512]{1,0:T(8,128)(2,1)S(1)}, bf16[4096,512]{1,0:T(8,128)(2,1)}, u32[]{:S(2)}) copy-start(bf16[4096,512]{1,0:T(8,128)(2,1)} %all-gather.2.cloned.1.call-done) | copy-start | bytes 12582916
  155.0 10.2 %copy-start.2 = (bf16[256,4096]{1,0:T(8,128)(2,1)S(1)}, bf16[256,4096]{1,0:T(8,128)(2,1)}, u32[]{:S(2)}) copy-start(bf16[256,4096]{1,0:T(8,128)(2,1)} %half_rows.3) | copy-start | bytes 6291460
  158.4 21.4 %collective-permute-start.5 = (f32[128,512]{1,0:T(8,128)S(1)}, f32[128,512]{1,0:T(8,128)S(1)}, u32[]{:S(2)}, u32[]{:S(2)}) collective-permute-start(f32[128,512]{1,0:T(8,128)S(1)} %fusion.2), channel_id=1, source_target_pairs={{0,16},{16,0},{32,48},{48,32},{1,17},{17,1},{33,49},{49,33},{2,18}... | collective-permute-start | bytes 786440 | tf_op jit(solution)/shard_map/ppermute | solution.py:339
  162.2 21.9 %collective-permute-start.3 = (f32[128,512]{1,0:T(8,128)S(1)}, f32[128,512]{1,0:T(8,128)S(1)}, u32[]{:S(2)}, u32[]{:S(2)}) collective-permute-start(f32[128,512]{1,0:T(8,128)S(1)} %fusion.1), channel_id=1, source_target_pairs={{0,16},{16,0},{32,48},{48,32},{1,17},{17,1},{33,49},{49,33},{2,18}... | collective-permute-start | bytes 786440 | tf_op jit(solution)/shard_map/ppermute | solution.py:339
Sparse Core Ops, SparseCore 0:
  41.7 77.0 all-gather.1

commit v7 on v6

--- a/solution.py
+++ b/solution.py
@@ -53,20 +53,16 @@
         wide = states[:, j * depth : (j + 1) * depth].astype(jnp.float32)
         squares += wide * wide
     scale = lax.rsqrt(jnp.sum(squares, axis=-1, keepdims=True) / width + norm_epsilon)
-    even = choice[1] == 0
-    for k in range(z):
+    quarter = width // x
+    for index, out in enumerate(outs):
+        home = choice[1] if index == 0 else choice[1] + 1 - 2 * lax.rem(choice[1], 2)
         for m in range(x // 2):
-            blocks = []
-            for p in range(2):
-                start = ((2 * m + p) * z + k) * span
-                at = slice(start, start + span)
+            first = lax.rem(home + 2 * m, x) * quarter
+            for k in range(z):
+                at = pl.ds(pl.multiple_of(first + k * span, span), span)
                 wide = states[:, at].astype(jnp.float32)
-                blocks.append((wide * scale * gain[:, at]).astype(jnp.bfloat16))
-            start = (k * (x // 2) + m) * span
-            lanes = slice(start, start + span)
-            outs[0][:, lanes] = jnp.where(even, blocks[0], blocks[1])
-            if len(outs) > 1:
-                outs[1][:, lanes] = jnp.where(even, blocks[1], blocks[0])
+                start = m * quarter + k * span
+                out[:, start : start + span] = (wide * scale * gain[:, at]).astype(out.dtype)
 
 
 def half_rows(states, gain, choice, base, x, z):
@@ -324,25 +320,24 @@
     near = both[:, : 2 * head]
     pair_weight = (both, shift(near, "x", 1), far, shift(near, "x", 3))
 
-    rows_q = ordered(place < 2, both[:, 2 * head :], far[:, 2 * head :])
-    q_half = lax.all_gather(rows_q, "z", axis=0, tiled=True)
+    q_near = lax.all_gather(both[:, 2 * head :], "z", axis=0, tiled=True)
+    q_far = lax.all_gather(far[:, 2 * head :], "z", axis=0, tiled=True)
 
     columns = columns_of(vision.reshape(tokens, width), yl, x, z)
     here = exchange(columns.reshape(yl * z, tokens, width // z), ("yl", "z"))
 
     gate = jnp.tanh(gate_value)
 
-    mine = lax.rem(place, 2)
     gain = text_gain[None]
 
     def partner(array):
         return lax.ppermute(array, "x", [(i, i ^ 1) for i in range(x)])
 
-    choice = jnp.stack((core, mine)).astype(jnp.int32)
+    choice = jnp.stack((core, place)).astype(jnp.int32)
     text_half, sent = half_rows(text_states, gain, choice, None, x, z)
     guest = partner(sent)
     guest_other = shift(guest, "co", 1)
-    choice = jnp.stack((1 - core, mine)).astype(jnp.int32)
+    choice = jnp.stack((1 - core, place)).astype(jnp.int32)
     (text_half,) = half_rows(text_states, gain, choice, text_half, x, z)
 
     there = shift(here, "co", 1)
@@ -361,11 +356,21 @@
     own = own.transpose(1, 0, 2, 3).reshape(yl * co, z * yh * tokens, 2 * head)
     pieces = [own, *(shift(own, "x", k) for k in range(1, x))]
 
-    guest_near = jnp.dot(guest, q_half, preferred_element_type=jnp.float32)
-    guest_far = jnp.dot(guest_other, q_half, preferred_element_type=jnp.float32)
+    def product(left, right):
+        return jnp.dot(left, right, preferred_element_type=jnp.float32)
+
+    cut = q_near.shape[0]
+    guest_near_1 = product(guest[:, :cut], q_near)
+    guest_far_1 = product(guest_other[:, :cut], q_near)
+    query_1 = product(text_half[:, :cut], q_near)
+    guest_near_1, guest_far_1, query_1 = lax.optimization_barrier(
+        (guest_near_1, guest_far_1, query_1)
+    )
+    guest_near = guest_near_1 + product(guest[:, cut:], q_far)
+    guest_far = guest_far_1 + product(guest_other[:, cut:], q_far)
     back_near = partner(guest_near)
     back_far = partner(guest_far)
-    query = jnp.dot(text_half, q_half, preferred_element_type=jnp.float32)
+    query = query_1 + product(text_half[:, cut:], q_far)
     return attention(
         owners,
         counts,

time: 198 us -> 179 us (0.904)
  blocking collectives: 28 us -> 0 us
  starting transfers between devices: 52.7 us -> 65.4 us
  waiting for transfers between devices: 68.4 us -> 59.4 us
  matrix products: 6.19 us -> 9.52 us
    all_to_all x1 -> x0, blocking collectives: 28 us -> none  [exchange(): return lax.all_to_all(array, axes, 0, 0, tiled=True)]
    all_to_all x2 -> x3, starting transfers between devices: 11.1 us -> 24.2 us  [exchange(): return lax.all_to_all(array, axes, 0, 0, tiled=True)]
    all_to_all x2 -> x3, waiting for transfers between devices: 26.2 us -> 15.5 us  [exchange(): return lax.all_to_all(array, axes, 0, 0, tiled=True)]
    ppermute x3, waiting for transfers between devices: 11.1 us -> 17.4 us  [partner(): return lax.ppermute(array, 'x', [(i, i ^ 1) for i in range(x)])]
    ppermute x9, waiting for transfers between devices: 31.1 us -> 26.5 us  [shift(): lax.ppermute(array, axis, [(i, (i + step) % size) for i in range(size)])]
    dot_general x3 -> x6, matrix products: 6.19 us -> 9.52 us  [product(): return jnp.dot(left, right, preferred_element_type=jnp.float32)]
  transfers between devices with their start and end apart: 15 -> 17, of which waited for: 10 -> 11; matrix products, arithmetic and copies ran while one was open for 4% -> 7% of each run, Pallas kernels for 8% -> 9%
where the time goes in v7:
time: 179 us; the launch traced here: 178 us
  starting transfers between devices  65.4 us (37%)
  waiting for transfers between devices  59.4 us (33%)
  Pallas kernels  23.5 us (13%)
  between operations  14.4 us (8%)
  matrix products  9.52 us (5%)
  other arithmetic  3.33 us (2%)
  local copies, waits for them, and re-layouts  2.35 us (1%)
    ppermute x9, starting transfers between devices, shift(): lax.ppermute(array, axis, [(i, (i + step) % size) for i in range(size)])  31.7 us
    ppermute x9, waiting for transfers between devices, shift(): lax.ppermute(array, axis, [(i, (i + step) % size) for i in range(size)])  26.5 us
    all_to_all x3, starting transfers between devices, exchange(): return lax.all_to_all(array, axes, 0, 0, tiled=True)  24.2 us
    ppermute x3, waiting for transfers between devices, partner(): return lax.ppermute(array, 'x', [(i, i ^ 1) for i in range(x)])  17.4 us
    all_to_all x3, waiting for transfers between devices, exchange(): return lax.all_to_all(array, axes, 0, 0, tiled=True)  15.5 us
    pallas_call x2, Pallas kernels, half_rows(): pl.pallas_call(functools.partial(half_kernel, x, z), grid_spec=pltpu.Pref...  9.6 us
    dot_general x6, matrix products, product(): return jnp.dot(left, right, preferred_element_type=jnp.float32)  9.52 us
    ppermute x3, starting transfers between devices, partner(): return lax.ppermute(array, 'x', [(i, i ^ 1) for i in range(x)])  9.49 us
  transfers between devices with their start and end apart: 17, of which 11 were waited for; matrix products, arithmetic and copies ran while one was open for 7% of the time, Pallas kernels for 9%

profile of v7, /device:TPU:80, one launch (start us, length us, event | category | flops | bytes accessed | tf_op | source)
XLA Modules:
  0.0 177.9 jit_solution(17277166044768025804)
XLA Ops:
  6.5 0.0 all-gather.3.cloned.1.call-start
  6.5 1.6 join.1
  8.2 5.9 %collective-permute-start.1 = (bf16[128,768]{1,0:T(8,128)(2,1)}, bf16[128,768]{1,0:T(8,128)(2,1)S(1)}, u32[]{:S(2)}, u32[]{:S(2)}) collective-permute-start(bf16[128,768]{1,0:T(8,128)(2,1)} %join.1), channel_id=1, source_target_pairs={{0,1},{1,0},{2,3},{3,2},{4,5},{5,4},{6,7},{7,6},{8,9},{9,8},{10,11... | collective-permute-start | bytes 589832 | tf_op jit(solution)/shard_map/ppermute | solution.py:22
  14.1 11.0 %collective-permute-done.1 = bf16[128,768]{1,0:T(8,128)(2,1)S(1)} collective-permute-done((bf16[128,768]{1,0:T(8,128)(2,1)}, bf16[128,768]{1,0:T(8,128)(2,1)S(1)}, u32[]{:S(2)}, u32[]{:S(2)}) %collective-permute-start.1) | collective-permute-done | bytes 196640 | tf_op jit(solution)/shard_map/ppermute | solution.py:22
  25.1 1.1 maximum_select_fusion.rest_0_
  26.2 0.0 copy-start.2
  26.2 0.8 slice.37
  27.0 0.0 all-gather.3.cloned.1.call-update
  27.0 1.8 columns.1
  28.8 11.9 %all-to-all-start = ((bf16[32,8,1024]{2,1,0:T(8,128)(2,1)}), bf16[32,8,1024]{2,1,0:T(8,128)(2,1)S(1)}, u32[]{:S(2)}, u32[]{:S(2)}) async-start(bf16[32,8,1024]{2,1,0:T(8,128)(2,1)} %bitcast.23), calls=%async_computation | async-start | bytes 1048576 | tf_op jit(solution)/shard_map/all_to_all | solution.py:26
  40.7 0.0 all-gather.5.cloned.1.call-start
  40.8 4.9 %collective-permute-start.3 = (bf16[256,768]{1,0:T(8,128)(2,1)S(1)}, bf16[256,768]{1,0:T(8,128)(2,1)S(1)}, u32[]{:S(2)}, u32[]{:S(2)}) collective-permute-start(bf16[256,768]{1,0:T(8,128)(2,1)S(1)} %maximum_select_fusion.rest_0_), channel_id=1, source_target_pairs={{0,32},{16,48},{32,0},{48,16},{1,33},{17,49},{33,1},{49,17},{2,34}... | collective-permute-start | bytes 1179656 | tf_op jit(solution)/shard_map/ppermute | solution.py:22
  45.7 8.8 %collective-permute-done.3.rest_2_ = bf16[256,768]{1,0:T(8,128)(2,1)S(1)} collective-permute-done((bf16[256,768]{1,0:T(8,128)(2,1)S(1)}, bf16[256,768]{1,0:T(8,128)(2,1)S(1)}, u32[]{:S(2)}, u32[]{:S(2)}) %collective-permute-start.3) | collective-permute-done | bytes 393248 | tf_op jit(solution)/shard_map/ppermute | solution.py:22
  54.5 0.8 slice.41
  55.3 0.0 all-gather.5.cloned.1.call-update
  55.4 1.9 %all-to-all-done = bf16[32,8,1024]{2,1,0:T(8,128)(2,1)S(1)} async-done(((bf16[32,8,1024]{2,1,0:T(8,128)(2,1)}), bf16[32,8,1024]{2,1,0:T(8,128)(2,1)S(1)}, u32[]{:S(2)}, u32[]{:S(2)}) %all-to-all-start) | async-done | bytes 524320 | tf_op jit(solution)/shard_map/all_to_all | solution.py:26
  57.2 1.9 %collective-permute-start.6 = (bf16[32,8,1024]{2,1,0:T(8,128)(2,1)S(1)}, bf16[32,8,1024]{2,1,0:T(8,128)(2,1)S(1)}, u32[]{:S(2)}, u32[]{:S(2)}) collective-permute-start(bf16[32,8,1024]{2,1,0:T(8,128)(2,1)S(1)} %all-to-all-done), channel_id=1, source_target_pairs={{0,64},{64,0},{1,65},{65,1},{2,66},{66,2},{3,67},{67,3},{4,68},{68... | collective-permute-start | bytes 1572872 | tf_op jit(solution)/shard_map/ppermute | solution.py:22
  59.1 3.4 %collective-permute-start.7 = (bf16[256,256]{1,0:T(8,128)(2,1)S(1)}, bf16[256,256]{1,0:T(8,128)(2,1)S(1)}, u32[]{:S(2)}, u32[]{:S(2)}) collective-permute-start(bf16[256,256]{1,0:T(8,128)(2,1)S(1)} %slice.44), channel_id=1, source_target_pairs={{0,16},{16,32},{32,48},{48,0},{1,17},{17,33},{33,49},{49,1},{2,18}... | collective-permute-start | bytes 393224 | tf_op jit(solution)/shard_map/ppermute | solution.py:22
  62.5 3.7 %collective-permute-start.8 = (bf16[256,256]{1,0:T(8,128)(2,1)S(1)}, bf16[256,256]{1,0:T(8,128)(2,1)S(1)}, u32[]{:S(2)}, u32[]{:S(2)}) collective-permute-start(bf16[256,256]{1,0:T(8,128)(2,1)S(1)} %slice.44), channel_id=1, source_target_pairs={{0,48},{16,0},{32,16},{48,32},{1,49},{17,1},{33,17},{49,33},{2,50}... | collective-permute-start | bytes 393224 | tf_op jit(solution)/shard_map/ppermute | solution.py:22
  66.2 1.9 %collective-permute-done.7.rest_1_ = bf16[256,256]{1,0:T(8,128)(2,1)S(1)} collective-permute-done((bf16[256,256]{1,0:T(8,128)(2,1)S(1)}, bf16[256,256]{1,0:T(8,128)(2,1)S(1)}, u32[]{:S(2)}, u32[]{:S(2)}) %collective-permute-start.7) | collective-permute-done | bytes 131104 | tf_op jit(solution)/shard_map/ppermute | solution.py:22
  68.1 1.9 %collective-permute-done.8.rest_3_ = bf16[256,256]{1,0:T(8,128)(2,1)S(1)} collective-permute-done((bf16[256,256]{1,0:T(8,128)(2,1)S(1)}, bf16[256,256]{1,0:T(8,128)(2,1)S(1)}, u32[]{:S(2)}, u32[]{:S(2)}) %collective-permute-start.8) | collective-permute-done | bytes 131104 | tf_op jit(solution)/shard_map/ppermute | solution.py:22
  70.1 0.0 collective-permute-done.6
  70.1 0.0 copy-done.2
  70.1 0.0 copy-done.5
  70.1 0.0 copy-done.8
  70.1 0.6 copy-done.9
  70.7 2.4 %partial_sums.1 = f32[8,2,4,8,256]{4,3,2,1,0:T(8,128)} custom-call(bf16[256,1024]{1,0:T(8,128)(2,1)S(1)} %bitcast.21, bf16[256,1024]{1,0:T(8,128)(2,1)S(1)} %bitcast.22, bf16[256,768]{1,0:T(8,128)(2,1)} %copy-done.2, bf16[256,256]{1,0:T(8,128)(2,1)} %copy-done.8, bf16[256,768]{1,0:T(8,128)(2,1)} %copy-done.5, bf16[256,256]{1,0:T(8,128)(2,1)} %copy-done.9), custom_call_target="tpu_custom_call" | custom-call | tf_op jit(solution)/shard_map/partial_sums/pallas_call | solution.py:162
  73.1 5.4 %all-to-all-start.1 = ((f32[8,2,4,8,256]{4,3,2,1,0:T(8,128)}), f32[8,2,4,8,256]{4,3,2,1,0:T(8,128)S(1)}, u32[]{:S(2)}, u32[]{:S(2)}) async-start(f32[8,2,4,8,256]{4,3,2,1,0:T(8,128)} %partial_sums.1), calls=%async_computation.1 | async-start | bytes 1048576 | tf_op jit(solution)/shard_map/all_to_all | solution.py:26
  78.5 0.6 pad_add_fusion.choice
  79.1 4.9 %half_rows.2 = (bf16[256,4096]{1,0:T(8,128)(2,1)}, bf16[128,4096]{1,0:T(8,128)(2,1)}) custom-call(s32[2]{0:T(128)} %pad_add_fusion.choice, bf16[256,8192]{1,0:T(8,128)(2,1)} %states.3, f32[1,8192]{1,0:T(1,128)} %bitcast.24, f32[1,8192]{1,0:T(1,128)} %bitcast.25), custom_call_target="tpu_custom_call" | custom-call | tf_op jit(solution)/shard_map/half_rows/pallas_call | solution.py:80
  84.0 3.4 %collective-permute-start = (bf16[128,4096]{1,0:T(8,128)(2,1)}, bf16[128,4096]{1,0:T(8,128)(2,1)S(1)}, u32[]{:S(2)}, u32[]{:S(2)}) collective-permute-start(bf16[128,4096]{1,0:T(8,128)(2,1)} %get-tuple-element.10), channel_id=1, source_target_pairs={{0,16},{16,0},{32,48},{48,32},{1,17},{17,1},{33,49},{49,33},{2,18}... | collective-permute-start | bytes 3145736 | tf_op jit(solution)/shard_map/ppermute | solution.py:334
  87.4 6.7 %all-to-all-done.1.parts = f32[8,2,4,8,256]{4,3,2,1,0:T(8,128)S(1)} async-done(((f32[8,2,4,8,256]{4,3,2,1,0:T(8,128)}), f32[8,2,4,8,256]{4,3,2,1,0:T(8,128)S(1)}, u32[]{:S(2)}, u32[]{:S(2)}) %all-to-all-start.1) | async-done | bytes 524320 | tf_op jit(solution)/shard_map/all_to_all | solution.py:26
  94.2 1.6 key_value_pairs.1
  95.8 6.9 %all-to-all-start.2 = ((bf16[16,8,8,256]{3,2,1,0:T(8,128)(2,1)}), bf16[16,8,8,256]{3,2,1,0:T(8,128)(2,1)S(1)}, u32[]{:S(2)}, u32[]{:S(2)}) async-start(bf16[16,8,8,256]{3,2,1,0:T(8,128)(2,1)} %key_value_pairs.1), calls=%async_computation.2 | async-start | bytes 1048576 | tf_op jit(solution)/shard_map/all_to_all | solution.py:26
  102.7 7.4 %collective-permute-done = bf16[128,4096]{1,0:T(8,128)(2,1)S(1)} collective-permute-done((bf16[128,4096]{1,0:T(8,128)(2,1)}, bf16[128,4096]{1,0:T(8,128)(2,1)S(1)}, u32[]{:S(2)}, u32[]{:S(2)}) %collective-permute-start) | collective-permute-done | bytes 1048608 | tf_op jit(solution)/shard_map/ppermute | solution.py:334
  110.1 1.9 %collective-permute-start.2 = (bf16[128,4096]{1,0:T(8,128)(2,1)S(1)}, bf16[128,4096]{1,0:T(8,128)(2,1)}, u32[]{:S(2)}, u32[]{:S(2)}) collective-permute-start(bf16[128,4096]{1,0:T(8,128)(2,1)S(1)} %collective-permute-done), channel_id=1, source_target_pairs={{0,64},{64,0},{1,65},{65,1},{2,66},{66,2},{3,67},{67,3},{4,68},{68... | collective-permute-start | bytes 3145736 | tf_op jit(solution)/shard_map/ppermute | solution.py:22
  112.7 0.7 pad_add_fusion.1.choice
  113.4 4.7 %half_rows.3 = bf16[256,4096]{1,0:T(8,128)(2,1)} custom-call(s32[2]{0:T(128)} %pad_add_fusion.1.choice, bf16[256,8192]{1,0:T(8,128)(2,1)} %states.3, f32[1,8192]{1,0:T(1,128)} %bitcast.26, bf16[256,4096]{1,0:T(8,128)(2,1)} %get-tuple-element.11.rest_0_), custom_call_target="tpu_custom_call", output_to_operand_aliasing={{}: (3, {})} | custom-call | tf_op jit(solution)/shard_map/half_rows/pallas_call | solution.py:80
  118.0 6.9 %all-to-all-done.2 = bf16[16,8,8,256]{3,2,1,0:T(8,128)(2,1)S(1)} async-done(((bf16[16,8,8,256]{3,2,1,0:T(8,128)(2,1)}), bf16[16,8,8,256]{3,2,1,0:T(8,128)(2,1)S(1)}, u32[]{:S(2)}, u32[]{:S(2)}) %all-to-all-start.2) | async-done | bytes 524320 | tf_op jit(solution)/shard_map/all_to_all | solution.py:26
  125.0 3.7 %collective-permute-start.10 = (bf16[8,128,256]{2,1,0:T(8,128)(2,1)S(1)}, bf16[8,128,256]{2,1,0:T(8,128)(2,1)S(1)}, u32[]{:S(2)}, u32[]{:S(2)}) collective-permute-start(bf16[8,128,256]{2,1,0:T(8,128)(2,1)S(1)} %copy_bitcast_fusion.rest_0_), channel_id=1, source_target_pairs={{0,32},{16,48},{32,0},{48,16},{1,33},{17,49},{33,1},{49,17},{2,34}... | collective-permute-start | bytes 1572872 | tf_op jit(solution)/shard_map/ppermute | solution.py:22
  128.7 4.3 %collective-permute-start.11 = (bf16[8,128,256]{2,1,0:T(8,128)(2,1)S(1)}, bf16[8,128,256]{2,1,0:T(8,128)(2,1)S(1)}, u32[]{:S(2)}, u32[]{:S(2)}) collective-permute-start(bf16[8,128,256]{2,1,0:T(8,128)(2,1)S(1)} %copy_bitcast_fusion.rest_0_), channel_id=1, source_target_pairs={{0,48},{16,0},{32,16},{48,32},{1,49},{17,1},{33,17},{49,33},{2,50}... | collective-permute-start | bytes 1572872 | tf_op jit(solution)/shard_map/ppermute | solution.py:22
  133.0 1.9 %collective-permute-start.9 = (bf16[8,128,256]{2,1,0:T(8,128)(2,1)S(1)}, bf16[8,128,256]{2,1,0:T(8,128)(2,1)S(1)}, u32[]{:S(2)}, u32[]{:S(2)}) collective-permute-start(bf16[8,128,256]{2,1,0:T(8,128)(2,1)S(1)} %copy_bitcast_fusion.rest_0_), channel_id=1, source_target_pairs={{0,16},{16,32},{32,48},{48,0},{1,17},{17,33},{33,49},{49,1},{2,18}... | collective-permute-start | bytes 1572872 | tf_op jit(solution)/shard_map/ppermute | solution.py:22
  135.0 0.0 all-gather.3.cloned.1.call-done
  135.0 0.0 copy-start
  135.0 2.9 %fusion.9 = f32[128,512]{1,0:T(8,128)} fusion(bf16[2048,512]{1,0:T(8,128)(2,1)} %all-gather.3.cloned.1.call-done, bf16[128,4096]{1,0:T(8,128)(2,1)S(1)} %collective-permute-done), kind=kOutput, calls=%fused_computation.10 | convolution fusion | flops 268435456 | bytes 2883584 | tf_op jit(solution)/shard_map/dot_general | solution.py:360
  137.9 0.0 collective-permute-done.2
  137.9 0.0 copy-done
  137.9 1.6 fusion.7
  139.5 0.1 copy-done.3
  139.6 1.5 fusion.2
  141.1 2.3 %convolution_add_fusion = f32[128,512]{1,0:T(8,128)S(1)} fusion(f32[128,512]{1,0:T(8,128)S(1)} %fusion.7, bf16[2048,512]{1,0:T(8,128)(2,1)} %all-gather.5.cloned.1.call-done, bf16[128,4096]{1,0:T(8,128)(2,1)} %collective-permute-done.2), kind=kOutput, calls=%fused_computation | convolution fusion | flops 268500992 | bytes 3145728 | tf_op jit(solution)/shard_map/dot_general | solution.py:360
  143.5 0.0 copy-start.6
  143.5 3.5 %collective-permute-start.5 = (f32[128,512]{1,0:T(8,128)S(1)}, f32[128,512]{1,0:T(8,128)S(1)}, u32[]{:S(2)}, u32[]{:S(2)}) collective-permute-start(f32[128,512]{1,0:T(8,128)S(1)} %convolution_add_fusion), channel_id=1, source_target_pairs={{0,16},{16,0},{32,48},{48,32},{1,17},{17,1},{33,49},{49,33},{2,18}... | collective-permute-start | bytes 786440 | tf_op jit(solution)/shard_map/ppermute | solution.py:334
  147.0 0.4 fusion.5
  147.5 0.0 copy-start.7
  147.5 2.6 %collective-permute-start.4 = (f32[128,512]{1,0:T(8,128)S(1)}, f32[128,512]{1,0:T(8,128)S(1)}, u32[]{:S(2)}, u32[]{:S(2)}) collective-permute-start(f32[128,512]{1,0:T(8,128)S(1)} %add.10), channel_id=1, source_target_pairs={{0,16},{16,0},{32,48},{48,32},{1,17},{17,1},{33,49},{49,33},{2,18}... | collective-permute-start | bytes 786440 | tf_op jit(solution)/shard_map/ppermute | solution.py:334
  150.2 0.7 fusion
  150.9 0.9 add.9.query
  151.8 0.0 collective-permute-done.10.rest_2_
  151.8 2.8 %collective-permute-done.11.rest_3_ = bf16[8,128,256]{2,1,0:T(8,128)(2,1)S(1)} collective-permute-done((bf16[8,128,256]{2,1,0:T(8,128)(2,1)S(1)}, bf16[8,128,256]{2,1,0:T(8,128)(2,1)S(1)}, u32[]{:S(2)}, u32[]{:S(2)}) %collective-permute-start.11) | collective-permute-done | bytes 524320 | tf_op jit(solution)/shard_map/ppermute | solution.py:22
  154.6 0.0 collective-permute-done.9.rest_1_
  154.6 5.6 %collective-permute-done.5.far = f32[128,512]{1,0:T(8,128)S(1)} collective-permute-done((f32[128,512]{1,0:T(8,128)S(1)}, f32[128,512]{1,0:T(8,128)S(1)}, u32[]{:S(2)}, u32[]{:S(2)}) %collective-permute-start.5) | collective-permute-done | bytes 262176 | tf_op jit(solution)/shard_map/ppermute | solution.py:334
  160.2 4.4 %collective-permute-done.4.near = f32[128,512]{1,0:T(8,128)S(1)} collective-permute-done((f32[128,512]{1,0:T(8,128)S(1)}, f32[128,512]{1,0:T(8,128)S(1)}, u32[]{:S(2)}, u32[]{:S(2)}) %collective-permute-start.4) | collective-permute-done | bytes 262176 | tf_op jit(solution)/shard_map/ppermute | solution.py:334
  164.6 6.5 %attention.1 = bf16[256,512]{1,0:T(8,128)(2,1)} custom-call(s32[4,4]{1,0:T(4,128)} %owners.1, s32[4]{0:T(128)} %counts.1, f32[1]{0:T(128)S(6)} %tanh.3.gate, f32[256,512]{1,0:T(8,128)} %add.9.query, f32[128,512]{1,0:T(8,128)S(1)} %collective-permute-done.4.near, f32[128,512]{1,0:T(8,128)S(1)} %collective-permute-done.5.far, f32[1,128]{1,0:T(1,128)} %bitcast.29, ...), custom_call_target="tpu_custom_call" | custom-call | tf_op jit(solution)/shard_map/attention/pallas_call | solution.py:272
  (14 shorter events, 0.1 us)
Async XLA Ops:
  6.5 128.4 %all-gather.3.cloned.1.call-start = ((), (), s32[]{:S(2)}) async-start(), calls=%async_computation.3 | async-start | bytes 2359296 | tf_op jit(solution)/shard_map/all_gather | solution.py:323
  8.2 16.9 %collective-permute-start.1 = (bf16[128,768]{1,0:T(8,128)(2,1)}, bf16[128,768]{1,0:T(8,128)(2,1)S(1)}, u32[]{:S(2)}, u32[]{:S(2)}) collective-permute-start(bf16[128,768]{1,0:T(8,128)(2,1)} %join.1), channel_id=1, source_target_pairs={{0,1},{1,0},{2,3},{3,2},{4,5},{5,4},{6,7},{7,6},{8,9},{9,8},{10,11... | collective-permute-start | bytes 589832 | tf_op jit(solution)/shard_map/ppermute | solution.py:22
  26.2 43.9 %copy-start.2 = (bf16[256,768]{1,0:T(8,128)(2,1)}, bf16[256,768]{1,0:T(8,128)(2,1)S(1)}, u32[]{:S(2)}) copy-start(bf16[256,768]{1,0:T(8,128)(2,1)S(1)} %maximum_select_fusion.rest_0_) | copy-start | bytes 1179652
  28.8 28.4 %all-to-all-start = ((bf16[32,8,1024]{2,1,0:T(8,128)(2,1)}), bf16[32,8,1024]{2,1,0:T(8,128)(2,1)S(1)}, u32[]{:S(2)}, u32[]{:S(2)}) async-start(bf16[32,8,1024]{2,1,0:T(8,128)(2,1)} %bitcast.23), calls=%async_computation | async-start | bytes 1048576 | tf_op jit(solution)/shard_map/all_to_all | solution.py:26
  40.7 100.4 %all-gather.5.cloned.1.call-start = ((), (), s32[]{:S(2)}) async-start(), calls=%async_computation.4 | async-start | bytes 2359296 | tf_op jit(solution)/shard_map/all_gather | solution.py:324
  40.8 13.8 %collective-permute-start.3 = (bf16[256,768]{1,0:T(8,128)(2,1)S(1)}, bf16[256,768]{1,0:T(8,128)(2,1)S(1)}, u32[]{:S(2)}, u32[]{:S(2)}) collective-permute-start(bf16[256,768]{1,0:T(8,128)(2,1)S(1)} %maximum_select_fusion.rest_0_), channel_id=1, source_target_pairs={{0,32},{16,48},{32,0},{48,16},{1,33},{17,49},{33,1},{49,17},{2,34}... | collective-permute-start | bytes 1179656 | tf_op jit(solution)/shard_map/ppermute | solution.py:22
  54.5 15.5 %copy-start.5 = (bf16[256,768]{1,0:T(8,128)(2,1)}, bf16[256,768]{1,0:T(8,128)(2,1)S(1)}, u32[]{:S(2)}) copy-start(bf16[256,768]{1,0:T(8,128)(2,1)S(1)} %collective-permute-done.3.rest_2_) | copy-start | bytes 1179652
  57.2 12.9 %collective-permute-start.6 = (bf16[32,8,1024]{2,1,0:T(8,128)(2,1)S(1)}, bf16[32,8,1024]{2,1,0:T(8,128)(2,1)S(1)}, u32[]{:S(2)}, u32[]{:S(2)}) collective-permute-start(bf16[32,8,1024]{2,1,0:T(8,128)(2,1)S(1)} %all-to-all-done), channel_id=1, source_target_pairs={{0,64},{64,0},{1,65},{65,1},{2,66},{66,2},{3,67},{67,3},{4,68},{68... | collective-permute-start | bytes 1572872 | tf_op jit(solution)/shard_map/ppermute | solution.py:22
  59.1 9.0 %collective-permute-start.7 = (bf16[256,256]{1,0:T(8,128)(2,1)S(1)}, bf16[256,256]{1,0:T(8,128)(2,1)S(1)}, u32[]{:S(2)}, u32[]{:S(2)}) collective-permute-start(bf16[256,256]{1,0:T(8,128)(2,1)S(1)} %slice.44), channel_id=1, source_target_pairs={{0,16},{16,32},{32,48},{48,0},{1,17},{17,33},{33,49},{49,1},{2,18}... | collective-permute-start | bytes 393224 | tf_op jit(solution)/shard_map/ppermute | solution.py:22
  62.5 7.5 %collective-permute-start.8 = (bf16[256,256]{1,0:T(8,128)(2,1)S(1)}, bf16[256,256]{1,0:T(8,128)(2,1)S(1)}, u32[]{:S(2)}, u32[]{:S(2)}) collective-permute-start(bf16[256,256]{1,0:T(8,128)(2,1)S(1)} %slice.44), channel_id=1, source_target_pairs={{0,48},{16,0},{32,16},{48,32},{1,49},{17,1},{33,17},{49,33},{2,50}... | collective-permute-start | bytes 393224 | tf_op jit(solution)/shard_map/ppermute | solution.py:22
  68.1 1.9 %copy-start.8 = (bf16[256,256]{1,0:T(8,128)(2,1)}, bf16[256,256]{1,0:T(8,128)(2,1)S(1)}, u32[]{:S(2)}) copy-start(bf16[256,256]{1,0:T(8,128)(2,1)S(1)} %collective-permute-done.7.rest_1_) | copy-start | bytes 393220
  70.1 0.6 copy-start.9
  73.1 21.1 %all-to-all-start.1 = ((f32[8,2,4,8,256]{4,3,2,1,0:T(8,128)}), f32[8,2,4,8,256]{4,3,2,1,0:T(8,128)S(1)}, u32[]{:S(2)}, u32[]{:S(2)}) async-start(f32[8,2,4,8,256]{4,3,2,1,0:T(8,128)} %partial_sums.1), calls=%async_computation.1 | async-start | bytes 1048576 | tf_op jit(solution)/shard_map/all_to_all | solution.py:26
  84.0 26.1 %collective-permute-start = (bf16[128,4096]{1,0:T(8,128)(2,1)}, bf16[128,4096]{1,0:T(8,128)(2,1)S(1)}, u32[]{:S(2)}, u32[]{:S(2)}) collective-permute-start(bf16[128,4096]{1,0:T(8,128)(2,1)} %get-tuple-element.10), channel_id=1, source_target_pairs={{0,16},{16,0},{32,48},{48,32},{1,17},{17,1},{33,49},{49,33},{2,18}... | collective-permute-start | bytes 3145736 | tf_op jit(solution)/shard_map/ppermute | solution.py:334
  95.8 29.2 %all-to-all-start.2 = ((bf16[16,8,8,256]{3,2,1,0:T(8,128)(2,1)}), bf16[16,8,8,256]{3,2,1,0:T(8,128)(2,1)S(1)}, u32[]{:S(2)}, u32[]{:S(2)}) async-start(bf16[16,8,8,256]{3,2,1,0:T(8,128)(2,1)} %key_value_pairs.1), calls=%async_computation.2 | async-start | bytes 1048576 | tf_op jit(solution)/shard_map/all_to_all | solution.py:26
  110.1 27.8 %collective-permute-start.2 = (bf16[128,4096]{1,0:T(8,128)(2,1)S(1)}, bf16[128,4096]{1,0:T(8,128)(2,1)}, u32[]{:S(2)}, u32[]{:S(2)}) collective-permute-start(bf16[128,4096]{1,0:T(8,128)(2,1)S(1)} %collective-permute-done), channel_id=1, source_target_pairs={{0,64},{64,0},{1,65},{65,1},{2,66},{66,2},{3,67},{67,3},{4,68},{68... | collective-permute-start | bytes 3145736 | tf_op jit(solution)/shard_map/ppermute | solution.py:22
  125.0 26.8 %collective-permute-start.10 = (bf16[8,128,256]{2,1,0:T(8,128)(2,1)S(1)}, bf16[8,128,256]{2,1,0:T(8,128)(2,1)S(1)}, u32[]{:S(2)}, u32[]{:S(2)}) collective-permute-start(bf16[8,128,256]{2,1,0:T(8,128)(2,1)S(1)} %copy_bitcast_fusion.rest_0_), channel_id=1, source_target_pairs={{0,32},{16,48},{32,0},{48,16},{1,33},{17,49},{33,1},{49,17},{2,34}... | collective-permute-start | bytes 1572872 | tf_op jit(solution)/shard_map/ppermute | solution.py:22
  128.7 25.8 %collective-permute-start.11 = (bf16[8,128,256]{2,1,0:T(8,128)(2,1)S(1)}, bf16[8,128,256]{2,1,0:T(8,128)(2,1)S(1)}, u32[]{:S(2)}, u32[]{:S(2)}) collective-permute-start(bf16[8,128,256]{2,1,0:T(8,128)(2,1)S(1)} %copy_bitcast_fusion.rest_0_), channel_id=1, source_target_pairs={{0,48},{16,0},{32,16},{48,32},{1,49},{17,1},{33,17},{49,33},{2,50}... | collective-permute-start | bytes 1572872 | tf_op jit(solution)/shard_map/ppermute | solution.py:22
  133.0 21.5 %collective-permute-start.9 = (bf16[8,128,256]{2,1,0:T(8,128)(2,1)S(1)}, bf16[8,128,256]{2,1,0:T(8,128)(2,1)S(1)}, u32[]{:S(2)}, u32[]{:S(2)}) collective-permute-start(bf16[8,128,256]{2,1,0:T(8,128)(2,1)S(1)} %copy_bitcast_fusion.rest_0_), channel_id=1, source_target_pairs={{0,16},{16,32},{32,48},{48,0},{1,17},{17,33},{33,49},{49,1},{2,18}... | collective-permute-start | bytes 1572872 | tf_op jit(solution)/shard_map/ppermute | solution.py:22
  135.0 2.9 %copy-start = (bf16[2048,512]{1,0:T(8,128)(2,1)S(1)}, bf16[2048,512]{1,0:T(8,128)(2,1)}, u32[]{:S(2)}) copy-start(bf16[2048,512]{1,0:T(8,128)(2,1)} %all-gather.3.cloned.1.call-done) | copy-start | bytes 6291460
  137.9 1.7 copy-start.3
  141.1 5.9 %copy-start.1 = (bf16[2048,512]{1,0:T(8,128)(2,1)S(1)}, bf16[2048,512]{1,0:T(8,128)(2,1)}, u32[]{:S(2)}) copy-start(bf16[2048,512]{1,0:T(8,128)(2,1)} %all-gather.5.cloned.1.call-done) | copy-start | bytes 6291460
  143.5 4.0 %copy-start.6 = (f32[128,512]{1,0:T(8,128)S(1)}, f32[128,512]{1,0:T(8,128)}, u32[]{:S(2)}) copy-start(f32[128,512]{1,0:T(8,128)} %fusion.9) | copy-start | bytes 786436
  143.5 6.7 %copy-start.4 = (bf16[256,4096]{1,0:T(8,128)(2,1)S(1)}, bf16[256,4096]{1,0:T(8,128)(2,1)}, u32[]{:S(2)}) copy-start(bf16[256,4096]{1,0:T(8,128)(2,1)} %half_rows.3) | copy-start | bytes 6291460
  143.5 16.7 %collective-permute-start.5 = (f32[128,512]{1,0:T(8,128)S(1)}, f32[128,512]{1,0:T(8,128)S(1)}, u32[]{:S(2)}, u32[]{:S(2)}) collective-permute-start(f32[128,512]{1,0:T(8,128)S(1)} %convolution_add_fusion), channel_id=1, source_target_pairs={{0,16},{16,0},{32,48},{48,32},{1,17},{17,1},{33,49},{49,33},{2,18}... | collective-permute-start | bytes 786440 | tf_op jit(solution)/shard_map/ppermute | solution.py:334
  147.5 3.4 %copy-start.7 = (f32[256,512]{1,0:T(8,128)S(1)}, f32[256,512]{1,0:T(8,128)}, u32[]{:S(2)}) copy-start(f32[256,512]{1,0:T(8,128)} %fusion.2) | copy-start | bytes 1572868
  147.5 17.0 %collective-permute-start.4 = (f32[128,512]{1,0:T(8,128)S(1)}, f32[128,512]{1,0:T(8,128)S(1)}, u32[]{:S(2)}, u32[]{:S(2)}) collective-permute-start(f32[128,512]{1,0:T(8,128)S(1)} %add.10), channel_id=1, source_target_pairs={{0,16},{16,0},{32,48},{48,32},{1,17},{17,1},{33,49},{49,33},{2,18}... | collective-permute-start | bytes 786440 | tf_op jit(solution)/shard_map/ppermute | solution.py:334
Sparse Core Ops, SparseCore 0:
  27.1 54.2 all-gather.2
  83.5 50.8 all-gather.4
